TPU v7x, 128 devices: a whole 4x4x4 slice. The times are simulated.
128 devices in a mesh: layer: 16 (over x_lo, y, core), dp: 8 (over x_hi, z).
Axes of the slice: x: 4 (x_hi: 2, x_lo: 2; x = x_hi * 2 + x_lo), y: 4, z: 4, core: 2. Of those that a mesh axis runs over, the one named last changes fastest.
Arguments:
- activations: bfloat16 [16, 2048, 2048], P('layer', 'dp')
- factor_old: float32 [16, 2048, 2048], P('layer', 'dp'), as said below
- cross_old: float32 [16, 2048, 2048], P('layer', 'dp')
- gradients: bfloat16 [16, 2048, 1024], P('layer', 'dp'), may hold values from -6 to 6
- moments: bfloat16 [16, 2048, 1024], P('layer', 'dp'), may hold values from -6 to 6
- exponents: int32 [16, 16], P('layer', 'dp'), may hold values from -3 to 2
- master: float32 [16, 2048, 1024], P('layer', 'dp'), may hold values from -6 to 6
Outputs:
- factor_new: float32 [16, 2048, 2048], P('layer', 'dp')
- cross_new: float32 [16, 2048, 2048], P('layer', 'dp')
- moments_new: bfloat16 [16, 2048, 1024], P('layer', 'dp')
- master_new: float32 [16, 2048, 1024], P('layer', 'dp')
- replicas: bfloat16 [16, 2048, 1024], P('layer')
Inputs may be any that keep to these rules, and one draw needn't show every extreme that they name: factor_old is symmetric in its last two dimensions, and its diagonal entries lie between 0.6 and 1.4.
All inputs are finite; a program needn't handle non-finite values.
Results may differ from a plain program's by a relative error of at most 0.0025.
Values may be sent and summed in bfloat16 or wider, within the bound.
No kernel may reach another device: no remote copies, remote signals or barrier semaphores. Data moves between devices by JAX's collectives and lax.ppermute only.
A program may use at most 128 MiB of HBM per device.

v0:
```python
import jax
import jax.numpy as jnp
from jax import lax
from jax.sharding import Mesh
from jax.sharding import PartitionSpec as P

SCALE_BLOCK = 128
LAYER = ("layer_0", "layer_1", "layer_2")


FACTOR_DECAY = 0.9
DAMPING = 0.5
MOMENTUM = 0.8
STEP_SIZE = 0.05


def neutral_like(x, identity):
    return jax.tree.map(
        lambda a, e: jnp.broadcast_to(jnp.asarray(e, a.dtype), a.shape), x, identity
    )


def entering(x, axes, combine, identity, reverse):
    before = start = neutral_like(x, identity)
    total = x
    for axis in reversed(axes):
        peers, here = (lax.axis_size(axis), lax.axis_index(axis))
        pieces = jax.tree.map(lambda part: lax.all_gather(part, axis), total)
        inside, total = (start, start)
        for k in reversed(range(peers)) if reverse else range(peers):
            passed = k > here if reverse else k < here
            total = combine(total, jax.tree.map(lambda part: part[k], pieces))
            inside = jax.tree.map(lambda new, old: jnp.where(passed, new, old), total, inside)
        before = combine(inside, before)
    return before


def shifted(value, axis, steps):
    count = lax.axis_size(axis)
    leading, last = (max(0, -steps), min(count, count - steps))
    return lax.ppermute(value, axis, [(source, source + steps) for source in range(leading, last)])


def compose(earlier, nearer):
    return (nearer[0] * earlier[0], nearer[0] * earlier[1] + nearer[1])


def chain_solve(target, pivots, coupling):
    coupling_ratio = (coupling / pivots)[:, None]
    unit_scale = jnp.ones_like(coupling_ratio)
    zero_shift = jnp.zeros_like(target)
    passed = entering(
        (-coupling_ratio, coupling_ratio * target), LAYER, compose, (unit_scale, zero_shift), False
    )
    scaled = (target - passed[1]) / pivots[:, None]
    arrived = entering((-coupling_ratio, scaled), LAYER, compose, (unit_scale, zero_shift), True)
    return scaled - coupling_ratio * arrived[1]


def row_products(left_rows, right_rows):
    return lax.dot_general(
        left_rows, right_rows, (((0,), (0,)), ((), ())), preferred_element_type=jnp.float32
    )


def exact_product(left_block, right_block):
    return jnp.dot(
        left_block, right_block, precision=lax.Precision.HIGHEST, preferred_element_type=jnp.float32
    )


def body(activations, factor_old, cross_old, gradients, moments, exponents, master):
    row_count = factor_old.shape[1]
    row_start = lax.axis_index("dp") * row_count
    fresh_weight = (1.0 - FACTOR_DECAY) / (activations.shape[1] * lax.axis_size("dp"))
    all_tokens = lax.all_gather(activations, "dp", axis=1, tiled=True)[0]
    upper_acts = shifted(all_tokens, LAYER, -1)
    own_columns = lax.dynamic_slice_in_dim(all_tokens, row_start, row_count, 1)
    batch_factor = row_products(own_columns, all_tokens)
    batch_cross = row_products(own_columns, upper_acts)
    factor_new = FACTOR_DECAY * factor_old[0] + fresh_weight * batch_factor
    cross_new = FACTOR_DECAY * cross_old[0] + fresh_weight * batch_cross
    pivots = DAMPING + jnp.diagonal(lax.dynamic_slice_in_dim(factor_new, row_start, row_count, 1))
    coupling = jnp.diagonal(lax.dynamic_slice_in_dim(cross_new, row_start, row_count, 1))
    grad_wide = gradients[0].astype(jnp.float32)
    initial = chain_solve(grad_wide, pivots, coupling).astype(jnp.bfloat16)
    initial_wide = initial.astype(jnp.float32)
    own_full = lax.all_gather(initial, "dp", axis=0, tiled=True)
    upper_full = shifted(own_full, LAYER, -1)
    applied = exact_product(factor_new, own_full.astype(jnp.float32))
    applied = applied + DAMPING * initial_wide
    applied = applied + exact_product(cross_new, upper_full.astype(jnp.float32))
    cross_columns = lax.all_to_all(cross_new, "dp", split_axis=1, concat_axis=0, tiled=True)
    columns_lower = shifted(cross_columns, LAYER, 1)
    lower_full = shifted(own_full, LAYER, 1)
    applied = applied + lax.dot_general(
        columns_lower,
        lower_full.astype(jnp.float32),
        (((0,), (0,)), ((), ())),
        precision=lax.Precision.HIGHEST,
        preferred_element_type=jnp.float32,
    )
    update = initial_wide + chain_solve(grad_wide - applied, pivots, coupling)
    dequant = jnp.repeat(jnp.exp2(exponents[0].astype(jnp.float32)), SCALE_BLOCK)[:, None]
    requant = jnp.repeat(jnp.exp2(-exponents[0].astype(jnp.float32)), SCALE_BLOCK)[:, None]
    moment = MOMENTUM * moments[0].astype(jnp.float32) * dequant + (1.0 - MOMENTUM) * update
    moments_new = (moment * requant).astype(jnp.bfloat16)
    master_new = master[0] - STEP_SIZE * moment
    replicas = lax.all_gather(master_new.astype(jnp.bfloat16), "dp", axis=0, tiled=True)
    return (factor_new[None], cross_new[None], moments_new[None], master_new[None], replicas[None])


def solution(mesh):
    finer = Mesh(
        mesh.devices.reshape(2, 4, 2, mesh.shape["dp"]), ("layer_0", "layer_1", "layer_2", "dp")
    )
    in_specs = (
        P(LAYER, "dp", None),
        P(LAYER, "dp", None),
        P(LAYER, "dp", None),
        P(LAYER, "dp", None),
        P(LAYER, "dp", None),
        P(LAYER, "dp"),
        P(LAYER, "dp", None),
    )
    out_specs = (
        P(LAYER, "dp", None),
        P(LAYER, "dp", None),
        P(LAYER, "dp", None),
        P(LAYER, "dp", None),
        P(LAYER, None, None),
    )
    return jax.shard_map(body, mesh=finer, in_specs=in_specs, out_specs=out_specs, check_vma=False)
```

profile of v0, /device:TPU:6, one launch (start us, length us, event | category | flops | bytes accessed | tf_op | source)
XLA Modules:
  0.0 937.5 jit_solution(18379451437130043277)
XLA Ops:
  7.9 110.5 %all-gather.22.cloned.1.call-done = bf16[1,2048,2048]{2,1,0:T(8,128)(2,1)} async-done(((bf16[1,256,2048]{2,1,0:T(8,128)(2,1)}), bf16[1,2048,2048]{2,1,0:T(8,128)(2,1)}) %all-gather.22.cloned.1.call-update) | async-done | bytes 8388624 | tf_op jit(solution)/shard_map/all_gather | solution.py:76
  118.4 3.1 collective-permute-start
  121.5 6.7 fusion
  129.6 2.3 gather_fusion.1
  131.9 80.8 %collective-permute-done = bf16[2048,2048]{1,0:T(8,128)(2,1)} collective-permute-done((bf16[2048,2048]{1,0:T(8,128)(2,1)}, bf16[2048,2048]{1,0:T(8,128)(2,1)}, u32[]{:S(2)}, u32[]{:S(2)}) %collective-permute-start) | collective-permute-done | bytes 8388640 | tf_op jit(solution)/shard_map/ppermute | solution.py:41
  212.8 6.7 fusion.1
  219.5 2.3 gather_fusion
  223.1 2.1 all-gather.4
  225.2 8.4 all-gather.5
  233.6 3.2 all-gather.24.cloned.1.call-done
  236.9 2.7 multiply_add_fusion.7
  239.7 49.7 %all-gather.26.cloned.1.call-done = f32[4,256,1024]{2,1,0:T(8,128)} async-done(((f32[1,256,1024]{2,1,0:T(8,128)}), f32[4,256,1024]{2,1,0:T(8,128)}) %all-gather.26.cloned.1.call-update) | async-done | bytes 4194320 | tf_op jit(solution)/shard_map/all_gather | solution.py:28
  289.3 3.5 multiply_add_fusion.4
  292.9 4.2 all_gather.45
  297.1 31.2 %all-gather.28.cloned.1.call-done = f32[2,256,1024]{2,1,0:T(8,128)} async-done(((f32[1,256,1024]{2,1,0:T(8,128)}), f32[2,256,1024]{2,1,0:T(8,128)}) %all-gather.28.cloned.1.call-update) | async-done | bytes 2097168 | tf_op jit(solution)/shard_map/all_gather | solution.py:28
  328.3 5.4 fusion.10
  333.8 15.0 %all-gather.30.cloned.1.call-done = f32[2,256,1024]{2,1,0:T(8,128)} async-done(((f32[1,256,1024]{2,1,0:T(8,128)}), f32[2,256,1024]{2,1,0:T(8,128)}) %all-gather.30.cloned.1.call-update) | async-done | bytes 2097168 | tf_op jit(solution)/shard_map/all_gather | solution.py:28
  348.8 2.7 multiply_add_fusion.3
  351.6 49.7 %all-gather.32.cloned.1.call-done = f32[4,256,1024]{2,1,0:T(8,128)} async-done(((f32[1,256,1024]{2,1,0:T(8,128)}), f32[4,256,1024]{2,1,0:T(8,128)}) %all-gather.32.cloned.1.call-update) | async-done | bytes 4194320 | tf_op jit(solution)/shard_map/all_gather | solution.py:28
  401.2 3.5 multiply_add_fusion.2
  404.8 4.2 all_gather.49
  409.1 31.2 %all-gather.34.cloned.1.call-done = f32[2,256,1024]{2,1,0:T(8,128)} async-done(((f32[1,256,1024]{2,1,0:T(8,128)}), f32[2,256,1024]{2,1,0:T(8,128)}) %all-gather.34.cloned.1.call-update) | async-done | bytes 2097168 | tf_op jit(solution)/shard_map/all_gather | solution.py:28
  440.2 8.7 fusion.9
  449.0 71.8 %all-gather.36.cloned.1.call-done = bf16[2048,1024]{1,0:T(8,128)(2,1)} async-done(((bf16[256,1024]{1,0:T(8,128)(2,1)}), bf16[2048,1024]{1,0:T(8,128)(2,1)}) %all-gather.36.cloned.1.call-update) | async-done | bytes 4194320 | tf_op jit(solution)/shard_map/all_gather | solution.py:88
  520.7 1.9 collective-permute-start.3
  524.2 6.5 all-to-all-start
  530.6 4.9 collective-permute-start.1
  535.5 21.8 %all-to-all-done = f32[256,8,256]{2,0,1:T(8,128)} async-done(((f32[256,8,256]{2,0,1:T(8,128)}), f32[256,8,256]{2,0,1:T(8,128)}, u32[]{:S(2)}, u32[]{:S(2)}) %all-to-all-start) | async-done | bytes 2097184 | tf_op jit(solution)/shard_map/all_to_all | solution.py:93
  557.3 2.5 collective-permute-start.2
  559.9 6.1 convolution_add_fusion.1
  566.0 56.2 %collective-permute-done.2 = f32[2048,256]{1,0:T(8,128)S(1)} collective-permute-done((f32[2048,256]{1,0:T(8,128)}, f32[2048,256]{1,0:T(8,128)S(1)}, u32[]{:S(2)}, u32[]{:S(2)}) %collective-permute-start.2) | collective-permute-done | bytes 2097184 | tf_op jit(solution)/shard_map/ppermute | solution.py:41
  622.3 5.4 fusion.70
  627.7 7.1 broadcast_multiply_fusion
  634.9 10.2 %all-gather.48.cloned.1.call-done = f32[512,1024]{1,0:T(8,128)} async-done(((f32[256,1024]{1,0:T(8,128)}), f32[512,1024]{1,0:T(8,128)}) %all-gather.48.cloned.1.call-update) | async-done | bytes 2097168 | tf_op jit(solution)/shard_map/all_gather | solution.py:28
  645.1 2.7 bitcast_add_fusion.10
  647.9 49.6 %all-gather.38.cloned.1.call-done = f32[4,256,1024]{2,1,0:T(8,128)} async-done(((f32[1,256,1024]{2,1,0:T(8,128)}), f32[4,256,1024]{2,1,0:T(8,128)}) %all-gather.38.cloned.1.call-update) | async-done | bytes 4194320 | tf_op jit(solution)/shard_map/all_gather | solution.py:28
  697.5 3.5 multiply_add_fusion.1
  701.1 35.4 %all-gather.40.cloned.1.call-done = f32[2,256,1024]{2,1,0:T(8,128)} async-done(((f32[1,256,1024]{2,1,0:T(8,128)}), f32[2,256,1024]{2,1,0:T(8,128)}) %all-gather.40.cloned.1.call-update) | async-done | bytes 2097168 | tf_op jit(solution)/shard_map/all_gather | solution.py:28
  736.6 5.1 fusion.23
  741.7 15.0 %all-gather.50.cloned.1.call-done = f32[512,1024]{1,0:T(8,128)} async-done(((f32[256,1024]{1,0:T(8,128)}), f32[512,1024]{1,0:T(8,128)}) %all-gather.50.cloned.1.call-update) | async-done | bytes 2097168 | tf_op jit(solution)/shard_map/all_gather | solution.py:28
  756.7 2.7 bitcast_add_fusion.4
  759.6 49.6 %all-gather.42.cloned.1.call-done = f32[4,256,1024]{2,1,0:T(8,128)} async-done(((f32[1,256,1024]{2,1,0:T(8,128)}), f32[4,256,1024]{2,1,0:T(8,128)}) %all-gather.42.cloned.1.call-update) | async-done | bytes 4194320 | tf_op jit(solution)/shard_map/all_gather | solution.py:28
  809.2 3.5 multiply_add_fusion
  812.8 35.3 %all-gather.44.cloned.1.call-done = f32[2,256,1024]{2,1,0:T(8,128)} async-done(((f32[1,256,1024]{2,1,0:T(8,128)}), f32[2,256,1024]{2,1,0:T(8,128)}) %all-gather.44.cloned.1.call-update) | async-done | bytes 2097168 | tf_op jit(solution)/shard_map/all_gather | solution.py:28
  848.2 6.4 fusion.55
  854.7 2.5 fusion.56
  857.2 69.2 %all-gather.46.cloned.1.call-done = bf16[2048,1024]{1,0:T(8,128)(2,1)} async-done(((bf16[256,1024]{1,0:T(8,128)(2,1)}), bf16[2048,1024]{1,0:T(8,128)(2,1)}) %all-gather.46.cloned.1.call-update) | async-done | bytes 4194320 | tf_op jit(solution)/shard_map/all_gather | solution.py:109
  926.4 4.6 copy.18
  (66 shorter events, 5.7 us)
Async XLA Ops:
  7.2 111.3 %all-gather.22.cloned.1.call-start = ((), (), s32[]{:S(2)}) async-start(), calls=%async_computation.1 | async-start | bytes 9437184 | tf_op jit(solution)/shard_map/all_gather | solution.py:76
  7.9 229.0 %all-gather.24.cloned.1.call-start = ((), (), s32[]{:S(2)}) async-start(), calls=%async_computation.2 | async-start | bytes 3145728 | tf_op jit(solution)/shard_map/all_gather | solution.py:28
  118.4 94.3 %collective-permute-start = (bf16[2048,2048]{1,0:T(8,128)(2,1)}, bf16[2048,2048]{1,0:T(8,128)(2,1)}, u32[]{:S(2)}, u32[]{:S(2)}) collective-permute-start(bf16[2048,2048]{1,0:T(8,128)(2,1)} %bitcast.304), channel_id=1, source_target_pairs={{8,0},{16,8},{24,16},{32,24},{40,32},{48,40},{56,48},{64,56},{72,6... | collective-permute-start | bytes 25165832 | tf_op jit(solution)/shard_map/ppermute | solution.py:41
  128.2 1.3 copy-start.6
  131.9 90.0 %copy-start.3 = (bf16[1,256,1024]{2,1,0:T(8,128)(2,1)S(1)}, bf16[1,256,1024]{2,1,0:T(8,128)(2,1)}, u32[]{:S(2)}) copy-start(bf16[1,256,1024]{2,1,0:T(8,128)(2,1)} %param.10) | copy-start | bytes 1572868
  219.5 408.2 %copy-start = (f32[256,2048]{1,0:T(8,128)}, f32[256,2048]{1,0:T(8,128)S(1)}, u32[]{:S(2)}) copy-start(f32[256,2048]{1,0:T(8,128)S(1)} %fusion.1) | copy-start | bytes 6291460
  223.0 66.3 %all-gather.26.cloned.1.call-start = ((), (), s32[]{:S(2)}) async-start(), calls=%async_computation.3 | async-start | bytes 5242880 | tf_op jit(solution)/shard_map/all_gather | solution.py:28
  239.6 88.7 %all-gather.28.cloned.1.call-start = ((), (), s32[]{:S(2)}) async-start(), calls=%async_computation.4 | async-start | bytes 3145728 | tf_op jit(solution)/shard_map/all_gather | solution.py:28
  292.8 56.0 %all-gather.30.cloned.1.call-start = ((), (), s32[]{:S(2)}) async-start(), calls=%async_computation.5 | async-start | bytes 3145728 | tf_op jit(solution)/shard_map/all_gather | solution.py:28
  333.7 67.5 %all-gather.32.cloned.1.call-start = ((), (), s32[]{:S(2)}) async-start(), calls=%async_computation.6 | async-start | bytes 5242880 | tf_op jit(solution)/shard_map/all_gather | solution.py:28
  351.5 88.7 %all-gather.34.cloned.1.call-start = ((), (), s32[]{:S(2)}) async-start(), calls=%async_computation.7 | async-start | bytes 3145728 | tf_op jit(solution)/shard_map/all_gather | solution.py:28
  404.8 116.0 %all-gather.36.cloned.1.call-start = ((), (), s32[]{:S(2)}) async-start(), calls=%async_computation.8 | async-start | bytes 4718592 | tf_op jit(solution)/shard_map/all_gather | solution.py:88
  520.7 101.5 %collective-permute-start.3 = (bf16[2048,1024]{1,0:T(8,128)(2,1)}, bf16[2048,1024]{1,0:T(8,128)(2,1)}, u32[]{:S(2)}, u32[]{:S(2)}) collective-permute-start(bf16[2048,1024]{1,0:T(8,128)(2,1)} %all-gather.36.cloned.1.call-done), channel_id=1, source_target_pairs={{0,8},{8,16},{16,24},{24,32},{32,40},{40,48},{48,56},{56,64},{64,7... | collective-permute-start | bytes 12582920 | tf_op jit(solution)/shard_map/ppermute | solution.py:41
  524.2 35.7 %copy-start.4 = (bf16[256,1024]{1,0:T(8,128)(2,1)S(1)}, bf16[256,1024]{1,0:T(8,128)(2,1)}, u32[]{:S(2)}) copy-start(bf16[256,1024]{1,0:T(8,128)(2,1)} %fusion.9) | copy-start | bytes 1572868
  524.2 33.1 %all-to-all-start = ((f32[256,8,256]{2,0,1:T(8,128)}), f32[256,8,256]{2,0,1:T(8,128)}, u32[]{:S(2)}, u32[]{:S(2)}) async-start(f32[256,8,256]{2,0,1:T(8,128)} %bitcast.307), calls=%async_computation | async-start | bytes 4194304 | tf_op jit(solution)/shard_map/all_to_all | solution.py:93
  530.6 114.5 %all-gather.48.cloned.1.call-start = ((), (), s32[]{:S(2)}) async-start(), calls=%async_computation.14 | async-start | bytes 3145728 | tf_op jit(solution)/shard_map/all_gather | solution.py:28
  530.6 97.1 %collective-permute-start.1 = (bf16[2048,1024]{1,0:T(8,128)(2,1)}, bf16[2048,1024]{1,0:T(8,128)(2,1)}, u32[]{:S(2)}, u32[]{:S(2)}) collective-permute-start(bf16[2048,1024]{1,0:T(8,128)(2,1)} %all-gather.36.cloned.1.call-done), channel_id=1, source_target_pairs={{8,0},{16,8},{24,16},{32,24},{40,32},{48,40},{56,48},{64,56},{72,6... | collective-permute-start | bytes 12582920 | tf_op jit(solution)/shard_map/ppermute | solution.py:41
  557.3 64.9 %collective-permute-start.2 = (f32[2048,256]{1,0:T(8,128)}, f32[2048,256]{1,0:T(8,128)S(1)}, u32[]{:S(2)}, u32[]{:S(2)}) collective-permute-start(f32[2048,256]{1,0:T(8,128)} %bitcast.44), channel_id=1, source_target_pairs={{0,8},{8,16},{16,24},{24,32},{32,40},{40,48},{48,56},{56,64},{64,7... | collective-permute-start | bytes 6291464 | tf_op jit(solution)/shard_map/ppermute | solution.py:41
  634.8 62.7 %all-gather.38.cloned.1.call-start = ((), (), s32[]{:S(2)}) async-start(), calls=%async_computation.9 | async-start | bytes 5242880 | tf_op jit(solution)/shard_map/all_gather | solution.py:28
  647.8 88.7 %copy-start.2 = (f32[512,1024]{1,0:T(8,128)S(1)}, f32[512,1024]{1,0:T(8,128)}, u32[]{:S(2)}) copy-start(f32[512,1024]{1,0:T(8,128)} %all-gather.48.cloned.1.call-done) | copy-start | bytes 6291460
  647.9 88.7 %all-gather.40.cloned.1.call-start = ((), (), s32[]{:S(2)}) async-start(), calls=%async_computation.10 | async-start | bytes 3145728 | tf_op jit(solution)/shard_map/all_gather | solution.py:28
  701.1 55.7 %all-gather.50.cloned.1.call-start = ((), (), s32[]{:S(2)}) async-start(), calls=%async_computation.15 | async-start | bytes 3145728 | tf_op jit(solution)/shard_map/all_gather | solution.py:28
  741.6 67.5 %all-gather.42.cloned.1.call-start = ((), (), s32[]{:S(2)}) async-start(), calls=%async_computation.11 | async-start | bytes 5242880 | tf_op jit(solution)/shard_map/all_gather | solution.py:28
  759.5 53.3 %copy-start.8 = (s32[1,2]{1,0:T(1,128)S(1)}, s32[1,2]{1,0:T(1,128)}, u32[]{:S(2)}) copy-start(s32[1,2]{1,0:T(1,128)} %param.12) | copy-start | bytes 28
  759.5 88.7 %copy-start.1 = (f32[256,1024]{1,0:T(8,128)S(1)}, f32[256,1024]{1,0:T(8,128)}, u32[]{:S(2)}) copy-start(f32[256,1024]{1,0:T(8,128)} %fusion.23) | copy-start | bytes 3145732
  759.5 88.7 %copy-start.5 = (f32[1,256,1024]{2,1,0:T(8,128)S(1)}, f32[1,256,1024]{2,1,0:T(8,128)}, u32[]{:S(2)}) copy-start(f32[1,256,1024]{2,1,0:T(8,128)} %param.13) | copy-start | bytes 3145732
  759.5 88.7 %copy-start.7 = (bf16[1,256,1024]{2,1,0:T(8,128)(2,1)S(1)}, bf16[1,256,1024]{2,1,0:T(8,128)(2,1)}, u32[]{:S(2)}) copy-start(bf16[1,256,1024]{2,1,0:T(8,128)(2,1)} %param.11) | copy-start | bytes 1572868
  759.5 88.7 %all-gather.44.cloned.1.call-start = ((), (), s32[]{:S(2)}) async-start(), calls=%async_computation.12 | async-start | bytes 3145728 | tf_op jit(solution)/shard_map/all_gather | solution.py:28
  812.7 113.7 %all-gather.46.cloned.1.call-start = ((), (), s32[]{:S(2)}) async-start(), calls=%async_computation.13 | async-start | bytes 4718592 | tf_op jit(solution)/shard_map/all_gather | solution.py:109
Sparse Core Ops, SparseCore 0:
  10.4 108.0 all-gather.21
  223.1 13.6 all-gather.23
  239.7 49.5 all-gather.25
  292.9 35.3 all-gather.27
  333.8 14.9 all-gather.29
  351.7 49.5 all-gather.31
  404.9 35.3 all-gather.33
  449.1 71.6 all-gather.35
  635.0 10.1 all-gather.47
  648.0 49.5 all-gather.37
  701.2 35.3 all-gather.39
  741.8 14.9 all-gather.49
  759.6 49.5 all-gather.41
  812.8 35.3 all-gather.43
  854.7 71.6 all-gather.45
where the time goes:
time: 940 us; the launch traced here: 938 us
  waiting for transfers between devices  786 us (84%)
  other arithmetic  54 us (6%)
  matrix products  32 us (3%)
  starting transfers between devices  19.4 us (2%)
  blocking collectives  19 us (2%)
  between operations  14.2 us (2%)
  local copies, waits for them, and re-layouts  12.4 us (1%)
    all_gather x12, waiting for transfers between devices, entering(): pieces = jax.tree.map(lambda part: lax.all_gather(part, axis), total)  375 us
    ppermute x4, waiting for transfers between devices, shifted(): lax.ppermute(value, axis, [(source, source + steps) for source in range(l...  137 us
    all_gather x1, waiting for transfers between devices, body(): all_tokens = lax.all_gather(activations, 'dp', axis=1, tiled=True)[0]  110 us
    all_gather x1, waiting for transfers between devices, body(): own_full = lax.all_gather(initial, 'dp', axis=0, tiled=True)  71.8 us
    all_gather x1, waiting for transfers between devices, body(): lax.all_gather(master_new.astype(jnp.bfloat16), 'dp', axis=0, tiled=True)  69.2 us
    add x8, other arithmetic, compose(): return (nearer[0] * earlier[0], nearer[0] * earlier[1] + nearer[1])  24.8 us
    all_to_all x1, waiting for transfers between devices, body(): lax.all_to_all(cross_new, 'dp', split_axis=1, concat_axis=0, tiled=True)  21.8 us
    all_gather x4, blocking collectives, entering(): pieces = jax.tree.map(lambda part: lax.all_gather(part, axis), total)  19 us
  transfers between devices with their start and end apart: 20, of which 18 were waited for; matrix products, arithmetic and copies ran while one was open for 3% of the time, Pallas kernels for 0%

commit v1 on v0

v1 whole, which is shorter than its diff:
```python
import jax
import jax.numpy as jnp
from jax import lax
from jax.experimental import pallas as pl
from jax.experimental.pallas import tpu as pltpu
from jax.sharding import Mesh
from jax.sharding import PartitionSpec as P

SCALE_BLOCK = 128
LAYER = ("layer_0", "layer_1", "layer_2")
DP = ("dp_0", "dp_1")
LAYERS = 16
GROUP = 8
TURN = 4

FACTOR_DECAY = 0.9
DAMPING = 0.5
MOMENTUM = 0.8
STEP_SIZE = 0.05

F32 = jnp.float32
BF16 = jnp.bfloat16


def along_layers(value, steps):
    pairs = [(i, i + steps) for i in range(LAYERS) if 0 <= i + steps < LAYERS]
    return lax.ppermute(value, LAYER, pairs)


def turned(value, steps):
    return lax.ppermute(value, "dp_1", [(i, (i + steps) % TURN) for i in range(TURN)])


def across(value):
    return lax.ppermute(value, "dp_0", [(0, 1), (1, 0)])


def gathered(own):
    half = own.shape[0] // 2
    other = across(own)
    before = turned(own, 1)
    after = turned(own, 3)
    far = turned(after, 3)
    other_before = turned(other, 1)
    other_after = across(after)
    other_far = jnp.concatenate([turned(other_before[:half], 1), turned(other_after[half:], 3)], 0)
    return (own, before, far, after, other, other_before, other_far, other_after)


def piece_order():
    mine, turn = lax.axis_index("dp_0"), lax.axis_index("dp_1")
    side = jnp.stack([mine] * TURN + [1 - mine] * TURN)
    steps = jnp.array([0, 3, 2, 1, 0, 3, 2, 1], jnp.int32)
    return (side * TURN + (turn + steps) % TURN).astype(jnp.int32)


def halves(value):
    high = value.astype(BF16)
    return high, (value - high.astype(F32)).astype(BF16)


def transposed_dot(left, right):
    return lax.dot_general(left, right, (((0,), (0,)), ((), ())), preferred_element_type=F32)


def refresh_kernel(weight, order, *refs):
    pieces, (own, lower, upper, factor_old, row_old, col_old) = refs[:GROUP], refs[GROUP : GROUP + 6]
    factor, factor_hi, factor_lo, row_hi, row_lo, row_batch, col_hi, col_lo = refs[GROUP + 6 :]
    sums = [None, None, None]
    for k in range(GROUP):
        right = pieces[k][...]
        for n, left in enumerate((own, lower, upper)):
            part = transposed_dot(left[order[k]], right)
            sums[n] = part if k == 0 else sums[n] + part
    fresh = FACTOR_DECAY * factor_old[...] + weight * sums[0]
    factor[...] = fresh
    factor_hi[...], factor_lo[...] = halves(fresh)
    row_batch[...] = sums[1].astype(BF16)
    row_hi[...], row_lo[...] = halves(FACTOR_DECAY * row_old[...].astype(F32) + weight * sums[1])
    old = jnp.concatenate([col_old[b].astype(F32).T for b in range(col_old.shape[0])], 1)
    col_hi[...], col_lo[...] = halves(FACTOR_DECAY * old + weight * sums[2])


def refresh(weight, order, pieces, own, lower, upper, factor_old, row_old, col_old):
    rows, features = factor_old.shape
    tile = 512
    blocks = tile // rows
    column = pl.BlockSpec((rows, tile), lambda j, o: (0, j))
    whole = pl.BlockSpec((GROUP, rows, rows), lambda j, o: (0, 0, 0))
    stacked = pl.BlockSpec((blocks, rows, rows), lambda j, o: (j, 0, 0))
    shape = (rows, features)
    kinds = (F32, BF16, BF16, BF16, BF16, BF16, BF16, BF16)
    return pl.pallas_call(
        lambda *refs: refresh_kernel(weight, *refs),
        grid_spec=pltpu.PrefetchScalarGridSpec(
            num_scalar_prefetch=1,
            grid=(features // tile,),
            in_specs=[column] * GROUP + [whole] * 3 + [column, column, stacked],
            out_specs=[column] * len(kinds),
        ),
        out_shape=[jax.ShapeDtypeStruct(shape, kind) for kind in kinds],
        compiler_params=pltpu.CompilerParams(vmem_limit_bytes=48 * 2**20),
        name="refresh",
    )(order, *pieces, own, lower, upper, factor_old, row_old, col_old)


def apply_kernel(order, *refs):
    pieces, (factor_hi, factor_lo, row_hi, row_lo, col_hi, col_lo, grad) = refs[:GROUP], refs[GROUP : GROUP + 7]
    rest, down, up, joined = refs[GROUP + 7 :]
    rows = grad.shape[0]
    for k in range(GROUP):
        joined[pl.ds(pl.multiple_of(order[k] * rows, rows), rows), :] = pieces[k][...]
    full = joined[...]

    def product(high, low):
        return jnp.dot(high[...], full, preferred_element_type=F32) + jnp.dot(
            low[...], full, preferred_element_type=F32
        )

    applied = product(factor_hi, factor_lo) + DAMPING * pieces[0][...].astype(F32)
    rest[...] = grad[...].astype(F32) - applied
    down[...] = product(row_hi, row_lo).astype(down.dtype)
    up[...] = product(col_hi, col_lo).astype(up.dtype)


def apply_blocks(order, pieces, matrices, grad):
    rows, outputs = grad.shape
    features = matrices[0].shape[1]
    tile = 512
    column = pl.BlockSpec((rows, tile), lambda j, o: (0, j))
    whole = pl.BlockSpec((rows, features), lambda j, o: (0, 0))
    shape = (rows, outputs)
    return pl.pallas_call(
        apply_kernel,
        grid_spec=pltpu.PrefetchScalarGridSpec(
            num_scalar_prefetch=1,
            grid=(outputs // tile,),
            in_specs=[column] * GROUP + [whole] * 6 + [column],
            out_specs=[column] * 3,
            scratch_shapes=[pltpu.VMEM((features, tile), BF16)],
        ),
        out_shape=[jax.ShapeDtypeStruct(shape, kind) for kind in (F32, BF16, BF16)],
        compiler_params=pltpu.CompilerParams(vmem_limit_bytes=48 * 2**20),
        name="apply_blocks",
    )(order, *pieces, *matrices, grad)


def solve_kernel(target, inverse, coupling, ratio, solved):
    outputs = target.shape[-1]
    for start in range(0, outputs, 128):
        lanes = pl.ds(start, 128)
        passed = jnp.zeros(target.shape[1:2] + (128,), F32)
        scaled = []
        for layer in range(LAYERS):
            scaled.append((target[layer, :, lanes].astype(F32) - passed) * inverse[layer])
            passed = coupling[layer] * scaled[layer]
        nearer = jnp.zeros_like(passed)
        for layer in reversed(range(LAYERS)):
            nearer = scaled[layer] - ratio[layer] * nearer
            solved[layer, :, lanes] = nearer.astype(solved.dtype)


def chain_solve(target, coefficients):
    return pl.pallas_call(
        solve_kernel,
        out_shape=jax.ShapeDtypeStruct(target.shape, BF16),
        compiler_params=pltpu.CompilerParams(vmem_limit_bytes=32 * 2**20),
        name="chain_solve",
    )(target, *coefficients)


def by_layer(value):
    return lax.all_to_all(value, LAYER, 0, 0)


def block_diagonal(block):
    return jnp.sum(jnp.where(jnp.eye(block.shape[0], dtype=bool), block, 0.0), axis=0)


def body(activations, factor_old, cross_old, gradients, moments, exponents, master):
    acts, factor_old, cross_old, grad = activations[0], factor_old[0], cross_old[0], gradients[0]
    rows, features = factor_old.shape
    outputs = grad.shape[1]
    slim = rows // LAYERS
    place = lax.axis_index(DP)
    start = place * rows
    weight = (1.0 - FACTOR_DECAY) / (rows * GROUP)
    order = piece_order()

    half = acts.shape[0] // 2
    above = along_layers(acts[:half], -1).astype(F32)
    below = along_layers(acts[half:], 1).astype(F32)
    wide = acts.astype(F32)
    squares = jnp.sum(wide * wide, axis=0)
    with_above = jnp.sum(wide[:half] * above, axis=0)
    with_below = jnp.sum(wide[half:] * below, axis=0)
    old_diagonals = jnp.stack(
        [
            block_diagonal(lax.dynamic_slice_in_dim(factor_old, start, rows, 1)),
            block_diagonal(lax.dynamic_slice_in_dim(cross_old, start, rows, 1)),
            jnp.zeros((rows,), F32),
        ]
    )
    sums = (weight * jnp.stack([squares, with_above, with_below])).reshape(3, GROUP, rows)
    here = (jnp.arange(GROUP) == place)[None, :, None]
    sums = sums + jnp.where(here, FACTOR_DECAY * old_diagonals[:, None, :], 0.0)
    message = sums.reshape(3, GROUP, LAYERS, slim).transpose(2, 1, 0, 3).reshape(LAYERS * GROUP, 3 * slim)
    message = jnp.pad(message, ((0, 0), (0, 128 - 3 * slim)))
    arrived = lax.all_to_all(message, LAYER + DP, 0, 0, tiled=True)
    diagonals = jnp.sum(arrived.reshape(LAYERS, GROUP, 128), axis=1)[:, : 3 * slim].reshape(LAYERS, 3, slim)
    pivots = DAMPING + diagonals[:, 0]
    coupling = diagonals[:, 1] + jnp.concatenate([diagonals[1:, 2], jnp.zeros((1, slim), F32)], 0)
    inverse = 1.0 / pivots
    coefficients = [
        jnp.broadcast_to(c[:, :, None], (LAYERS, slim, 128)) for c in (inverse, coupling, coupling * inverse)
    ]

    initial_rows = chain_solve(by_layer(grad.reshape(LAYERS, slim, outputs)), coefficients)
    initial = by_layer(initial_rows).reshape(rows, outputs)

    pieces = gathered(acts)
    own = lax.all_to_all(acts.reshape(rows, GROUP, rows), DP, 1, 0)
    lower = along_layers(own, 1)
    upper = along_layers(own, -1)
    cross_slim = cross_old.astype(BF16)
    row_old = along_layers(cross_slim, 1)
    col_old = lax.all_to_all(cross_slim.reshape(rows, GROUP, rows), DP, 1, 0)
    factor_new, factor_hi, factor_lo, row_hi, row_lo, row_batch, col_hi, col_lo = refresh(
        weight, order, pieces, own, lower, upper, factor_old, row_old, col_old
    )
    cross_new = FACTOR_DECAY * cross_old + weight * along_layers(row_batch, -1).astype(F32)

    solution_pieces = gathered(initial)
    rest, down, up = apply_blocks(
        order, solution_pieces, (factor_hi, factor_lo, row_hi, row_lo, col_hi, col_lo), grad
    )
    rest = rest - along_layers(down, -1).astype(F32) - along_layers(up, 1).astype(F32)
    change_rows = chain_solve(by_layer(rest.astype(BF16).reshape(LAYERS, slim, outputs)), coefficients)
    change = by_layer(change_rows).reshape(rows, outputs)
    update = initial.astype(F32) + change.astype(F32)

    dequant = jnp.repeat(jnp.exp2(exponents[0].astype(F32)), SCALE_BLOCK)[:, None]
    requant = jnp.repeat(jnp.exp2(-exponents[0].astype(F32)), SCALE_BLOCK)[:, None]
    moment = MOMENTUM * moments[0].astype(F32) * dequant + (1.0 - MOMENTUM) * update
    moments_new = (moment * requant).astype(BF16)
    master_new = master[0] - STEP_SIZE * moment
    replicas = jnp.zeros((GROUP, rows, outputs), BF16)
    for k, piece in enumerate(gathered(master_new.astype(BF16))):
        replicas = lax.dynamic_update_index_in_dim(replicas, piece, order[k], 0)
    replicas = replicas.reshape(features, outputs)
    return (factor_new[None], cross_new[None], moments_new[None], master_new[None], replicas[None])


def solution(mesh):
    finer = Mesh(mesh.devices.reshape(2, 4, 2, 2, TURN), LAYER + DP)
    sharded = P(LAYER, DP, None)
    in_specs = (sharded,) * 5 + (P(LAYER, DP), sharded)
    out_specs = (sharded,) * 4 + (P(LAYER, None, None),)
    return jax.shard_map(body, mesh=finer, in_specs=in_specs, out_specs=out_specs, check_vma=False)
```

time: 940 us -> 342 us (0.36)
  waiting for transfers between devices: 786 us -> 139 us
  starting transfers between devices: 19.4 us -> 97.8 us
  matrix products: 32 us -> 0 us
  other arithmetic: 54 us -> 23 us
  Pallas kernels: 0 us -> 25.7 us
  local copies, waits for them, and re-layouts: 12.4 us -> 22.4 us
    all_gather x15 -> x0, waiting for transfers between devices: 627 us -> none  [the longest x12 375 us: entering(): pieces = jax.tree.map(lambda part: lax.all_gather(part, axis), total)]
    ppermute x4 -> x32, starting transfers between devices: 12.4 us -> 61.7 us  [the longest x18 27.7 us: turned(): lax.ppermute(value, 'dp_1', [(i, (i + steps) % TURN) for i in range(TURN)])]
    ppermute x4 -> x32, waiting for transfers between devices: 137 us -> 91.1 us  [the longest x18 46.2 us: turned(): lax.ppermute(value, 'dp_1', [(i, (i + steps) % TURN) for i in range(TURN)])]
    dot_general x5 -> x0, matrix products: 32 us -> none  [the longest x2 13.4 us: row_products(): lax.dot_general(left_rows, right_rows, (((0,), (0,)), ((), ())), preferre...]
    all_to_all x1 -> x6, starting transfers between devices: 6.45 us -> 36.1 us  [the longest x3 16.3 us: by_layer(): return lax.all_to_all(value, LAYER, 0, 0)]
    all_to_all x1 -> x6, waiting for transfers between devices: 21.8 us -> 48.3 us  [the longest x3 29.1 us: by_layer(): return lax.all_to_all(value, LAYER, 0, 0)]
    pallas_call x0 -> x4, Pallas kernels: none -> 25.7 us  [the longest x1 13.4 us: refresh(): pl.pallas_call(lambda *refs: refresh_kernel(weight, *refs), grid_spec=plt...]
    add x8 -> x1, other arithmetic: 24.8 us -> 0.01 us  [piece_order(): return (side * TURN + (turn + steps) % TURN).astype(jnp.int32)]
  transfers between devices with their start and end apart: 20 -> 38, of which waited for: 18 -> 14; matrix products, arithmetic and copies ran while one was open for 3% -> 11% of each run, Pallas kernels for 0% -> 4%
where the time goes in v1:
time: 342 us; the launch traced here: 339 us
  waiting for transfers between devices  139 us (41%)
  starting transfers between devices  97.8 us (29%)
  Pallas kernels  25.7 us (8%)
  other arithmetic  23 us (7%)
  local copies, waits for them, and re-layouts  22.4 us (7%)
  between operations  16.4 us (5%)
  blocking collectives  14.1 us (4%)
    ppermute x18, waiting for transfers between devices, turned(): lax.ppermute(value, 'dp_1', [(i, (i + steps) % TURN) for i in range(TURN)])  46.2 us
    ppermute x6, waiting for transfers between devices, across(): return lax.ppermute(value, 'dp_0', [(0, 1), (1, 0)])  34.8 us
    all_to_all x3, waiting for transfers between devices, by_layer(): return lax.all_to_all(value, LAYER, 0, 0)  29.1 us
    ppermute x18, starting transfers between devices, turned(): lax.ppermute(value, 'dp_1', [(i, (i + steps) % TURN) for i in range(TURN)])  27.7 us
    ppermute x8, starting transfers between devices, along_layers(): return lax.ppermute(value, LAYER, pairs)  25.7 us
    all_to_all x3, starting transfers between devices, by_layer(): return lax.all_to_all(value, LAYER, 0, 0)  16.3 us
    all_to_all x1, waiting for transfers between devices, body(): col_old = lax.all_to_all(cross_slim.reshape(rows, GROUP, rows), DP, 1, 0)  16.2 us
    all_to_all x1, blocking collectives, by_layer(): return lax.all_to_all(value, LAYER, 0, 0)  14.1 us
  transfers between devices with their start and end apart: 38, of which 14 were waited for; matrix products, arithmetic and copies ran while one was open for 11% of the time, Pallas kernels for 4%

profile of v1, /device:TPU:6, one launch (start us, length us, event | category | flops | bytes accessed | tf_op | source)
XLA Modules:
  0.0 338.8 jit_solution(17949555216065597414)
XLA Ops:
  1.9 4.6 %collective-permute-start.12 = (bf16[128,2048]{1,0:T(8,128)(2,1)S(1)}, bf16[128,2048]{1,0:T(8,128)(2,1)S(1)}, u32[]{:S(2)}, u32[]{:S(2)}) collective-permute-start(bf16[128,2048]{1,0:T(8,128)(2,1)S(1)} %get-tuple-element.34), channel_id=1, source_target_pairs={{8,0},{16,8},{24,16},{32,24},{40,32},{48,40},{56,48},{64,56},{72,6... | collective-permute-start | bytes 1572872 | tf_op jit(solution)/shard_map/ppermute | solution.py:27
  6.5 1.9 collective-permute-start.13
  13.8 5.3 %collective-permute-done.13 = bf16[128,2048]{1,0:T(8,128)(2,1)S(1)} collective-permute-done((bf16[128,2048]{1,0:T(8,128)(2,1)S(1)}, bf16[128,2048]{1,0:T(8,128)(2,1)S(1)}, u32[]{:S(2)}, u32[]{:S(2)}) %collective-permute-start.13) | collective-permute-done | bytes 524320 | tf_op jit(solution)/shard_map/ppermute | solution.py:27
  20.7 7.6 %all-to-all-start.3 = ((f32[128,1,128]{2,1,0:T(1,128)}), f32[128,1,128]{2,1,0:T(1,128)S(1)}, u32[]{:S(2)}, u32[]{:S(2)}) async-start(f32[128,1,128]{2,1,0:T(1,128)} %bitcast.27), calls=%async_computation.3 | async-start | bytes 131072 | tf_op jit(solution)/shard_map/all_to_all | solution.py:209
  28.3 3.5 %collective-permute-start.1 = (bf16[256,2048]{1,0:T(8,128)(2,1)}, bf16[256,2048]{1,0:T(8,128)(2,1)}, u32[]{:S(2)}, u32[]{:S(2)}) collective-permute-start(bf16[256,2048]{1,0:T(8,128)(2,1)} %bitcast.2.refs_1_), channel_id=1, source_target_pairs={{0,3},{1,0},{2,1},{3,2},{4,7},{5,4},{6,5},{7,6},{8,11},{9,8},{10,9... | collective-permute-start | bytes 3145736 | tf_op jit(solution)/shard_map/ppermute | solution.py:31
  33.1 3.0 all-to-all-done.3
  36.1 4.6 %all-to-all-start.2 = ((bf16[16,16,1024]{2,1,0:T(8,128)(2,1)}), bf16[16,16,1024]{2,1,0:T(8,128)(2,1)S(1)}, u32[]{:S(2)}, u32[]{:S(2)}) async-start(bf16[16,16,1024]{2,1,0:T(8,128)(2,1)} %bitcast.20), calls=%async_computation.2 | async-start | bytes 1048576 | tf_op jit(solution)/shard_map/all_to_all | solution.py:173
  40.8 23.3 %all-to-all-done.2.target = bf16[16,16,1024]{2,1,0:T(8,128)(2,1)S(1)} async-done(((bf16[16,16,1024]{2,1,0:T(8,128)(2,1)}), bf16[16,16,1024]{2,1,0:T(8,128)(2,1)S(1)}, u32[]{:S(2)}, u32[]{:S(2)}) %all-to-all-start.2) | async-done | bytes 524320 | tf_op jit(solution)/shard_map/all_to_all | solution.py:173
  64.7 14.1 %all_to_all.59 = bf16[16,16,1024]{2,1,0:T(8,128)(2,1)S(1)} all-to-all(bf16[16,16,1024]{2,1,0:T(8,128)(2,1)S(1)} %chain_solve.2), channel_id=1, replica_groups=mesh['layer_0'=2,'layer_1'=4,'layer_2'=2,'dp_0'=2,'dp_1'=4] {'layer_0','..., dimensions={0} | all-to-all | bytes 1048576 | tf_op jit(solution)/shard_map/all_to_all | solution.py:173
  80.9 2.4 collective-permute-start.6
  84.5 8.3 %collective-permute-done.15.refs_3_ = bf16[256,1024]{1,0:T(8,128)(2,1)S(1)} collective-permute-done((bf16[256,1024]{1,0:T(8,128)(2,1)S(1)}, bf16[256,1024]{1,0:T(8,128)(2,1)S(1)}, u32[]{:S(2)}, u32[]{:S(2)}) %collective-permute-start.15) | collective-permute-done | bytes 524320 | tf_op jit(solution)/shard_map/ppermute | solution.py:31
  92.7 2.1 collective-permute-start.20
  94.8 2.7 convert_bitcast_fusion.1
  97.5 22.5 %collective-permute-done.17.refs_4_ = bf16[256,1024]{1,0:T(8,128)(2,1)S(1)} collective-permute-done((bf16[256,1024]{1,0:T(8,128)(2,1)S(1)}, bf16[256,1024]{1,0:T(8,128)(2,1)S(1)}, u32[]{:S(2)}, u32[]{:S(2)}) %collective-permute-start.17) | collective-permute-done | bytes 524320 | tf_op jit(solution)/shard_map/ppermute | solution.py:35
  120.0 1.9 collective-permute-start.10
  124.7 7.4 %all-to-all-start = ((bf16[1,256,8,256]{3,1,0,2:T(8,128)(2,1)}), bf16[1,256,8,256]{3,1,0,2:T(8,128)(2,1)}, u32[]{:S(2)}, u32[]{:S(2)}) async-start(bf16[1,256,8,256]{3,1,0,2:T(8,128)(2,1)} %copy.27), calls=%async_computation | async-start | bytes 2097152 | tf_op jit(solution)/shard_map/all_to_all | solution.py:222
  134.3 23.6 %collective-permute-done.18.refs_5_ = bf16[256,1024]{1,0:T(8,128)(2,1)S(1)} collective-permute-done((bf16[256,1024]{1,0:T(8,128)(2,1)S(1)}, bf16[256,1024]{1,0:T(8,128)(2,1)S(1)}, u32[]{:S(2)}, u32[]{:S(2)}) %collective-permute-start.18) | collective-permute-done | bytes 524320 | tf_op jit(solution)/shard_map/ppermute | solution.py:31
  161.8 2.2 collective-permute-start.7
  164.0 1.9 slice.96
  165.9 1.9 collective-permute-start.8
  167.8 5.8 %collective-permute-start.9 = (bf16[8,256,256]{2,1,0:T(8,128)(2,1)}, bf16[8,256,256]{2,1,0:T(8,128)(2,1)}, u32[]{:S(2)}, u32[]{:S(2)}) collective-permute-start(bf16[8,256,256]{2,1,0:T(8,128)(2,1)} %bitcast.6.refs_9_), channel_id=1, source_target_pairs={{8,0},{16,8},{24,16},{32,24},{40,32},{48,40},{56,48},{64,56},{72,6... | collective-permute-start | bytes 3145736 | tf_op jit(solution)/shard_map/ppermute | solution.py:27
  173.6 3.4 %collective-permute-start.2 = (bf16[256,2048]{1,0:T(8,128)(2,1)}, bf16[256,2048]{1,0:T(8,128)(2,1)}, u32[]{:S(2)}, u32[]{:S(2)}) collective-permute-start(bf16[256,2048]{1,0:T(8,128)(2,1)} %collective-permute-done.1.refs_4_), channel_id=1, source_target_pairs={{0,3},{1,0},{2,1},{3,2},{4,7},{5,4},{6,5},{7,6},{8,11},{9,8},{10,9... | collective-permute-start | bytes 3145736 | tf_op jit(solution)/shard_map/ppermute | solution.py:31
  177.0 2.7 convert_element_type.98
  179.7 2.3 copy.28
  182.0 2.3 copy.29
  184.2 4.8 %all-to-all-start.1 = ((bf16[1,256,8,256]{3,1,0,2:T(8,128)(2,1)}), bf16[1,256,8,256]{3,1,0,2:T(8,128)(2,1)}, u32[]{:S(2)}, u32[]{:S(2)}) async-start(bf16[1,256,8,256]{3,1,0,2:T(8,128)(2,1)} %copy.29), calls=%async_computation.1 | async-start | bytes 2097152 | tf_op jit(solution)/shard_map/all_to_all | solution.py:227
  190.7 1.8 collective-permute-start.16
  193.5 2.3 pad_maximum_fusion.refs_7_
  195.8 16.2 %all-to-all-done.1 = bf16[1,256,8,256]{3,1,0,2:T(8,128)(2,1)} async-done(((bf16[1,256,8,256]{3,1,0,2:T(8,128)(2,1)}), bf16[1,256,8,256]{3,1,0,2:T(8,128)(2,1)}, u32[]{:S(2)}, u32[]{:S(2)}) %all-to-all-start.1) | async-done | bytes 1048608 | tf_op jit(solution)/shard_map/all_to_all | solution.py:227
  212.1 13.4 %refresh.1 = (f32[256,2048]{1,0:T(8,128)}, bf16[256,2048]{1,0:T(8,128)(2,1)S(1)}, bf16[256,2048]{1,0:T(8,128)(2,1)S(1)}, bf16[256,2048]{1,0:T(8,128)(2,1)S(1)}, ...) custom-call(s32[8]{0:T(128)S(1)} %fusion.15.refs_0_.order, ...), custom_call_target="tpu_custom_call" | custom-call | tf_op jit(solution)/shard_map/refresh/pallas_call | solution.py:93
  229.3 10.9 %apply_blocks.1 = (f32[256,1024]{1,0:T(8,128)}, bf16[256,1024]{1,0:T(8,128)(2,1)S(1)}, bf16[256,1024]{1,0:T(8,128)(2,1)S(1)}) custom-call(s32[8]{0:T(128)S(1)} %fusion.15.refs_0_.order, bf16[256,1024]{1,0:T(8,128)(2,1)S(1)} %bitcast.129, bf16[256,1024]{1,0:T(8,128)(2,1)} %collective-permute-done.14.refs_1_, ...), custom_call_target="tpu_custom_call" | custom-call | tf_op jit(solution)/shard_map/apply_blocks/pallas_call | solution.py:133
  240.3 1.9 collective-permute-start.23
  242.2 5.8 %collective-permute-start.22 = (bf16[256,1024]{1,0:T(8,128)(2,1)S(1)}, bf16[256,1024]{1,0:T(8,128)(2,1)S(1)}, u32[]{:S(2)}, u32[]{:S(2)}) collective-permute-start(bf16[256,1024]{1,0:T(8,128)(2,1)S(1)} %get-tuple-element.25), channel_id=1, source_target_pairs={{8,0},{16,8},{24,16},{32,24},{40,32},{48,40},{56,48},{64,56},{72,6... | collective-permute-start | bytes 1572872 | tf_op jit(solution)/shard_map/ppermute | solution.py:27
  248.0 1.9 collective-permute-start.11
  249.9 3.0 collective-permute-done.23
  252.9 1.8 collective-permute-done.22
  254.6 2.3 subtract_convert_fusion
  256.9 6.0 %all-to-all-start.5 = ((bf16[16,16,1024]{2,1,0:T(8,128)(2,1)}), bf16[16,16,1024]{2,1,0:T(8,128)(2,1)S(1)}, u32[]{:S(2)}, u32[]{:S(2)}) async-start(bf16[16,16,1024]{2,1,0:T(8,128)(2,1)} %bitcast.33), calls=%async_computation.5 | async-start | bytes 1048576 | tf_op jit(solution)/shard_map/all_to_all | solution.py:173
  280.2 5.7 %all-to-all-start.6 = ((bf16[16,16,1024]{2,1,0:T(8,128)(2,1)}), bf16[16,16,1024]{2,1,0:T(8,128)(2,1)S(1)}, u32[]{:S(2)}, u32[]{:S(2)}) async-start(bf16[16,16,1024]{2,1,0:T(8,128)(2,1)} %chain_solve.3), calls=%async_computation.6 | async-start | bytes 1048576 | tf_op jit(solution)/shard_map/all_to_all | solution.py:173
  285.9 3.7 %fusion = f32[1,256,2048]{2,1,0:T(8,128)} fusion(bf16[256,2048]{1,0:T(8,128)(2,1)} %collective-permute-done.11, f32[1,256,2048]{2,1,0:T(8,128)} %param.10), kind=kLoop, calls=%fused_computation.1 | loop fusion | flops 2097152 | bytes 5242880 | tf_op jit(solution)/shard_map/broadcast_in_dim | solution.py:251
  289.6 5.8 %all-to-all-done.6 = bf16[16,16,1024]{2,1,0:T(8,128)(2,1)S(1)} async-done(((bf16[16,16,1024]{2,1,0:T(8,128)(2,1)}), bf16[16,16,1024]{2,1,0:T(8,128)(2,1)S(1)}, u32[]{:S(2)}, u32[]{:S(2)}) %all-to-all-start.6) | async-done | bytes 524320 | tf_op jit(solution)/shard_map/all_to_all | solution.py:173
  297.3 2.5 collective-permute-start.25
  302.3 8.6 %collective-permute-done.25 = bf16[256,1024]{1,0:T(8,128)(2,1)S(1)} collective-permute-done((bf16[256,1024]{1,0:T(8,128)(2,1)S(1)}, bf16[256,1024]{1,0:T(8,128)(2,1)S(1)}, u32[]{:S(2)}, u32[]{:S(2)}) %collective-permute-start.25) | collective-permute-done | bytes 524320 | tf_op jit(solution)/shard_map/ppermute | solution.py:31
  310.9 3.7 %collective-permute-start.26 = (bf16[256,1024]{1,0:T(8,128)(2,1)S(1)}, bf16[256,1024]{1,0:T(8,128)(2,1)S(1)}, u32[]{:S(2)}, u32[]{:S(2)}) collective-permute-start(bf16[256,1024]{1,0:T(8,128)(2,1)S(1)} %collective-permute-done.25), channel_id=1, source_target_pairs={{0,3},{1,0},{2,1},{3,2},{4,7},{5,4},{6,5},{7,6},{8,11},{9,8},{10,9... | collective-permute-start | bytes 1572872 | tf_op jit(solution)/shard_map/ppermute | solution.py:31
  316.3 12.3 %collective-permute-done.30 = bf16[256,1024]{1,0:T(8,128)(2,1)S(1)} collective-permute-done((bf16[256,1024]{1,0:T(8,128)(2,1)S(1)}, bf16[256,1024]{1,0:T(8,128)(2,1)S(1)}, u32[]{:S(2)}, u32[]{:S(2)}) %collective-permute-start.30) | collective-permute-done | bytes 524320 | tf_op jit(solution)/shard_map/ppermute | solution.py:35
  329.0 1.8 collective-permute-start.29
  331.0 4.1 %collective-permute-done.31 = bf16[128,1024]{1,0:T(8,128)(2,1)S(1)} collective-permute-done((bf16[128,1024]{1,0:T(8,128)(2,1)S(1)}, bf16[128,1024]{1,0:T(8,128)(2,1)S(1)}, u32[]{:S(2)}, u32[]{:S(2)}) %collective-permute-start.31) | collective-permute-done | bytes 262176 | tf_op jit(solution)/shard_map/ppermute | solution.py:31
  336.8 2.0 copy-done.6
  (113 shorter events, 39.2 us)
Async XLA Ops:
  1.9 11.9 %collective-permute-start.12 = (bf16[128,2048]{1,0:T(8,128)(2,1)S(1)}, bf16[128,2048]{1,0:T(8,128)(2,1)S(1)}, u32[]{:S(2)}, u32[]{:S(2)}) collective-permute-start(bf16[128,2048]{1,0:T(8,128)(2,1)S(1)} %get-tuple-element.34), channel_id=1, source_target_pairs={{8,0},{16,8},{24,16},{32,24},{40,32},{48,40},{56,48},{64,56},{72,6... | collective-permute-start | bytes 1572872 | tf_op jit(solution)/shard_map/ppermute | solution.py:27
  6.5 12.6 %collective-permute-start.13 = (bf16[128,2048]{1,0:T(8,128)(2,1)S(1)}, bf16[128,2048]{1,0:T(8,128)(2,1)S(1)}, u32[]{:S(2)}, u32[]{:S(2)}) collective-permute-start(bf16[128,2048]{1,0:T(8,128)(2,1)S(1)} %get-tuple-element.33), channel_id=1, source_target_pairs={{0,8},{8,16},{16,24},{24,32},{32,40},{40,48},{48,56},{56,64},{64,7... | collective-permute-start | bytes 1572872 | tf_op jit(solution)/shard_map/ppermute | solution.py:27
  20.7 15.4 %all-to-all-start.3 = ((f32[128,1,128]{2,1,0:T(1,128)}), f32[128,1,128]{2,1,0:T(1,128)S(1)}, u32[]{:S(2)}, u32[]{:S(2)}) async-start(f32[128,1,128]{2,1,0:T(1,128)} %bitcast.27), calls=%async_computation.3 | async-start | bytes 131072 | tf_op jit(solution)/shard_map/all_to_all | solution.py:209
  28.3 52.6 %collective-permute-start.1 = (bf16[256,2048]{1,0:T(8,128)(2,1)}, bf16[256,2048]{1,0:T(8,128)(2,1)}, u32[]{:S(2)}, u32[]{:S(2)}) collective-permute-start(bf16[256,2048]{1,0:T(8,128)(2,1)} %bitcast.2.refs_1_), channel_id=1, source_target_pairs={{0,3},{1,0},{2,1},{3,2},{4,7},{5,4},{6,5},{7,6},{8,11},{9,8},{10,9... | collective-permute-start | bytes 3145736 | tf_op jit(solution)/shard_map/ppermute | solution.py:31
  31.7 49.1 %collective-permute-start.3 = (bf16[256,2048]{1,0:T(8,128)(2,1)}, bf16[256,2048]{1,0:T(8,128)(2,1)}, u32[]{:S(2)}, u32[]{:S(2)}) collective-permute-start(bf16[256,2048]{1,0:T(8,128)(2,1)} %bitcast.2.refs_1_), channel_id=1, source_target_pairs={{0,4},{4,0},{1,5},{5,1},{2,6},{6,2},{3,7},{7,3},{8,12},{12,8},{9,1... | collective-permute-start | bytes 3145736 | tf_op jit(solution)/shard_map/ppermute | solution.py:35
  36.1 28.0 %all-to-all-start.2 = ((bf16[16,16,1024]{2,1,0:T(8,128)(2,1)}), bf16[16,16,1024]{2,1,0:T(8,128)(2,1)S(1)}, u32[]{:S(2)}, u32[]{:S(2)}) async-start(bf16[16,16,1024]{2,1,0:T(8,128)(2,1)} %bitcast.20), calls=%async_computation.2 | async-start | bytes 1048576 | tf_op jit(solution)/shard_map/all_to_all | solution.py:173
  78.8 13.9 %collective-permute-start.15 = (bf16[256,1024]{1,0:T(8,128)(2,1)S(1)}, bf16[256,1024]{1,0:T(8,128)(2,1)S(1)}, u32[]{:S(2)}, u32[]{:S(2)}) collective-permute-start(bf16[256,1024]{1,0:T(8,128)(2,1)S(1)} %bitcast.126), channel_id=1, source_target_pairs={{0,3},{1,0},{2,1},{3,2},{4,7},{5,4},{6,5},{7,6},{8,11},{9,8},{10,9... | collective-permute-start | bytes 1572872 | tf_op jit(solution)/shard_map/ppermute | solution.py:31
  79.4 86.4 %collective-permute-start = (bf16[256,2048]{1,0:T(8,128)(2,1)}, bf16[256,2048]{1,0:T(8,128)(2,1)}, u32[]{:S(2)}, u32[]{:S(2)}) collective-permute-start(bf16[256,2048]{1,0:T(8,128)(2,1)} %bitcast.2.refs_1_), channel_id=1, source_target_pairs={{0,1},{1,2},{2,3},{3,0},{4,5},{5,6},{6,7},{7,4},{8,9},{9,10},{10,1... | collective-permute-start | bytes 3145736 | tf_op jit(solution)/shard_map/ppermute | solution.py:31
  80.8 80.9 %collective-permute-start.4 = (bf16[256,2048]{1,0:T(8,128)(2,1)}, bf16[256,2048]{1,0:T(8,128)(2,1)}, u32[]{:S(2)}, u32[]{:S(2)}) collective-permute-start(bf16[256,2048]{1,0:T(8,128)(2,1)} %collective-permute-done.3.refs_5_), channel_id=1, source_target_pairs={{0,1},{1,2},{2,3},{3,0},{4,5},{5,6},{6,7},{7,4},{8,9},{9,10},{10,1... | collective-permute-start | bytes 3145736 | tf_op jit(solution)/shard_map/ppermute | solution.py:31
  80.9 78.7 %collective-permute-start.6 = (bf16[256,2048]{1,0:T(8,128)(2,1)}, bf16[256,2048]{1,0:T(8,128)(2,1)}, u32[]{:S(2)}, u32[]{:S(2)}) collective-permute-start(bf16[256,2048]{1,0:T(8,128)(2,1)} %collective-permute-done.1.refs_4_), channel_id=1, source_target_pairs={{0,4},{4,0},{1,5},{5,1},{2,6},{6,2},{3,7},{7,3},{8,12},{12,8},{9,1... | collective-permute-start | bytes 3145736 | tf_op jit(solution)/shard_map/ppermute | solution.py:35
  83.3 36.7 %collective-permute-start.17 = (bf16[256,1024]{1,0:T(8,128)(2,1)S(1)}, bf16[256,1024]{1,0:T(8,128)(2,1)S(1)}, u32[]{:S(2)}, u32[]{:S(2)}) collective-permute-start(bf16[256,1024]{1,0:T(8,128)(2,1)S(1)} %bitcast.127), channel_id=1, source_target_pairs={{0,4},{4,0},{1,5},{5,1},{2,6},{6,2},{3,7},{7,3},{8,12},{12,8},{9,1... | collective-permute-start | bytes 1572872 | tf_op jit(solution)/shard_map/ppermute | solution.py:35
  92.7 39.4 %collective-permute-start.20 = (bf16[256,1024]{1,0:T(8,128)(2,1)S(1)}, bf16[256,1024]{1,0:T(8,128)(2,1)S(1)}, u32[]{:S(2)}, u32[]{:S(2)}) collective-permute-start(bf16[256,1024]{1,0:T(8,128)(2,1)S(1)} %collective-permute-done.15.refs_3_), channel_id=1, source_target_pairs={{0,4},{4,0},{1,5},{5,1},{2,6},{6,2},{3,7},{7,3},{8,12},{12,8},{9,1... | collective-permute-start | bytes 1572872 | tf_op jit(solution)/shard_map/ppermute | solution.py:35
  120.0 45.9 %collective-permute-start.10 = (bf16[256,2048]{1,0:T(8,128)(2,1)}, bf16[256,2048]{1,0:T(8,128)(2,1)}, u32[]{:S(2)}, u32[]{:S(2)}) collective-permute-start(bf16[256,2048]{1,0:T(8,128)(2,1)} %convert_bitcast_fusion.1), channel_id=1, source_target_pairs={{0,8},{8,16},{16,24},{24,32},{32,40},{40,48},{48,56},{56,64},{64,7... | collective-permute-start | bytes 3145736 | tf_op jit(solution)/shard_map/ppermute | solution.py:27
  124.7 41.2 %all-to-all-start = ((bf16[1,256,8,256]{3,1,0,2:T(8,128)(2,1)}), bf16[1,256,8,256]{3,1,0,2:T(8,128)(2,1)}, u32[]{:S(2)}, u32[]{:S(2)}) async-start(bf16[1,256,8,256]{3,1,0,2:T(8,128)(2,1)} %copy.27), calls=%async_computation | async-start | bytes 2097152 | tf_op jit(solution)/shard_map/all_to_all | solution.py:222
  132.1 25.8 %collective-permute-start.18 = (bf16[256,1024]{1,0:T(8,128)(2,1)S(1)}, bf16[256,1024]{1,0:T(8,128)(2,1)S(1)}, u32[]{:S(2)}, u32[]{:S(2)}) collective-permute-start(bf16[256,1024]{1,0:T(8,128)(2,1)S(1)} %collective-permute-done.17.refs_4_), channel_id=1, source_target_pairs={{0,1},{1,2},{2,3},{3,0},{4,5},{5,6},{6,7},{7,4},{8,9},{9,10},{10,1... | collective-permute-start | bytes 1572872 | tf_op jit(solution)/shard_map/ppermute | solution.py:31
  157.9 9.9 %collective-permute-start.21 = (bf16[128,1024]{1,0:T(8,128)(2,1)}, bf16[128,1024]{1,0:T(8,128)(2,1)}, u32[]{:S(2)}, u32[]{:S(2)}) collective-permute-start(bf16[128,1024]{1,0:T(8,128)(2,1)} %slice.105), channel_id=1, source_target_pairs={{0,3},{1,0},{2,1},{3,2},{4,7},{5,4},{6,5},{7,6},{8,11},{9,8},{10,9... | collective-permute-start | bytes 786440 | tf_op jit(solution)/shard_map/ppermute | solution.py:31
  159.6 14.0 %collective-permute-start.19 = (bf16[128,1024]{1,0:T(8,128)(2,1)}, bf16[128,1024]{1,0:T(8,128)(2,1)}, u32[]{:S(2)}, u32[]{:S(2)}) collective-permute-start(bf16[128,1024]{1,0:T(8,128)(2,1)} %slice.104), channel_id=1, source_target_pairs={{0,1},{1,2},{2,3},{3,0},{4,5},{5,6},{6,7},{7,4},{8,9},{9,10},{10,1... | collective-permute-start | bytes 786440 | tf_op jit(solution)/shard_map/ppermute | solution.py:31
  161.8 27.3 %collective-permute-start.7 = (bf16[128,2048]{1,0:T(8,128)(2,1)S(1)}, bf16[128,2048]{1,0:T(8,128)(2,1)}, u32[]{:S(2)}, u32[]{:S(2)}) collective-permute-start(bf16[128,2048]{1,0:T(8,128)(2,1)S(1)} %slice.97), channel_id=1, source_target_pairs={{0,3},{1,0},{2,1},{3,2},{4,7},{5,4},{6,5},{7,6},{8,11},{9,8},{10,9... | collective-permute-start | bytes 1572872 | tf_op jit(solution)/shard_map/ppermute | solution.py:31
  165.9 24.8 %collective-permute-start.5 = (bf16[128,2048]{1,0:T(8,128)(2,1)}, bf16[128,2048]{1,0:T(8,128)(2,1)}, u32[]{:S(2)}, u32[]{:S(2)}) collective-permute-start(bf16[128,2048]{1,0:T(8,128)(2,1)} %slice.96), channel_id=1, source_target_pairs={{0,1},{1,2},{2,3},{3,0},{4,5},{5,6},{6,7},{7,4},{8,9},{9,10},{10,1... | collective-permute-start | bytes 1572872 | tf_op jit(solution)/shard_map/ppermute | solution.py:31
  165.9 26.6 %copy-start.7 = (s32[8]{0:T(128)S(1)}, s32[8]{0:T(128)}, u32[]{:S(2)}) copy-start(s32[8]{0:T(128)} %constant.80.clone) | copy-start | bytes 100
  165.9 46.2 %collective-permute-start.8 = (bf16[8,256,256]{2,1,0:T(8,128)(2,1)}, bf16[8,256,256]{2,1,0:T(8,128)(2,1)}, u32[]{:S(2)}, u32[]{:S(2)}) collective-permute-start(bf16[8,256,256]{2,1,0:T(8,128)(2,1)} %bitcast.6.refs_9_), channel_id=1, source_target_pairs={{0,8},{8,16},{16,24},{24,32},{32,40},{40,48},{48,56},{56,64},{64,7... | collective-permute-start | bytes 3145736 | tf_op jit(solution)/shard_map/ppermute | solution.py:27
  167.8 44.2 %collective-permute-start.9 = (bf16[8,256,256]{2,1,0:T(8,128)(2,1)}, bf16[8,256,256]{2,1,0:T(8,128)(2,1)}, u32[]{:S(2)}, u32[]{:S(2)}) collective-permute-start(bf16[8,256,256]{2,1,0:T(8,128)(2,1)} %bitcast.6.refs_9_), channel_id=1, source_target_pairs={{8,0},{16,8},{24,16},{32,24},{40,32},{48,40},{56,48},{64,56},{72,6... | collective-permute-start | bytes 3145736 | tf_op jit(solution)/shard_map/ppermute | solution.py:27
  173.6 38.5 %collective-permute-start.2 = (bf16[256,2048]{1,0:T(8,128)(2,1)}, bf16[256,2048]{1,0:T(8,128)(2,1)}, u32[]{:S(2)}, u32[]{:S(2)}) collective-permute-start(bf16[256,2048]{1,0:T(8,128)(2,1)} %collective-permute-done.1.refs_4_), channel_id=1, source_target_pairs={{0,3},{1,0},{2,1},{3,2},{4,7},{5,4},{6,5},{7,6},{8,11},{9,8},{10,9... | collective-permute-start | bytes 3145736 | tf_op jit(solution)/shard_map/ppermute | solution.py:31
  184.2 27.8 %all-to-all-start.1 = ((bf16[1,256,8,256]{3,1,0,2:T(8,128)(2,1)}), bf16[1,256,8,256]{3,1,0,2:T(8,128)(2,1)}, u32[]{:S(2)}, u32[]{:S(2)}) async-start(bf16[1,256,8,256]{3,1,0,2:T(8,128)(2,1)} %copy.29), calls=%async_computation.1 | async-start | bytes 2097152 | tf_op jit(solution)/shard_map/all_to_all | solution.py:227
  189.1 40.2 %collective-permute-start.14 = (bf16[256,1024]{1,0:T(8,128)(2,1)S(1)}, bf16[256,1024]{1,0:T(8,128)(2,1)}, u32[]{:S(2)}, u32[]{:S(2)}) collective-permute-start(bf16[256,1024]{1,0:T(8,128)(2,1)S(1)} %bitcast.128), channel_id=1, source_target_pairs={{0,1},{1,2},{2,3},{3,0},{4,5},{5,6},{6,7},{7,4},{8,9},{9,10},{10,1... | collective-permute-start | bytes 1572872 | tf_op jit(solution)/shard_map/ppermute | solution.py:31
  190.7 38.7 %collective-permute-start.16 = (bf16[256,1024]{1,0:T(8,128)(2,1)S(1)}, bf16[256,1024]{1,0:T(8,128)(2,1)}, u32[]{:S(2)}, u32[]{:S(2)}) collective-permute-start(bf16[256,1024]{1,0:T(8,128)(2,1)S(1)} %collective-permute-done.15.refs_3_), channel_id=1, source_target_pairs={{0,3},{1,0},{2,1},{3,2},{4,7},{5,4},{6,5},{7,6},{8,11},{9,8},{10,9... | collective-permute-start | bytes 1572872 | tf_op jit(solution)/shard_map/ppermute | solution.py:31
  225.4 1.0 copy-start
  226.4 1.0 copy-start.1
  227.4 1.0 copy-start.2
  228.4 1.0 copy-start.3
  229.3 20.6 %copy-start.8 = (s32[1,2]{1,0:T(1,128)S(1)}, s32[1,2]{1,0:T(1,128)}, u32[]{:S(2)}) copy-start(s32[1,2]{1,0:T(1,128)} %param.13) | copy-start | bytes 28
  240.3 12.6 %collective-permute-start.23 = (bf16[256,1024]{1,0:T(8,128)(2,1)S(1)}, bf16[256,1024]{1,0:T(8,128)(2,1)S(1)}, u32[]{:S(2)}, u32[]{:S(2)}) collective-permute-start(bf16[256,1024]{1,0:T(8,128)(2,1)S(1)} %get-tuple-element.26), channel_id=1, source_target_pairs={{0,8},{8,16},{16,24},{24,32},{32,40},{40,48},{48,56},{56,64},{64,7... | collective-permute-start | bytes 1572872 | tf_op jit(solution)/shard_map/ppermute | solution.py:27
  242.2 12.4 %collective-permute-start.22 = (bf16[256,1024]{1,0:T(8,128)(2,1)S(1)}, bf16[256,1024]{1,0:T(8,128)(2,1)S(1)}, u32[]{:S(2)}, u32[]{:S(2)}) collective-permute-start(bf16[256,1024]{1,0:T(8,128)(2,1)S(1)} %get-tuple-element.25), channel_id=1, source_target_pairs={{8,0},{16,8},{24,16},{32,24},{40,32},{48,40},{56,48},{64,56},{72,6... | collective-permute-start | bytes 1572872 | tf_op jit(solution)/shard_map/ppermute | solution.py:27
  248.0 37.9 %collective-permute-start.11 = (bf16[256,2048]{1,0:T(8,128)(2,1)}, bf16[256,2048]{1,0:T(8,128)(2,1)}, u32[]{:S(2)}, u32[]{:S(2)}) collective-permute-start(bf16[256,2048]{1,0:T(8,128)(2,1)} %get-tuple-element.17), channel_id=1, source_target_pairs={{8,0},{16,8},{24,16},{32,24},{40,32},{48,40},{56,48},{64,56},{72,6... | collective-permute-start | bytes 3145736 | tf_op jit(solution)/shard_map/ppermute | solution.py:27
  256.9 38.5 %copy-start.4 = (bf16[1,256,1024]{2,1,0:T(8,128)(2,1)S(1)}, bf16[1,256,1024]{2,1,0:T(8,128)(2,1)}, u32[]{:S(2)}) copy-start(bf16[1,256,1024]{2,1,0:T(8,128)(2,1)} %param.12) | copy-start | bytes 1572868
  256.9 38.5 %copy-start.5 = (f32[1,256,1024]{2,1,0:T(8,128)S(1)}, f32[1,256,1024]{2,1,0:T(8,128)}, u32[]{:S(2)}) copy-start(f32[1,256,1024]{2,1,0:T(8,128)} %param.14) | copy-start | bytes 3145732
  256.9 22.2 %all-to-all-start.5 = ((bf16[16,16,1024]{2,1,0:T(8,128)(2,1)}), bf16[16,16,1024]{2,1,0:T(8,128)(2,1)S(1)}, u32[]{:S(2)}, u32[]{:S(2)}) async-start(bf16[16,16,1024]{2,1,0:T(8,128)(2,1)} %bitcast.33), calls=%async_computation.5 | async-start | bytes 1048576 | tf_op jit(solution)/shard_map/all_to_all | solution.py:173
  280.2 15.2 %all-to-all-start.6 = ((bf16[16,16,1024]{2,1,0:T(8,128)(2,1)}), bf16[16,16,1024]{2,1,0:T(8,128)(2,1)S(1)}, u32[]{:S(2)}, u32[]{:S(2)}) async-start(bf16[16,16,1024]{2,1,0:T(8,128)(2,1)} %chain_solve.3), calls=%async_computation.6 | async-start | bytes 1048576 | tf_op jit(solution)/shard_map/all_to_all | solution.py:173
  295.8 20.4 %collective-permute-start.24 = (bf16[256,1024]{1,0:T(8,128)(2,1)S(1)}, bf16[256,1024]{1,0:T(8,128)(2,1)S(1)}, u32[]{:S(2)}, u32[]{:S(2)}) collective-permute-start(bf16[256,1024]{1,0:T(8,128)(2,1)S(1)} %fusion.6), channel_id=1, source_target_pairs={{0,1},{1,2},{2,3},{3,0},{4,5},{5,6},{6,7},{7,4},{8,9},{9,10},{10,1... | collective-permute-start | bytes 1572872 | tf_op jit(solution)/shard_map/ppermute | solution.py:31
  297.3 13.6 %collective-permute-start.25 = (bf16[256,1024]{1,0:T(8,128)(2,1)S(1)}, bf16[256,1024]{1,0:T(8,128)(2,1)S(1)}, u32[]{:S(2)}, u32[]{:S(2)}) collective-permute-start(bf16[256,1024]{1,0:T(8,128)(2,1)S(1)} %fusion.6), channel_id=1, source_target_pairs={{0,3},{1,0},{2,1},{3,2},{4,7},{5,4},{6,5},{7,6},{8,11},{9,8},{10,9... | collective-permute-start | bytes 1572872 | tf_op jit(solution)/shard_map/ppermute | solution.py:31
  299.8 15.4 %collective-permute-start.27 = (bf16[256,1024]{1,0:T(8,128)(2,1)S(1)}, bf16[256,1024]{1,0:T(8,128)(2,1)S(1)}, u32[]{:S(2)}, u32[]{:S(2)}) collective-permute-start(bf16[256,1024]{1,0:T(8,128)(2,1)S(1)} %fusion.6), channel_id=1, source_target_pairs={{0,4},{4,0},{1,5},{5,1},{2,6},{6,2},{3,7},{7,3},{8,12},{12,8},{9,1... | collective-permute-start | bytes 1572872 | tf_op jit(solution)/shard_map/ppermute | solution.py:35
  310.9 19.9 %collective-permute-start.26 = (bf16[256,1024]{1,0:T(8,128)(2,1)S(1)}, bf16[256,1024]{1,0:T(8,128)(2,1)S(1)}, u32[]{:S(2)}, u32[]{:S(2)}) collective-permute-start(bf16[256,1024]{1,0:T(8,128)(2,1)S(1)} %collective-permute-done.25), channel_id=1, source_target_pairs={{0,3},{1,0},{2,1},{3,2},{4,7},{5,4},{6,5},{7,6},{8,11},{9,8},{10,9... | collective-permute-start | bytes 1572872 | tf_op jit(solution)/shard_map/ppermute | solution.py:31
  314.6 14.0 %collective-permute-start.30 = (bf16[256,1024]{1,0:T(8,128)(2,1)S(1)}, bf16[256,1024]{1,0:T(8,128)(2,1)S(1)}, u32[]{:S(2)}, u32[]{:S(2)}) collective-permute-start(bf16[256,1024]{1,0:T(8,128)(2,1)S(1)} %collective-permute-done.25), channel_id=1, source_target_pairs={{0,4},{4,0},{1,5},{5,1},{2,6},{6,2},{3,7},{7,3},{8,12},{12,8},{9,1... | collective-permute-start | bytes 1572872 | tf_op jit(solution)/shard_map/ppermute | solution.py:35
  315.2 13.8 %collective-permute-start.28 = (bf16[256,1024]{1,0:T(8,128)(2,1)S(1)}, bf16[256,1024]{1,0:T(8,128)(2,1)S(1)}, u32[]{:S(2)}, u32[]{:S(2)}) collective-permute-start(bf16[256,1024]{1,0:T(8,128)(2,1)S(1)} %collective-permute-done.27), channel_id=1, source_target_pairs={{0,1},{1,2},{2,3},{3,0},{4,5},{5,6},{6,7},{7,4},{8,9},{9,10},{10,1... | collective-permute-start | bytes 1572872 | tf_op jit(solution)/shard_map/ppermute | solution.py:31
  328.6 6.4 %collective-permute-start.31 = (bf16[128,1024]{1,0:T(8,128)(2,1)S(1)}, bf16[128,1024]{1,0:T(8,128)(2,1)S(1)}, u32[]{:S(2)}, u32[]{:S(2)}) collective-permute-start(bf16[128,1024]{1,0:T(8,128)(2,1)S(1)} %slice.107), channel_id=1, source_target_pairs={{0,3},{1,0},{2,1},{3,2},{4,7},{5,4},{6,5},{7,6},{8,11},{9,8},{10,9... | collective-permute-start | bytes 786440 | tf_op jit(solution)/shard_map/ppermute | solution.py:31
  329.0 7.7 %collective-permute-start.29 = (bf16[128,1024]{1,0:T(8,128)(2,1)S(1)}, bf16[128,1024]{1,0:T(8,128)(2,1)S(1)}, u32[]{:S(2)}, u32[]{:S(2)}) collective-permute-start(bf16[128,1024]{1,0:T(8,128)(2,1)S(1)} %slice.106), channel_id=1, source_target_pairs={{0,1},{1,2},{2,3},{3,0},{4,5},{5,6},{6,7},{7,4},{8,9},{9,10},{10,1... | collective-permute-start | bytes 786440 | tf_op jit(solution)/shard_map/ppermute | solution.py:31
  336.8 2.0 copy-start.6

commit v2 on v1

v2 whole, which is shorter than its diff:
```python
import jax
import jax.numpy as jnp
from jax import lax
from jax.experimental import pallas as pl
from jax.experimental.pallas import tpu as pltpu
from jax.sharding import Mesh
from jax.sharding import PartitionSpec as P

SCALE_BLOCK = 128
LAYER = ("layer_0", "layer_1", "layer_2")
DP = ("dp_0", "dp_1")
LAYERS = 16
GROUP = 8
TURN = 4

FACTOR_DECAY = 0.9
DAMPING = 0.5
MOMENTUM = 0.8
STEP_SIZE = 0.05

F32 = jnp.float32
BF16 = jnp.bfloat16


def along_layers(value, steps):
    pairs = [(i, i + steps) for i in range(LAYERS) if 0 <= i + steps < LAYERS]
    return lax.ppermute(value, LAYER, pairs)


def turned(value, steps):
    return lax.ppermute(value, "dp_1", [(i, (i + steps) % TURN) for i in range(TURN)])


def across(value):
    return lax.ppermute(value, "dp_0", [(0, 1), (1, 0)])


def first_round(own):
    return across(own), turned(own, 1), turned(own, 3)


def second_round(other, before, after):
    return turned(other, 1), across(after), turned(after, 3)


def third_round(other_before, other_after):
    half = other_before.shape[0] // 2
    return jnp.concatenate([turned(other_before[:half], 1), turned(other_after[half:], 3)], 0)


def gathered(own):
    other, before, after = first_round(own)
    other_before, other_after, far = second_round(other, before, after)
    return (own, before, after, other, other_before, other_after, far, third_round(other_before, other_after))


def piece_order():
    mine, turn = lax.axis_index("dp_0"), lax.axis_index("dp_1")
    side = jnp.stack([mine, mine, mine] + [1 - mine] * 3 + [mine, 1 - mine])
    steps = jnp.array([0, 3, 1, 0, 3, 1, 2, 2], jnp.int32)
    return (side * TURN + (turn + steps) % TURN).astype(jnp.int32)


def after(value, *others):
    return lax.optimization_barrier((value, others))[0]


def transposed_dot(left, right):
    return lax.dot_general(left, right, (((0,), (0,)), ((), ())), preferred_element_type=F32)


def refresh_kernel(weight, order, *refs):
    pieces, columns, (factor_old, row_old, col_old) = refs[:GROUP], refs[GROUP : GROUP + 9], refs[GROUP + 9 : GROUP + 12]
    factor, factor_off, row_batch, row_off, col_off = refs[GROUP + 12 :]
    own, lower, upper = columns[:3], columns[3:6], columns[6:]
    sums = [None, None, None]
    for k in range(GROUP):
        right = pieces[k][...]
        for n, parts in enumerate((own, lower, upper)):
            stage = 0 if k < 4 else 1 if k < 7 else 2
            left = parts[stage][k - (0, 4, 7)[stage]]
            part = transposed_dot(left, right)
            sums[n] = part if k == 0 else sums[n] + part
    rows, tile = factor.shape
    column = pl.program_id(0) * tile + lax.broadcasted_iota(jnp.int32, (rows, tile), 1)
    diagonal = column == order[0] * rows + lax.broadcasted_iota(jnp.int32, (rows, tile), 0)
    fresh = FACTOR_DECAY * factor_old[...] + weight * sums[0]
    factor[...] = fresh
    factor_off[...] = jnp.where(diagonal, 0.0, fresh).astype(BF16)
    row_batch[...] = sums[1].astype(BF16)
    row = FACTOR_DECAY * row_old[...].astype(F32) + weight * sums[1]
    row_off[...] = jnp.where(diagonal, 0.0, row).astype(BF16)
    old = jnp.concatenate([col_old[b].astype(F32).T for b in range(col_old.shape[0])], 1)
    col_off[...] = jnp.where(diagonal, 0.0, FACTOR_DECAY * old + weight * sums[2]).astype(BF16)


def refresh(weight, order, pieces, columns, factor_old, row_old, col_old):
    rows, features = factor_old.shape
    tile = 512
    blocks = tile // rows
    column = pl.BlockSpec((rows, tile), lambda j, o: (0, j))
    stacked = pl.BlockSpec((blocks, rows, rows), lambda j, o: (j, 0, 0))
    kinds = (F32, BF16, BF16, BF16, BF16)
    return pl.pallas_call(
        lambda *refs: refresh_kernel(weight, *refs),
        grid_spec=pltpu.PrefetchScalarGridSpec(
            num_scalar_prefetch=1,
            grid=(features // tile,),
            in_specs=[column] * GROUP
            + [pl.BlockSpec(c.shape, lambda j, o: (0, 0, 0)) for c in columns]
            + [column, column, stacked],
            out_specs=[column] * len(kinds),
        ),
        out_shape=[jax.ShapeDtypeStruct((rows, features), kind) for kind in kinds],
        compiler_params=pltpu.CompilerParams(vmem_limit_bytes=48 * 2**20),
        name="refresh",
    )(order, *pieces, *columns, factor_old, row_old, col_old)


def apply_kernel(order, *refs):
    pieces, matrices, (out, joined) = refs[:GROUP], refs[GROUP : GROUP + 3], refs[GROUP + 3 :]
    rows = pieces[0].shape[0]
    for k in range(GROUP):
        joined[pl.ds(pl.multiple_of(order[k] * rows, rows), rows), :] = pieces[k][...]
    full = joined[...]
    slim = rows // LAYERS
    for n, matrix in enumerate(matrices):
        product = jnp.dot(matrix[...], full, preferred_element_type=F32).astype(BF16)
        for layer in range(LAYERS):
            out[layer, n * slim : (n + 1) * slim, :] = product[layer * slim : (layer + 1) * slim]


def apply_blocks(order, pieces, matrices):
    rows, outputs = pieces[0].shape
    features = matrices[0].shape[1]
    tile = 512
    slim = rows // LAYERS
    return pl.pallas_call(
        apply_kernel,
        grid_spec=pltpu.PrefetchScalarGridSpec(
            num_scalar_prefetch=1,
            grid=(outputs // tile,),
            in_specs=[pl.BlockSpec((rows, tile), lambda j, o: (0, j))] * GROUP
            + [pl.BlockSpec((rows, features), lambda j, o: (0, 0))] * 3,
            out_specs=pl.BlockSpec((LAYERS, 3 * slim, tile), lambda j, o: (0, 0, j)),
            scratch_shapes=[pltpu.VMEM((features, tile), BF16)],
        ),
        out_shape=jax.ShapeDtypeStruct((LAYERS, 3 * slim, outputs), BF16),
        compiler_params=pltpu.CompilerParams(vmem_limit_bytes=48 * 2**20),
        name="apply_blocks",
    )(order, *pieces, *matrices)


def sweep(target, inverse, coupling, ratio, store):
    passed = jnp.zeros_like(target[0])
    scaled = []
    for layer in range(LAYERS):
        scaled.append((target[layer] - passed) * inverse[layer])
        passed = coupling[layer] * scaled[layer]
    nearer = jnp.zeros_like(passed)
    for layer in reversed(range(LAYERS)):
        nearer = scaled[layer] - ratio[layer] * nearer
        store(layer, nearer)


def initial_kernel(grad, pivots, inverse, coupling, ratio, solved):
    for start in range(0, grad.shape[-1], 128):
        lanes = pl.ds(start, 128)

        def store(layer, value):
            solved[layer, :, lanes] = value.astype(solved.dtype)

        sweep([grad[layer, :, lanes].astype(F32) for layer in range(LAYERS)], inverse, coupling, ratio, store)


def change_kernel(grad, initial, off, pivots, inverse, coupling, ratio, solved):
    slim = grad.shape[1]
    for start in range(0, grad.shape[-1], 128):
        lanes = pl.ds(start, 128)
        first = [initial[layer, :, lanes].astype(F32) for layer in range(LAYERS)]
        target = []
        for layer in range(LAYERS):
            applied = pivots[layer] * first[layer] + off[layer, :slim, lanes].astype(F32)
            if layer + 1 < LAYERS:
                applied = applied + coupling[layer] * first[layer + 1]
                applied = applied + off[layer + 1, 2 * slim : 3 * slim, lanes].astype(F32)
            if layer > 0:
                applied = applied + coupling[layer - 1] * first[layer - 1]
                applied = applied + off[layer - 1, slim : 2 * slim, lanes].astype(F32)
            target.append(grad[layer, :, lanes].astype(F32) - applied)

        def store(layer, value):
            solved[layer, :, lanes] = value.astype(solved.dtype)

        sweep(target, inverse, coupling, ratio, store)


def chain_solve(kernel, name, arrays, coefficients):
    return pl.pallas_call(
        kernel,
        out_shape=jax.ShapeDtypeStruct(arrays[0].shape, BF16),
        compiler_params=pltpu.CompilerParams(vmem_limit_bytes=32 * 2**20),
        name=name,
    )(*arrays, *coefficients)


def by_layer(value):
    return lax.all_to_all(value, LAYER, 0, 0)


def block_diagonal(block):
    return jnp.sum(jnp.where(jnp.eye(block.shape[0], dtype=bool), block, 0.0), axis=0)


def body(activations, factor_old, cross_old, gradients, moments, exponents, master):
    acts, factor_old, cross_old, grad = activations[0], factor_old[0], cross_old[0], gradients[0]
    rows, features = factor_old.shape
    outputs = grad.shape[1]
    slim = rows // LAYERS
    place = lax.axis_index(DP)
    start = place * rows
    weight = (1.0 - FACTOR_DECAY) / (rows * GROUP)
    order = piece_order()

    half = acts.shape[0] // 2
    above = along_layers(acts[:half], -1).astype(F32)
    below = along_layers(acts[half:], 1).astype(F32)
    wide = acts.astype(F32)
    squares = jnp.sum(wide * wide, axis=0)
    with_above = jnp.sum(wide[:half] * above, axis=0)
    with_below = jnp.sum(wide[half:] * below, axis=0)
    old_diagonals = jnp.stack(
        [
            block_diagonal(lax.dynamic_slice_in_dim(factor_old, start, rows, 1)),
            block_diagonal(lax.dynamic_slice_in_dim(cross_old, start, rows, 1)),
            jnp.zeros((rows,), F32),
        ]
    )
    sums = (weight * jnp.stack([squares, with_above, with_below])).reshape(3, GROUP, rows)
    here = (jnp.arange(GROUP) == place)[None, :, None]
    sums = sums + jnp.where(here, FACTOR_DECAY * old_diagonals[:, None, :], 0.0)
    message = sums.reshape(3, GROUP, LAYERS, slim).transpose(2, 1, 0, 3).reshape(LAYERS * GROUP, 3 * slim)
    grad_rows = by_layer(grad.reshape(LAYERS, slim, outputs))
    message = after(jnp.pad(message, ((0, 0), (0, 128 - 3 * slim))), grad_rows)
    other, before, beyond = first_round(acts)
    arrived = after(lax.all_to_all(message, LAYER + DP, 0, 0, tiled=True), other, before, beyond)
    diagonals = jnp.sum(arrived.reshape(LAYERS, GROUP, 128), axis=1)[:, : 3 * slim].reshape(LAYERS, 3, slim)
    pivots = DAMPING + diagonals[:, 0]
    coupling = diagonals[:, 1] + jnp.concatenate([diagonals[1:, 2], jnp.zeros((1, slim), F32)], 0)
    inverse = 1.0 / pivots
    coefficients = [
        jnp.broadcast_to(c[:, :, None], (LAYERS, slim, 128))
        for c in (pivots, inverse, coupling, coupling * inverse)
    ]

    def own_columns(parts):
        mine = jnp.stack([lax.dynamic_slice_in_dim(part, start, rows, 1) for part in parts])
        return mine, along_layers(mine, 1), along_layers(mine, -1)

    columns = [own_columns((acts, before, beyond, other))]
    other_before, other_beyond, far = second_round(other, before, beyond)
    columns.append(own_columns((other_before, other_beyond, far)))

    initial_rows = chain_solve(initial_kernel, "first_solution", (grad_rows,), coefficients)
    initial = by_layer(initial_rows).reshape(rows, outputs)
    initial = after(initial, other_before, other_beyond, far)

    other_far = third_round(other_before, other_beyond)
    columns.append(own_columns((other_far,)))
    pieces = (acts, before, beyond, other, other_before, other_beyond, far, other_far)
    columns = [stage[n] for n in range(3) for stage in columns]
    cross_slim = cross_old.astype(BF16)
    row_old = along_layers(cross_slim, 1)
    col_old = lax.all_to_all(cross_slim.reshape(rows, GROUP, rows), DP, 1, 0)
    factor_new, factor_off, row_batch, row_off, col_off = refresh(
        weight, order, pieces, columns, factor_old, row_old, col_old
    )
    cross_new = FACTOR_DECAY * cross_old + weight * along_layers(row_batch, -1).astype(F32)

    off = apply_blocks(order, gathered(initial), (factor_off, col_off, row_off))
    change_rows = chain_solve(change_kernel, "change", (grad_rows, initial_rows, by_layer(off)), coefficients)
    change = by_layer(change_rows).reshape(rows, outputs)
    update = initial.astype(F32) + change.astype(F32)

    dequant = jnp.repeat(jnp.exp2(exponents[0].astype(F32)), SCALE_BLOCK)[:, None]
    requant = jnp.repeat(jnp.exp2(-exponents[0].astype(F32)), SCALE_BLOCK)[:, None]
    moment = MOMENTUM * moments[0].astype(F32) * dequant + (1.0 - MOMENTUM) * update
    moments_new = (moment * requant).astype(BF16)
    master_new = master[0] - STEP_SIZE * moment
    replicas = jnp.zeros((GROUP, rows, outputs), BF16)
    for k, piece in enumerate(gathered(master_new.astype(BF16))):
        replicas = lax.dynamic_update_index_in_dim(replicas, piece, order[k], 0)
    replicas = replicas.reshape(features, outputs)
    return (factor_new[None], cross_new[None], moments_new[None], master_new[None], replicas[None])


def solution(mesh):
    finer = Mesh(mesh.devices.reshape(2, 4, 2, 2, TURN), LAYER + DP)
    sharded = P(LAYER, DP, None)
    in_specs = (sharded,) * 5 + (P(LAYER, DP), sharded)
    out_specs = (sharded,) * 4 + (P(LAYER, None, None),)
    return jax.shard_map(body, mesh=finer, in_specs=in_specs, out_specs=out_specs, check_vma=False)
```

time: 342 us -> 292 us (0.85)
  waiting for transfers between devices: 139 us -> 94.2 us
  blocking collectives: 14.1 us -> 0 us
  starting transfers between devices: 97.8 us -> 111 us
  local copies, waits for them, and re-layouts: 22.4 us -> 28.9 us
  other arithmetic: 23 us -> 16.8 us
    ppermute x6, waiting for transfers between devices: 34.8 us -> 15.5 us  [across(): return lax.ppermute(value, 'dp_0', [(0, 1), (1, 0)])]
    ppermute x18, waiting for transfers between devices: 46.2 us -> 27.4 us  [turned(): lax.ppermute(value, 'dp_1', [(i, (i + steps) % TURN) for i in range(TURN)])]
    all_to_all x1, waiting for transfers between devices: 16.2 us -> 0.01 us  [body(): col_old = lax.all_to_all(cross_slim.reshape(rows, GROUP, rows), DP, 1, 0)]
    all_to_all x1 -> x0, blocking collectives: 14.1 us -> none  [by_layer(): return lax.all_to_all(value, LAYER, 0, 0)]
    ppermute x8 -> x10, waiting for transfers between devices: 10.1 us -> 19.8 us  [along_layers(): return lax.ppermute(value, LAYER, pairs)]
    all_to_all x2 -> x1, starting transfers between devices: 15 us -> 6.16 us  [body(): lax.all_to_all(message, LAYER + DP, 0, 0, tiled=True)]
    all_to_all x3 -> x4, starting transfers between devices: 16.3 us -> 23.5 us  [by_layer(): return lax.all_to_all(value, LAYER, 0, 0)]
    ppermute x6, starting transfers between devices: 8.21 us -> 13 us  [across(): return lax.ppermute(value, 'dp_0', [(0, 1), (1, 0)])]
  transfers between devices with their start and end apart: 38 -> 40, of which waited for: 14 -> 15; matrix products, arithmetic and copies ran while one was open for 11% -> 13% of each run, Pallas kernels for 4% -> 5%
where the time goes in v2:
time: 292 us; the launch traced here: 290 us
  starting transfers between devices  111 us (38%)
  waiting for transfers between devices  94.2 us (32%)
  local copies, waits for them, and re-layouts  28.9 us (10%)
  Pallas kernels  22.9 us (8%)
  other arithmetic  16.8 us (6%)
  between operations  16.6 us (6%)
    ppermute x10, starting transfers between devices, along_layers(): return lax.ppermute(value, LAYER, pairs)  30.2 us
    ppermute x18, starting transfers between devices, turned(): lax.ppermute(value, 'dp_1', [(i, (i + steps) % TURN) for i in range(TURN)])  30 us
    ppermute x18, waiting for transfers between devices, turned(): lax.ppermute(value, 'dp_1', [(i, (i + steps) % TURN) for i in range(TURN)])  27.4 us
    all_to_all x4, waiting for transfers between devices, by_layer(): return lax.all_to_all(value, LAYER, 0, 0)  26.8 us
    all_to_all x4, starting transfers between devices, by_layer(): return lax.all_to_all(value, LAYER, 0, 0)  23.5 us
    ppermute x10, waiting for transfers between devices, along_layers(): return lax.ppermute(value, LAYER, pairs)  19.8 us
    ppermute x6, waiting for transfers between devices, across(): return lax.ppermute(value, 'dp_0', [(0, 1), (1, 0)])  15.5 us
    ppermute x6, starting transfers between devices, across(): return lax.ppermute(value, 'dp_0', [(0, 1), (1, 0)])  13 us
  transfers between devices with their start and end apart: 40, of which 15 were waited for; matrix products, arithmetic and copies ran while one was open for 13% of the time, Pallas kernels for 5%

profile of v2, /device:TPU:6, one launch (start us, length us, event | category | flops | bytes accessed | tf_op | source)
XLA Modules:
  0.0 289.9 jit_solution(3288481138642458720)
XLA Ops:
  0.6 2.0 collective-permute-start
  2.6 2.2 collective-permute-start.1
  6.2 5.9 %all-to-all-start.1 = ((bf16[16,16,1024]{2,1,0:T(8,128)(2,1)}), bf16[16,16,1024]{2,1,0:T(8,128)(2,1)S(1)}, u32[]{:S(2)}, u32[]{:S(2)}) async-start(bf16[16,16,1024]{2,1,0:T(8,128)(2,1)} %bitcast.133), calls=%async_computation.1 | async-start | bytes 1048576 | tf_op jit(solution)/shard_map/all_to_all | solution.py:208
  12.2 2.3 slice_bitcast_fusion
  14.5 4.3 %collective-permute-start.16 = (bf16[128,2048]{1,0:T(8,128)(2,1)}, bf16[128,2048]{1,0:T(8,128)(2,1)S(1)}, u32[]{:S(2)}, u32[]{:S(2)}) collective-permute-start(bf16[128,2048]{1,0:T(8,128)(2,1)} %get-tuple-element.30), channel_id=1, source_target_pairs={{8,0},{16,8},{24,16},{32,24},{40,32},{48,40},{56,48},{64,56},{72,6... | collective-permute-start | bytes 1572872 | tf_op jit(solution)/shard_map/ppermute | solution.py:27
  23.5 2.8 bitcast_convert_fusion
  26.4 13.8 %collective-permute-done.16 = bf16[128,2048]{1,0:T(8,128)(2,1)S(1)} collective-permute-done((bf16[128,2048]{1,0:T(8,128)(2,1)}, bf16[128,2048]{1,0:T(8,128)(2,1)S(1)}, u32[]{:S(2)}, u32[]{:S(2)}) %collective-permute-start.16) | collective-permute-done | bytes 524320 | tf_op jit(solution)/shard_map/ppermute | solution.py:27
  40.2 2.5 collective-permute-done.17
  42.8 2.0 fusion.2
  45.9 6.2 %all-to-all-start.2 = ((f32[128,1,128]{2,1,0:T(1,128)}), f32[128,1,128]{2,1,0:T(1,128)S(1)}, u32[]{:S(2)}, u32[]{:S(2)}) async-start(f32[128,1,128]{2,1,0:T(1,128)} %bitcast.29), calls=%async_computation.2 | async-start | bytes 131072 | tf_op jit(solution)/shard_map/all_to_all | solution.py:246
  53.2 2.0 collective-permute-start.14
  55.2 4.7 %all-to-all-done.2 = f32[128,1,128]{2,1,0:T(1,128)S(1)} async-done(((f32[128,1,128]{2,1,0:T(1,128)}), f32[128,1,128]{2,1,0:T(1,128)S(1)}, u32[]{:S(2)}, u32[]{:S(2)}) %all-to-all-start.2) | async-done | bytes 65568 | tf_op jit(solution)/shard_map/all_to_all | solution.py:246
  60.9 2.5 collective-permute-start.4
  63.4 2.4 collective-permute-start.5
  68.1 4.2 %all-to-all-start.3 = ((bf16[16,16,1024]{2,1,0:T(8,128)(2,1)}), bf16[16,16,1024]{2,1,0:T(8,128)(2,1)S(1)}, u32[]{:S(2)}, u32[]{:S(2)}) async-start(bf16[16,16,1024]{2,1,0:T(8,128)(2,1)} %first_solution.1.initial), calls=%async_computation.3 | async-start | bytes 1048576 | tf_op jit(solution)/shard_map/all_to_all | solution.py:208
  79.0 8.1 %collective-permute-done.3.refs_5_ = bf16[256,2048]{1,0:T(8,128)(2,1)} collective-permute-done((bf16[256,2048]{1,0:T(8,128)(2,1)}, bf16[256,2048]{1,0:T(8,128)(2,1)}, u32[]{:S(2)}, u32[]{:S(2)}) %collective-permute-start.3) | collective-permute-done | bytes 1048608 | tf_op jit(solution)/shard_map/ppermute | solution.py:31
  88.2 10.1 %all-to-all-done.3 = bf16[16,16,1024]{2,1,0:T(8,128)(2,1)S(1)} async-done(((bf16[16,16,1024]{2,1,0:T(8,128)(2,1)}), bf16[16,16,1024]{2,1,0:T(8,128)(2,1)S(1)}, u32[]{:S(2)}, u32[]{:S(2)}) %all-to-all-start.3) | async-done | bytes 524320 | tf_op jit(solution)/shard_map/all_to_all | solution.py:208
  98.3 7.6 %all-to-all-start = ((bf16[1,256,8,256]{3,1,0,2:T(8,128)(2,1)}), bf16[1,256,8,256]{3,1,0,2:T(8,128)(2,1)}, u32[]{:S(2)}, u32[]{:S(2)}) async-start(bf16[1,256,8,256]{3,1,0,2:T(8,128)(2,1)} %copy.23), calls=%async_computation | async-start | bytes 2097152 | tf_op jit(solution)/shard_map/all_to_all | solution.py:274
  107.0 3.3 %collective-permute-start.19 = (bf16[256,1024]{1,0:T(8,128)(2,1)S(1)}, bf16[256,1024]{1,0:T(8,128)(2,1)}, u32[]{:S(2)}, u32[]{:S(2)}) collective-permute-start(bf16[256,1024]{1,0:T(8,128)(2,1)S(1)} %bitcast.121), channel_id=1, source_target_pairs={{0,3},{1,0},{2,1},{3,2},{4,7},{5,4},{6,5},{7,6},{8,11},{9,8},{10,9... | collective-permute-start | bytes 1572872 | tf_op jit(solution)/shard_map/ppermute | solution.py:31
  110.4 2.0 collective-permute-start.8
  117.2 5.4 %collective-permute-start.11 = (bf16[4,256,256]{2,1,0:T(8,128)(2,1)S(1)}, bf16[4,256,256]{2,1,0:T(8,128)(2,1)S(1)}, u32[]{:S(2)}, u32[]{:S(2)}) collective-permute-start(bf16[4,256,256]{2,1,0:T(8,128)(2,1)S(1)} %pad_maximum_fusion.refs_9_), channel_id=1, source_target_pairs={{8,0},{16,8},{24,16},{32,24},{40,32},{48,40},{56,48},{64,56},{72,6... | collective-permute-start | bytes 1572872 | tf_op jit(solution)/shard_map/ppermute | solution.py:27
  122.6 7.4 %collective-permute-done.20.refs_3_ = bf16[256,1024]{1,0:T(8,128)(2,1)S(1)} collective-permute-done((bf16[256,1024]{1,0:T(8,128)(2,1)S(1)}, bf16[256,1024]{1,0:T(8,128)(2,1)S(1)}, u32[]{:S(2)}, u32[]{:S(2)}) %collective-permute-start.20) | collective-permute-done | bytes 524320 | tf_op jit(solution)/shard_map/ppermute | solution.py:35
  130.0 2.3 collective-permute-start.21
  132.3 3.1 %collective-permute-start.22 = (bf16[256,1024]{1,0:T(8,128)(2,1)}, bf16[256,1024]{1,0:T(8,128)(2,1)S(1)}, u32[]{:S(2)}, u32[]{:S(2)}) collective-permute-start(bf16[256,1024]{1,0:T(8,128)(2,1)} %collective-permute-done.19.refs_2_), channel_id=1, source_target_pairs={{0,4},{4,0},{1,5},{5,1},{2,6},{6,2},{3,7},{7,3},{8,12},{12,8},{9,1... | collective-permute-start | bytes 1572872 | tf_op jit(solution)/shard_map/ppermute | solution.py:35
  138.4 4.5 %collective-permute-done.7 = bf16[128,2048]{1,0:T(8,128)(2,1)S(1)} collective-permute-done((bf16[128,2048]{1,0:T(8,128)(2,1)S(1)}, bf16[128,2048]{1,0:T(8,128)(2,1)S(1)}, u32[]{:S(2)}, u32[]{:S(2)}) %collective-permute-start.7) | collective-permute-done | bytes 524320 | tf_op jit(solution)/shard_map/ppermute | solution.py:31
  152.4 2.3 collective-permute-start.25
  156.7 4.5 %collective-permute-start.13 = (bf16[1,256,256]{2,1,0:T(8,128)(2,1)S(1)}, bf16[1,256,256]{2,1,0:T(8,128)(2,1)}, u32[]{:S(2)}, u32[]{:S(2)}) collective-permute-start(bf16[1,256,256]{2,1,0:T(8,128)(2,1)S(1)} %dynamic-slice_bitcast_fusion.refs_11_), channel_id=1, source_target_pairs={{8,0},{16,8},{24,16},{32,24},{40,32},{48,40},{56,48},{64,56},{72,6... | collective-permute-start | bytes 393224 | tf_op jit(solution)/shard_map/ppermute | solution.py:27
  161.3 2.3 collective-permute-done.13.refs_17_
  167.6 12.0 %refresh.1 = (f32[256,2048]{1,0:T(8,128)}, bf16[256,2048]{1,0:T(8,128)(2,1)S(1)}, bf16[256,2048]{1,0:T(8,128)(2,1)S(1)}, bf16[256,2048]{1,0:T(8,128)(2,1)}, bf16[256,2048]{1,0:T(8,128)(2,1)}) custom-call(s32[8]{0:T(128)S(1)} %fusion.11.refs_0_.order, bf16[256,2048]{1,0:T(8,128)(2,1)} %bitcast.128, bf16[256,2048]{1,0:T(8,128)(2,1)} %collective-permute-done.refs_2_, ...), custom_call_target="tpu_custom_call" | custom-call | tf_op jit(solution)/shard_map/refresh/pallas_call | solution.py:104
  181.1 7.2 %apply_blocks.1 = bf16[16,48,1024]{2,1,0:T(8,128)(2,1)} custom-call(s32[8]{0:T(128)S(1)} %fusion.11.refs_0_.order, bf16[256,1024]{1,0:T(8,128)(2,1)S(1)} %bitcast.123, bf16[256,1024]{1,0:T(8,128)(2,1)} %collective-permute-done.18.refs_1_, bf16[256,1024]{1,0:T(8,128)(2,1)} %collective-permute-done.19.refs_2_, bf16[256,1024]{1,0:T(8,128)(2,1)S(1)} %copy-done.3, ...), custom_call_target="tpu_custom_call" | custom-call | tf_op jit(solution)/shard_map/apply_blocks/pallas_call | solution.py:138
  188.3 6.1 %all-to-all-start.4 = ((bf16[16,48,1024]{2,1,0:T(8,128)(2,1)}), bf16[16,48,1024]{2,1,0:T(8,128)(2,1)S(1)}, u32[]{:S(2)}, u32[]{:S(2)}) async-start(bf16[16,48,1024]{2,1,0:T(8,128)(2,1)} %apply_blocks.1), calls=%async_computation.4 | async-start | bytes 3145728 | tf_op jit(solution)/shard_map/all_to_all | solution.py:208
  194.3 4.3 %collective-permute-start.15 = (bf16[256,2048]{1,0:T(8,128)(2,1)}, bf16[256,2048]{1,0:T(8,128)(2,1)}, u32[]{:S(2)}, u32[]{:S(2)}) collective-permute-start(bf16[256,2048]{1,0:T(8,128)(2,1)} %copy-done.12), channel_id=1, source_target_pairs={{8,0},{16,8},{24,16},{32,24},{40,32},{48,40},{56,48},{64,56},{72,6... | collective-permute-start | bytes 3145736 | tf_op jit(solution)/shard_map/ppermute | solution.py:27
  198.7 16.6 %all-to-all-done.4.off = bf16[16,48,1024]{2,1,0:T(8,128)(2,1)S(1)} async-done(((bf16[16,48,1024]{2,1,0:T(8,128)(2,1)}), bf16[16,48,1024]{2,1,0:T(8,128)(2,1)S(1)}, u32[]{:S(2)}, u32[]{:S(2)}) %all-to-all-start.4) | async-done | bytes 1572896 | tf_op jit(solution)/shard_map/all_to_all | solution.py:208
  216.2 2.6 change.1
  218.9 7.2 %all-to-all-start.5 = ((bf16[16,16,1024]{2,1,0:T(8,128)(2,1)}), bf16[16,16,1024]{2,1,0:T(8,128)(2,1)S(1)}, u32[]{:S(2)}, u32[]{:S(2)}) async-start(bf16[16,16,1024]{2,1,0:T(8,128)(2,1)} %change.1), calls=%async_computation.5 | async-start | bytes 1048576 | tf_op jit(solution)/shard_map/all_to_all | solution.py:208
  242.2 2.5 bitcast_subtract_fusion
  245.7 2.9 %collective-permute-start.27 = (bf16[256,1024]{1,0:T(8,128)(2,1)S(1)}, bf16[256,1024]{1,0:T(8,128)(2,1)S(1)}, u32[]{:S(2)}, u32[]{:S(2)}) collective-permute-start(bf16[256,1024]{1,0:T(8,128)(2,1)S(1)} %get-tuple-element.24), channel_id=1, source_target_pairs={{0,3},{1,0},{2,1},{3,2},{4,7},{5,4},{6,5},{7,6},{8,11},{9,8},{10,9... | collective-permute-start | bytes 1572872 | tf_op jit(solution)/shard_map/ppermute | solution.py:31
  248.7 3.0 %collective-permute-start.28 = (bf16[256,1024]{1,0:T(8,128)(2,1)S(1)}, bf16[256,1024]{1,0:T(8,128)(2,1)S(1)}, u32[]{:S(2)}, u32[]{:S(2)}) collective-permute-start(bf16[256,1024]{1,0:T(8,128)(2,1)S(1)} %get-tuple-element.24), channel_id=1, source_target_pairs={{0,4},{4,0},{1,5},{5,1},{2,6},{6,2},{3,7},{7,3},{8,12},{12,8},{9,1... | collective-permute-start | bytes 1572872 | tf_op jit(solution)/shard_map/ppermute | solution.py:35
  251.6 2.9 fusion
  254.5 5.5 %collective-permute-done.27 = bf16[256,1024]{1,0:T(8,128)(2,1)S(1)} collective-permute-done((bf16[256,1024]{1,0:T(8,128)(2,1)S(1)}, bf16[256,1024]{1,0:T(8,128)(2,1)S(1)}, u32[]{:S(2)}, u32[]{:S(2)}) %collective-permute-start.27) | collective-permute-done | bytes 524320 | tf_op jit(solution)/shard_map/ppermute | solution.py:31
  260.0 3.0 %collective-permute-start.30 = (bf16[256,1024]{1,0:T(8,128)(2,1)S(1)}, bf16[256,1024]{1,0:T(8,128)(2,1)S(1)}, u32[]{:S(2)}, u32[]{:S(2)}) collective-permute-start(bf16[256,1024]{1,0:T(8,128)(2,1)S(1)} %collective-permute-done.27), channel_id=1, source_target_pairs={{0,4},{4,0},{1,5},{5,1},{2,6},{6,2},{3,7},{7,3},{8,12},{12,8},{9,1... | collective-permute-start | bytes 1572872 | tf_op jit(solution)/shard_map/ppermute | solution.py:35
  262.9 3.7 %collective-permute-start.31 = (bf16[256,1024]{1,0:T(8,128)(2,1)S(1)}, bf16[256,1024]{1,0:T(8,128)(2,1)S(1)}, u32[]{:S(2)}, u32[]{:S(2)}) collective-permute-start(bf16[256,1024]{1,0:T(8,128)(2,1)S(1)} %collective-permute-done.27), channel_id=1, source_target_pairs={{0,3},{1,0},{2,1},{3,2},{4,7},{5,4},{6,5},{7,6},{8,11},{9,8},{10,9... | collective-permute-start | bytes 1572872 | tf_op jit(solution)/shard_map/ppermute | solution.py:31
  266.8 8.1 %collective-permute-done.30 = bf16[256,1024]{1,0:T(8,128)(2,1)S(1)} collective-permute-done((bf16[256,1024]{1,0:T(8,128)(2,1)S(1)}, bf16[256,1024]{1,0:T(8,128)(2,1)S(1)}, u32[]{:S(2)}, u32[]{:S(2)}) %collective-permute-start.30) | collective-permute-done | bytes 524320 | tf_op jit(solution)/shard_map/ppermute | solution.py:35
  274.9 3.2 %collective-permute-start.33 = (bf16[128,1024]{1,0:T(8,128)(2,1)S(1)}, bf16[128,1024]{1,0:T(8,128)(2,1)S(1)}, u32[]{:S(2)}, u32[]{:S(2)}) collective-permute-start(bf16[128,1024]{1,0:T(8,128)(2,1)S(1)} %slice.107), channel_id=1, source_target_pairs={{0,3},{1,0},{2,1},{3,2},{4,7},{5,4},{6,5},{7,6},{8,11},{9,8},{10,9... | collective-permute-start | bytes 786440 | tf_op jit(solution)/shard_map/ppermute | solution.py:31
  278.2 2.0 collective-permute-done.29
  280.5 1.9 collective-permute-done.33
  282.4 5.5 %collective-permute-done.32 = bf16[128,1024]{1,0:T(8,128)(2,1)S(1)} collective-permute-done((bf16[128,1024]{1,0:T(8,128)(2,1)S(1)}, bf16[128,1024]{1,0:T(8,128)(2,1)S(1)}, u32[]{:S(2)}, u32[]{:S(2)}) %collective-permute-start.32) | collective-permute-done | bytes 262176 | tf_op jit(solution)/shard_map/ppermute | solution.py:31
  287.9 2.0 copy-done.15
  (146 shorter events, 48.4 us)
Async XLA Ops:
  0.6 21.6 %copy-start.13 = (f32[1,256,2048]{2,1,0:T(8,128)S(1)}, f32[1,256,2048]{2,1,0:T(8,128)}, u32[]{:S(2)}) copy-start(f32[1,256,2048]{2,1,0:T(8,128)} %param.10) | copy-start | bytes 6291460
  0.6 59.3 %collective-permute-start = (bf16[256,2048]{1,0:T(8,128)(2,1)}, bf16[256,2048]{1,0:T(8,128)(2,1)}, u32[]{:S(2)}, u32[]{:S(2)}) collective-permute-start(bf16[256,2048]{1,0:T(8,128)(2,1)} %bitcast.125), channel_id=1, source_target_pairs={{0,1},{1,2},{2,3},{3,0},{4,5},{5,6},{6,7},{7,4},{8,9},{9,10},{10,1... | collective-permute-start | bytes 3145736 | tf_op jit(solution)/shard_map/ppermute | solution.py:31
  2.6 57.3 %collective-permute-start.1 = (bf16[256,2048]{1,0:T(8,128)(2,1)}, bf16[256,2048]{1,0:T(8,128)(2,1)}, u32[]{:S(2)}, u32[]{:S(2)}) collective-permute-start(bf16[256,2048]{1,0:T(8,128)(2,1)} %bitcast.126), channel_id=1, source_target_pairs={{0,3},{1,0},{2,1},{3,2},{4,7},{5,4},{6,5},{7,6},{8,11},{9,8},{10,9... | collective-permute-start | bytes 3145736 | tf_op jit(solution)/shard_map/ppermute | solution.py:31
  4.8 55.1 %collective-permute-start.2 = (bf16[256,2048]{1,0:T(8,128)(2,1)}, bf16[256,2048]{1,0:T(8,128)(2,1)}, u32[]{:S(2)}, u32[]{:S(2)}) collective-permute-start(bf16[256,2048]{1,0:T(8,128)(2,1)} %bitcast.127), channel_id=1, source_target_pairs={{0,4},{4,0},{1,5},{5,1},{2,6},{6,2},{3,7},{7,3},{8,12},{12,8},{9,1... | collective-permute-start | bytes 3145736 | tf_op jit(solution)/shard_map/ppermute | solution.py:35
  6.2 39.7 %all-to-all-start.1 = ((bf16[16,16,1024]{2,1,0:T(8,128)(2,1)}), bf16[16,16,1024]{2,1,0:T(8,128)(2,1)S(1)}, u32[]{:S(2)}, u32[]{:S(2)}) async-start(bf16[16,16,1024]{2,1,0:T(8,128)(2,1)} %bitcast.133), calls=%async_computation.1 | async-start | bytes 1048576 | tf_op jit(solution)/shard_map/all_to_all | solution.py:208
  14.5 25.8 %collective-permute-start.16 = (bf16[128,2048]{1,0:T(8,128)(2,1)}, bf16[128,2048]{1,0:T(8,128)(2,1)S(1)}, u32[]{:S(2)}, u32[]{:S(2)}) collective-permute-start(bf16[128,2048]{1,0:T(8,128)(2,1)} %get-tuple-element.30), channel_id=1, source_target_pairs={{8,0},{16,8},{24,16},{32,24},{40,32},{48,40},{56,48},{64,56},{72,6... | collective-permute-start | bytes 1572872 | tf_op jit(solution)/shard_map/ppermute | solution.py:27
  18.8 24.0 %collective-permute-start.17 = (bf16[128,2048]{1,0:T(8,128)(2,1)}, bf16[128,2048]{1,0:T(8,128)(2,1)}, u32[]{:S(2)}, u32[]{:S(2)}) collective-permute-start(bf16[128,2048]{1,0:T(8,128)(2,1)} %get-tuple-element.29), channel_id=1, source_target_pairs={{0,8},{8,16},{16,24},{24,32},{32,40},{40,48},{48,56},{56,64},{64,7... | collective-permute-start | bytes 1572872 | tf_op jit(solution)/shard_map/ppermute | solution.py:27
  45.9 14.0 %all-to-all-start.2 = ((f32[128,1,128]{2,1,0:T(1,128)}), f32[128,1,128]{2,1,0:T(1,128)S(1)}, u32[]{:S(2)}, u32[]{:S(2)}) async-start(f32[128,1,128]{2,1,0:T(1,128)} %bitcast.29), calls=%async_computation.2 | async-start | bytes 131072 | tf_op jit(solution)/shard_map/all_to_all | solution.py:246
  53.2 61.2 %collective-permute-start.14 = (bf16[256,2048]{1,0:T(8,128)(2,1)}, bf16[256,2048]{1,0:T(8,128)(2,1)}, u32[]{:S(2)}, u32[]{:S(2)}) collective-permute-start(bf16[256,2048]{1,0:T(8,128)(2,1)} %convert_bitcast_fusion), channel_id=1, source_target_pairs={{0,8},{8,16},{16,24},{24,32},{32,40},{40,48},{48,56},{56,64},{64,7... | collective-permute-start | bytes 3145736 | tf_op jit(solution)/shard_map/ppermute | solution.py:27
  60.1 27.0 %collective-permute-start.3 = (bf16[256,2048]{1,0:T(8,128)(2,1)}, bf16[256,2048]{1,0:T(8,128)(2,1)}, u32[]{:S(2)}, u32[]{:S(2)}) collective-permute-start(bf16[256,2048]{1,0:T(8,128)(2,1)} %collective-permute-done.2.refs_4_), channel_id=1, source_target_pairs={{0,1},{1,2},{2,3},{3,0},{4,5},{5,6},{6,7},{7,4},{8,9},{9,10},{10,1... | collective-permute-start | bytes 3145736 | tf_op jit(solution)/shard_map/ppermute | solution.py:31
  60.9 45.0 %collective-permute-start.4 = (bf16[256,2048]{1,0:T(8,128)(2,1)}, bf16[256,2048]{1,0:T(8,128)(2,1)}, u32[]{:S(2)}, u32[]{:S(2)}) collective-permute-start(bf16[256,2048]{1,0:T(8,128)(2,1)} %collective-permute-done.1.refs_3_), channel_id=1, source_target_pairs={{0,4},{4,0},{1,5},{5,1},{2,6},{6,2},{3,7},{7,3},{8,12},{12,8},{9,1... | collective-permute-start | bytes 3145736 | tf_op jit(solution)/shard_map/ppermute | solution.py:35
  63.4 42.6 %collective-permute-start.5 = (bf16[256,2048]{1,0:T(8,128)(2,1)}, bf16[256,2048]{1,0:T(8,128)(2,1)}, u32[]{:S(2)}, u32[]{:S(2)}) collective-permute-start(bf16[256,2048]{1,0:T(8,128)(2,1)} %collective-permute-done.1.refs_3_), channel_id=1, source_target_pairs={{0,3},{1,0},{2,1},{3,2},{4,7},{5,4},{6,5},{7,6},{8,11},{9,8},{10,9... | collective-permute-start | bytes 3145736 | tf_op jit(solution)/shard_map/ppermute | solution.py:31
  68.1 30.2 %all-to-all-start.3 = ((bf16[16,16,1024]{2,1,0:T(8,128)(2,1)}), bf16[16,16,1024]{2,1,0:T(8,128)(2,1)S(1)}, u32[]{:S(2)}, u32[]{:S(2)}) async-start(bf16[16,16,1024]{2,1,0:T(8,128)(2,1)} %first_solution.1.initial), calls=%async_computation.3 | async-start | bytes 1048576 | tf_op jit(solution)/shard_map/all_to_all | solution.py:208
  88.1 29.0 %collective-permute-start.6 = (bf16[128,2048]{1,0:T(8,128)(2,1)S(1)}, bf16[128,2048]{1,0:T(8,128)(2,1)S(1)}, u32[]{:S(2)}, u32[]{:S(2)}) collective-permute-start(bf16[128,2048]{1,0:T(8,128)(2,1)S(1)} %slice.96), channel_id=1, source_target_pairs={{0,1},{1,2},{2,3},{3,0},{4,5},{5,6},{6,7},{7,4},{8,9},{9,10},{10,1... | collective-permute-start | bytes 1572872 | tf_op jit(solution)/shard_map/ppermute | solution.py:31
  98.3 63.0 %all-to-all-start = ((bf16[1,256,8,256]{3,1,0,2:T(8,128)(2,1)}), bf16[1,256,8,256]{3,1,0,2:T(8,128)(2,1)}, u32[]{:S(2)}, u32[]{:S(2)}) async-start(bf16[1,256,8,256]{3,1,0,2:T(8,128)(2,1)} %copy.23), calls=%async_computation | async-start | bytes 2097152 | tf_op jit(solution)/shard_map/all_to_all | solution.py:274
  106.0 55.3 %copy-start.19 = (s32[8]{0:T(128)S(1)}, s32[8]{0:T(128)}, u32[]{:S(2)}) copy-start(s32[8]{0:T(128)} %constant.81.clone) | copy-start | bytes 100
  106.0 24.0 %collective-permute-start.20 = (bf16[256,1024]{1,0:T(8,128)(2,1)S(1)}, bf16[256,1024]{1,0:T(8,128)(2,1)S(1)}, u32[]{:S(2)}, u32[]{:S(2)}) collective-permute-start(bf16[256,1024]{1,0:T(8,128)(2,1)S(1)} %bitcast.120), channel_id=1, source_target_pairs={{0,4},{4,0},{1,5},{5,1},{2,6},{6,2},{3,7},{7,3},{8,12},{12,8},{9,1... | collective-permute-start | bytes 1572872 | tf_op jit(solution)/shard_map/ppermute | solution.py:35
  107.0 25.3 %collective-permute-start.19 = (bf16[256,1024]{1,0:T(8,128)(2,1)S(1)}, bf16[256,1024]{1,0:T(8,128)(2,1)}, u32[]{:S(2)}, u32[]{:S(2)}) collective-permute-start(bf16[256,1024]{1,0:T(8,128)(2,1)S(1)} %bitcast.121), channel_id=1, source_target_pairs={{0,3},{1,0},{2,1},{3,2},{4,7},{5,4},{6,5},{7,6},{8,11},{9,8},{10,9... | collective-permute-start | bytes 1572872 | tf_op jit(solution)/shard_map/ppermute | solution.py:31
  110.4 26.1 %collective-permute-start.8 = (bf16[4,256,256]{2,1,0:T(8,128)(2,1)S(1)}, bf16[4,256,256]{2,1,0:T(8,128)(2,1)S(1)}, u32[]{:S(2)}, u32[]{:S(2)}) collective-permute-start(bf16[4,256,256]{2,1,0:T(8,128)(2,1)S(1)} %pad_maximum_fusion.refs_9_), channel_id=1, source_target_pairs={{0,8},{8,16},{16,24},{24,32},{32,40},{40,48},{48,56},{56,64},{64,7... | collective-permute-start | bytes 1572872 | tf_op jit(solution)/shard_map/ppermute | solution.py:27
  114.4 28.5 %collective-permute-start.7 = (bf16[128,2048]{1,0:T(8,128)(2,1)S(1)}, bf16[128,2048]{1,0:T(8,128)(2,1)S(1)}, u32[]{:S(2)}, u32[]{:S(2)}) collective-permute-start(bf16[128,2048]{1,0:T(8,128)(2,1)S(1)} %slice.97), channel_id=1, source_target_pairs={{0,3},{1,0},{2,1},{3,2},{4,7},{5,4},{6,5},{7,6},{8,11},{9,8},{10,9... | collective-permute-start | bytes 1572872 | tf_op jit(solution)/shard_map/ppermute | solution.py:31
  117.2 27.7 %collective-permute-start.11 = (bf16[4,256,256]{2,1,0:T(8,128)(2,1)S(1)}, bf16[4,256,256]{2,1,0:T(8,128)(2,1)S(1)}, u32[]{:S(2)}, u32[]{:S(2)}) collective-permute-start(bf16[4,256,256]{2,1,0:T(8,128)(2,1)S(1)} %pad_maximum_fusion.refs_9_), channel_id=1, source_target_pairs={{8,0},{16,8},{24,16},{32,24},{40,32},{48,40},{56,48},{64,56},{72,6... | collective-permute-start | bytes 1572872 | tf_op jit(solution)/shard_map/ppermute | solution.py:27
  130.0 24.7 %copy-start.2 = (bf16[256,1024]{1,0:T(8,128)(2,1)}, bf16[256,1024]{1,0:T(8,128)(2,1)S(1)}, u32[]{:S(2)}) copy-start(bf16[256,1024]{1,0:T(8,128)(2,1)S(1)} %collective-permute-done.20.refs_3_) | copy-start | bytes 1572868
  130.0 16.4 %collective-permute-start.21 = (bf16[256,1024]{1,0:T(8,128)(2,1)S(1)}, bf16[256,1024]{1,0:T(8,128)(2,1)S(1)}, u32[]{:S(2)}, u32[]{:S(2)}) collective-permute-start(bf16[256,1024]{1,0:T(8,128)(2,1)S(1)} %collective-permute-done.20.refs_3_), channel_id=1, source_target_pairs={{0,1},{1,2},{2,3},{3,0},{4,5},{5,6},{6,7},{7,4},{8,9},{9,10},{10,1... | collective-permute-start | bytes 1572872 | tf_op jit(solution)/shard_map/ppermute | solution.py:31
  132.3 15.9 %collective-permute-start.22 = (bf16[256,1024]{1,0:T(8,128)(2,1)}, bf16[256,1024]{1,0:T(8,128)(2,1)S(1)}, u32[]{:S(2)}, u32[]{:S(2)}) collective-permute-start(bf16[256,1024]{1,0:T(8,128)(2,1)} %collective-permute-done.19.refs_2_), channel_id=1, source_target_pairs={{0,4},{4,0},{1,5},{5,1},{2,6},{6,2},{3,7},{7,3},{8,12},{12,8},{9,1... | collective-permute-start | bytes 1572872 | tf_op jit(solution)/shard_map/ppermute | solution.py:35
  136.5 18.2 %copy-start.4 = (bf16[4,256,256]{2,1,0:T(8,128)(2,1)}, bf16[4,256,256]{2,1,0:T(8,128)(2,1)S(1)}, u32[]{:S(2)}) copy-start(bf16[4,256,256]{2,1,0:T(8,128)(2,1)S(1)} %collective-permute-done.8.refs_12_) | copy-start | bytes 1572868
  136.5 15.1 %collective-permute-start.9 = (bf16[3,256,256]{2,1,0:T(8,128)(2,1)S(1)}, bf16[3,256,256]{2,1,0:T(8,128)(2,1)S(1)}, u32[]{:S(2)}, u32[]{:S(2)}) collective-permute-start(bf16[3,256,256]{2,1,0:T(8,128)(2,1)S(1)} %pad_maximum_fusion.2.refs_10_), channel_id=1, source_target_pairs={{0,8},{8,16},{16,24},{24,32},{32,40},{40,48},{48,56},{56,64},{64,7... | collective-permute-start | bytes 1179656 | tf_op jit(solution)/shard_map/ppermute | solution.py:27
  142.9 11.8 %collective-permute-start.12 = (bf16[3,256,256]{2,1,0:T(8,128)(2,1)S(1)}, bf16[3,256,256]{2,1,0:T(8,128)(2,1)S(1)}, u32[]{:S(2)}, u32[]{:S(2)}) collective-permute-start(bf16[3,256,256]{2,1,0:T(8,128)(2,1)S(1)} %pad_maximum_fusion.2.refs_10_), channel_id=1, source_target_pairs={{8,0},{16,8},{24,16},{32,24},{40,32},{48,40},{56,48},{64,56},{72,6... | collective-permute-start | bytes 1179656 | tf_op jit(solution)/shard_map/ppermute | solution.py:27
  144.8 9.9 %copy-start.17 = (bf16[256,2048]{1,0:T(8,128)(2,1)}, bf16[256,2048]{1,0:T(8,128)(2,1)S(1)}, u32[]{:S(2)}) copy-start(bf16[256,2048]{1,0:T(8,128)(2,1)S(1)} %constant_dynamic-update-slice_fusion.refs_8_) | copy-start | bytes 3145732
  144.9 9.8 %copy-start.6 = (bf16[4,256,256]{2,1,0:T(8,128)(2,1)}, bf16[4,256,256]{2,1,0:T(8,128)(2,1)S(1)}, u32[]{:S(2)}) copy-start(bf16[4,256,256]{2,1,0:T(8,128)(2,1)S(1)} %collective-permute-done.11.refs_15_) | copy-start | bytes 1572868
  144.9 36.2 %collective-permute-start.18 = (bf16[256,1024]{1,0:T(8,128)(2,1)S(1)}, bf16[256,1024]{1,0:T(8,128)(2,1)}, u32[]{:S(2)}, u32[]{:S(2)}) collective-permute-start(bf16[256,1024]{1,0:T(8,128)(2,1)S(1)} %bitcast.122), channel_id=1, source_target_pairs={{0,1},{1,2},{2,3},{3,0},{4,5},{5,6},{6,7},{7,4},{8,9},{9,10},{10,1... | collective-permute-start | bytes 1572872 | tf_op jit(solution)/shard_map/ppermute | solution.py:31
  146.4 34.7 %collective-permute-start.23 = (bf16[256,1024]{1,0:T(8,128)(2,1)}, bf16[256,1024]{1,0:T(8,128)(2,1)}, u32[]{:S(2)}, u32[]{:S(2)}) collective-permute-start(bf16[256,1024]{1,0:T(8,128)(2,1)} %collective-permute-done.19.refs_2_), channel_id=1, source_target_pairs={{0,3},{1,0},{2,1},{3,2},{4,7},{5,4},{6,5},{7,6},{8,11},{9,8},{10,9... | collective-permute-start | bytes 1572872 | tf_op jit(solution)/shard_map/ppermute | solution.py:31
  148.2 8.5 %collective-permute-start.10 = (bf16[1,256,256]{2,1,0:T(8,128)(2,1)S(1)}, bf16[1,256,256]{2,1,0:T(8,128)(2,1)}, u32[]{:S(2)}, u32[]{:S(2)}) collective-permute-start(bf16[1,256,256]{2,1,0:T(8,128)(2,1)S(1)} %dynamic-slice_bitcast_fusion.refs_11_), channel_id=1, source_target_pairs={{0,8},{8,16},{16,24},{24,32},{32,40},{40,48},{48,56},{56,64},{64,7... | collective-permute-start | bytes 393224 | tf_op jit(solution)/shard_map/ppermute | solution.py:27
  152.4 27.2 %collective-permute-start.25 = (bf16[128,1024]{1,0:T(8,128)(2,1)}, bf16[128,1024]{1,0:T(8,128)(2,1)}, u32[]{:S(2)}, u32[]{:S(2)}) collective-permute-start(bf16[128,1024]{1,0:T(8,128)(2,1)} %slice.105), channel_id=1, source_target_pairs={{0,3},{1,0},{2,1},{3,2},{4,7},{5,4},{6,5},{7,6},{8,11},{9,8},{10,9... | collective-permute-start | bytes 786440 | tf_op jit(solution)/shard_map/ppermute | solution.py:31
  155.5 24.1 %collective-permute-start.24 = (bf16[128,1024]{1,0:T(8,128)(2,1)}, bf16[128,1024]{1,0:T(8,128)(2,1)}, u32[]{:S(2)}, u32[]{:S(2)}) collective-permute-start(bf16[128,1024]{1,0:T(8,128)(2,1)} %slice.104), channel_id=1, source_target_pairs={{0,1},{1,2},{2,3},{3,0},{4,5},{5,6},{6,7},{7,4},{8,9},{9,10},{10,1... | collective-permute-start | bytes 786440 | tf_op jit(solution)/shard_map/ppermute | solution.py:31
  156.7 6.8 %collective-permute-start.13 = (bf16[1,256,256]{2,1,0:T(8,128)(2,1)S(1)}, bf16[1,256,256]{2,1,0:T(8,128)(2,1)}, u32[]{:S(2)}, u32[]{:S(2)}) collective-permute-start(bf16[1,256,256]{2,1,0:T(8,128)(2,1)S(1)} %dynamic-slice_bitcast_fusion.refs_11_), channel_id=1, source_target_pairs={{8,0},{16,8},{24,16},{32,24},{40,32},{48,40},{56,48},{64,56},{72,6... | collective-permute-start | bytes 393224 | tf_op jit(solution)/shard_map/ppermute | solution.py:27
  167.6 13.5 %copy-start.3 = (bf16[256,1024]{1,0:T(8,128)(2,1)S(1)}, bf16[256,1024]{1,0:T(8,128)(2,1)}, u32[]{:S(2)}) copy-start(bf16[256,1024]{1,0:T(8,128)(2,1)} %copy-done.2) | copy-start | bytes 1572868
  188.3 53.8 %copy-start.20 = (s32[1,2]{1,0:T(1,128)S(1)}, s32[1,2]{1,0:T(1,128)}, u32[]{:S(2)}) copy-start(s32[1,2]{1,0:T(1,128)} %param.13) | copy-start | bytes 28
  188.3 27.1 %all-to-all-start.4 = ((bf16[16,48,1024]{2,1,0:T(8,128)(2,1)}), bf16[16,48,1024]{2,1,0:T(8,128)(2,1)S(1)}, u32[]{:S(2)}, u32[]{:S(2)}) async-start(bf16[16,48,1024]{2,1,0:T(8,128)(2,1)} %apply_blocks.1), calls=%async_computation.4 | async-start | bytes 3145728 | tf_op jit(solution)/shard_map/all_to_all | solution.py:208
  194.3 57.3 %collective-permute-start.15 = (bf16[256,2048]{1,0:T(8,128)(2,1)}, bf16[256,2048]{1,0:T(8,128)(2,1)}, u32[]{:S(2)}, u32[]{:S(2)}) collective-permute-start(bf16[256,2048]{1,0:T(8,128)(2,1)} %copy-done.12), channel_id=1, source_target_pairs={{8,0},{16,8},{24,16},{32,24},{40,32},{48,40},{56,48},{64,56},{72,6... | collective-permute-start | bytes 3145736 | tf_op jit(solution)/shard_map/ppermute | solution.py:27
  218.9 23.3 %all-to-all-start.5 = ((bf16[16,16,1024]{2,1,0:T(8,128)(2,1)}), bf16[16,16,1024]{2,1,0:T(8,128)(2,1)S(1)}, u32[]{:S(2)}, u32[]{:S(2)}) async-start(bf16[16,16,1024]{2,1,0:T(8,128)(2,1)} %change.1), calls=%async_computation.5 | async-start | bytes 1048576 | tf_op jit(solution)/shard_map/all_to_all | solution.py:208
  245.4 21.3 %collective-permute-start.26 = (bf16[256,1024]{1,0:T(8,128)(2,1)S(1)}, bf16[256,1024]{1,0:T(8,128)(2,1)S(1)}, u32[]{:S(2)}, u32[]{:S(2)}) collective-permute-start(bf16[256,1024]{1,0:T(8,128)(2,1)S(1)} %get-tuple-element.24), channel_id=1, source_target_pairs={{0,1},{1,2},{2,3},{3,0},{4,5},{5,6},{6,7},{7,4},{8,9},{9,10},{10,1... | collective-permute-start | bytes 1572872 | tf_op jit(solution)/shard_map/ppermute | solution.py:31
  245.7 14.2 %collective-permute-start.27 = (bf16[256,1024]{1,0:T(8,128)(2,1)S(1)}, bf16[256,1024]{1,0:T(8,128)(2,1)S(1)}, u32[]{:S(2)}, u32[]{:S(2)}) collective-permute-start(bf16[256,1024]{1,0:T(8,128)(2,1)S(1)} %get-tuple-element.24), channel_id=1, source_target_pairs={{0,3},{1,0},{2,1},{3,2},{4,7},{5,4},{6,5},{7,6},{8,11},{9,8},{10,9... | collective-permute-start | bytes 1572872 | tf_op jit(solution)/shard_map/ppermute | solution.py:31
  248.7 18.0 %collective-permute-start.28 = (bf16[256,1024]{1,0:T(8,128)(2,1)S(1)}, bf16[256,1024]{1,0:T(8,128)(2,1)S(1)}, u32[]{:S(2)}, u32[]{:S(2)}) collective-permute-start(bf16[256,1024]{1,0:T(8,128)(2,1)S(1)} %get-tuple-element.24), channel_id=1, source_target_pairs={{0,4},{4,0},{1,5},{5,1},{2,6},{6,2},{3,7},{7,3},{8,12},{12,8},{9,1... | collective-permute-start | bytes 1572872 | tf_op jit(solution)/shard_map/ppermute | solution.py:35
  260.0 14.9 %collective-permute-start.30 = (bf16[256,1024]{1,0:T(8,128)(2,1)S(1)}, bf16[256,1024]{1,0:T(8,128)(2,1)S(1)}, u32[]{:S(2)}, u32[]{:S(2)}) collective-permute-start(bf16[256,1024]{1,0:T(8,128)(2,1)S(1)} %collective-permute-done.27), channel_id=1, source_target_pairs={{0,4},{4,0},{1,5},{5,1},{2,6},{6,2},{3,7},{7,3},{8,12},{12,8},{9,1... | collective-permute-start | bytes 1572872 | tf_op jit(solution)/shard_map/ppermute | solution.py:35
  262.9 17.5 %collective-permute-start.31 = (bf16[256,1024]{1,0:T(8,128)(2,1)S(1)}, bf16[256,1024]{1,0:T(8,128)(2,1)S(1)}, u32[]{:S(2)}, u32[]{:S(2)}) collective-permute-start(bf16[256,1024]{1,0:T(8,128)(2,1)S(1)} %collective-permute-done.27), channel_id=1, source_target_pairs={{0,3},{1,0},{2,1},{3,2},{4,7},{5,4},{6,5},{7,6},{8,11},{9,8},{10,9... | collective-permute-start | bytes 1572872 | tf_op jit(solution)/shard_map/ppermute | solution.py:31
  266.6 13.6 %collective-permute-start.29 = (bf16[256,1024]{1,0:T(8,128)(2,1)S(1)}, bf16[256,1024]{1,0:T(8,128)(2,1)S(1)}, u32[]{:S(2)}, u32[]{:S(2)}) collective-permute-start(bf16[256,1024]{1,0:T(8,128)(2,1)S(1)} %collective-permute-done.28), channel_id=1, source_target_pairs={{0,1},{1,2},{2,3},{3,0},{4,5},{5,6},{6,7},{7,4},{8,9},{9,10},{10,1... | collective-permute-start | bytes 1572872 | tf_op jit(solution)/shard_map/ppermute | solution.py:31
  274.9 7.5 %collective-permute-start.33 = (bf16[128,1024]{1,0:T(8,128)(2,1)S(1)}, bf16[128,1024]{1,0:T(8,128)(2,1)S(1)}, u32[]{:S(2)}, u32[]{:S(2)}) collective-permute-start(bf16[128,1024]{1,0:T(8,128)(2,1)S(1)} %slice.107), channel_id=1, source_target_pairs={{0,3},{1,0},{2,1},{3,2},{4,7},{5,4},{6,5},{7,6},{8,11},{9,8},{10,9... | collective-permute-start | bytes 786440 | tf_op jit(solution)/shard_map/ppermute | solution.py:31
  280.2 7.7 %collective-permute-start.32 = (bf16[128,1024]{1,0:T(8,128)(2,1)S(1)}, bf16[128,1024]{1,0:T(8,128)(2,1)S(1)}, u32[]{:S(2)}, u32[]{:S(2)}) collective-permute-start(bf16[128,1024]{1,0:T(8,128)(2,1)S(1)} %slice.106), channel_id=1, source_target_pairs={{0,1},{1,2},{2,3},{3,0},{4,5},{5,6},{6,7},{7,4},{8,9},{9,10},{10,1... | collective-permute-start | bytes 786440 | tf_op jit(solution)/shard_map/ppermute | solution.py:31
  (13 other events, 32.7 us)

commit v3 on v2

v3 whole, which is shorter than its diff:
```python
import jax
import jax.numpy as jnp
from jax import lax
from jax.experimental import pallas as pl
from jax.experimental.pallas import tpu as pltpu
from jax.sharding import Mesh
from jax.sharding import PartitionSpec as P

SCALE_BLOCK = 128
LAYER = ("layer_0", "layer_1", "layer_2")
DP = ("dp_0", "dp_1")
LAYERS = 16
GROUP = 8
TURN = 4

FACTOR_DECAY = 0.9
DAMPING = 0.5
MOMENTUM = 0.8
STEP_SIZE = 0.05

F32 = jnp.float32
BF16 = jnp.bfloat16


def along_layers(value, steps):
    pairs = [(i, i + steps) for i in range(LAYERS) if 0 <= i + steps < LAYERS]
    return lax.ppermute(value, LAYER, pairs)


def turned(value, steps):
    return lax.ppermute(value, "dp_1", [(i, (i + steps) % TURN) for i in range(TURN)])


def across(value):
    return lax.ppermute(value, "dp_0", [(0, 1), (1, 0)])


def first_round(own):
    return across(own), turned(own, 1), turned(own, 3), turned(own, 2)


def second_round(other, far):
    return turned(other, 1), turned(other, 3), across(far)


def gathered(own):
    other, before, beyond, far = tied(*first_round(own))
    return own, before, beyond, other, far, *second_round(other, far)


def piece_order():
    mine, turn = lax.axis_index("dp_0"), lax.axis_index("dp_1")
    side = jnp.stack([mine] * 3 + [1 - mine, mine] + [1 - mine] * 3)
    steps = jnp.array([0, 3, 1, 0, 2, 3, 1, 2], jnp.int32)
    return (side * TURN + (turn + steps) % TURN).astype(jnp.int32)


def tied(*values):
    return lax.optimization_barrier(values)


def transposed_dot(left, right):
    return lax.dot_general(left, right, (((0,), (0,)), ((), ())), preferred_element_type=F32)


def pick_kernel(order, *refs):
    for k, piece in enumerate(refs[:-1]):
        refs[-1][k] = piece[...]


def own_columns(order, pieces):
    rows = pieces[0].shape[0]
    return pl.pallas_call(
        pick_kernel,
        grid_spec=pltpu.PrefetchScalarGridSpec(
            num_scalar_prefetch=1,
            grid=(1,),
            in_specs=[pl.BlockSpec((rows, rows), lambda j, o: (0, o[0]))] * len(pieces),
            out_specs=pl.BlockSpec((len(pieces), rows, rows), lambda j, o: (0, 0, 0)),
        ),
        out_shape=jax.ShapeDtypeStruct((len(pieces), rows, rows), pieces[0].dtype),
        name="own_columns",
    )(order, *pieces)


def refresh_kernel(weight, order, *refs):
    pieces, columns, (factor_old, row_old) = refs[:GROUP], refs[GROUP : GROUP + 3], refs[GROUP + 3 : GROUP + 5]
    factor, factor_off, row_batch, row_off, col_off = refs[GROUP + 5 :]
    sums = [None, None, None]
    for k in range(GROUP):
        right = pieces[k][...]
        for n in range(3):
            part = transposed_dot(columns[n][k], right)
            sums[n] = part if k == 0 else sums[n] + part
    rows, tile = factor.shape
    column = pl.program_id(0) * tile + lax.broadcasted_iota(jnp.int32, (rows, tile), 1)
    diagonal = column == order[0] * rows + lax.broadcasted_iota(jnp.int32, (rows, tile), 0)
    fresh = FACTOR_DECAY * factor_old[...] + weight * sums[0]
    factor[...] = fresh
    factor_off[...] = jnp.where(diagonal, 0.0, fresh).astype(BF16)
    row_batch[...] = sums[1].astype(BF16)
    row = FACTOR_DECAY * row_old[...].astype(F32) + weight * sums[1]
    row_off[...] = jnp.where(diagonal, 0.0, row).astype(BF16)
    col_off[...] = jnp.where(diagonal, 0.0, weight * sums[2]).astype(BF16)


def refresh(weight, order, pieces, columns, factor_old, row_old):
    rows, features = factor_old.shape
    tile = 512
    column = pl.BlockSpec((rows, tile), lambda j, o: (0, j))
    kinds = (F32, BF16, BF16, BF16, BF16)
    return pl.pallas_call(
        lambda *refs: refresh_kernel(weight, *refs),
        grid_spec=pltpu.PrefetchScalarGridSpec(
            num_scalar_prefetch=1,
            grid=(features // tile,),
            in_specs=[column] * GROUP
            + [pl.BlockSpec(c.shape, lambda j, o: (0, 0, 0)) for c in columns]
            + [column, column],
            out_specs=[column] * len(kinds),
        ),
        out_shape=[jax.ShapeDtypeStruct((rows, features), kind) for kind in kinds],
        compiler_params=pltpu.CompilerParams(vmem_limit_bytes=48 * 2**20),
        name="refresh",
    )(order, *pieces, *columns, factor_old, row_old)


def place_kernel(order, *refs):
    count = order.shape[0]
    for k in range(count):
        @pl.when(pl.program_id(0) == k)
        def _():
            refs[-1][...] = refs[k][...]


def place_rows(order, pieces, base):
    rows, outputs = pieces[0].shape
    arrays = list(pieces) + ([] if base is None else [base])
    return pl.pallas_call(
        place_kernel,
        grid_spec=pltpu.PrefetchScalarGridSpec(
            num_scalar_prefetch=1,
            grid=(len(pieces),),
            in_specs=[pl.BlockSpec((rows, outputs), lambda j, o: (0, 0))] * len(pieces)
            + [pl.BlockSpec(memory_space=pl.ANY)] * (len(arrays) - len(pieces)),
            out_specs=pl.BlockSpec((rows, outputs), lambda j, o: (o[j], 0)),
        ),
        out_shape=jax.ShapeDtypeStruct((GROUP * rows, outputs), pieces[0].dtype),
        input_output_aliases={} if base is None else {len(arrays): 0},
        name="place_rows",
    )(order, *arrays)


def apply_kernel(order, *refs):
    pieces, matrices, (col_old, out, joined) = refs[:GROUP], refs[GROUP : GROUP + 3], refs[GROUP + 3 :]
    rows = pieces[0].shape[0]
    for k in range(GROUP):
        joined[pl.ds(pl.multiple_of(order[k] * rows, rows), rows), :] = pieces[k][...]
    full = joined[...]
    slim = rows // LAYERS
    diagonal = lax.broadcasted_iota(jnp.int32, (rows, rows), 0) == lax.broadcasted_iota(jnp.int32, (rows, rows), 1)
    old = None
    for k in range(GROUP):
        block = col_old[order[k]]
        block = jnp.where(diagonal, jnp.zeros_like(block), block) if k == 0 else block
        part = transposed_dot(block, pieces[k][...])
        old = part if k == 0 else old + part
    for n, matrix in enumerate(matrices):
        product = jnp.dot(matrix[...], full, preferred_element_type=F32)
        product = (product + FACTOR_DECAY * old if n == 1 else product).astype(BF16)
        for layer in range(LAYERS):
            out[layer, n * slim : (n + 1) * slim, :] = product[layer * slim : (layer + 1) * slim]


def apply_blocks(order, pieces, matrices, col_old):
    rows, outputs = pieces[0].shape
    features = matrices[0].shape[1]
    tile = 512
    slim = rows // LAYERS
    return pl.pallas_call(
        apply_kernel,
        grid_spec=pltpu.PrefetchScalarGridSpec(
            num_scalar_prefetch=1,
            grid=(outputs // tile,),
            in_specs=[pl.BlockSpec((rows, tile), lambda j, o: (0, j))] * GROUP
            + [pl.BlockSpec((rows, features), lambda j, o: (0, 0))] * 3
            + [pl.BlockSpec((GROUP, rows, rows), lambda j, o: (0, 0, 0))],
            out_specs=pl.BlockSpec((LAYERS, 3 * slim, tile), lambda j, o: (0, 0, j)),
            scratch_shapes=[pltpu.VMEM((features, tile), BF16)],
        ),
        out_shape=jax.ShapeDtypeStruct((LAYERS, 3 * slim, outputs), BF16),
        compiler_params=pltpu.CompilerParams(vmem_limit_bytes=48 * 2**20),
        name="apply_blocks",
    )(order, *pieces, *matrices, col_old)


def sweep(target, inverse, coupling, ratio, store):
    passed = jnp.zeros_like(target[0])
    scaled = []
    for layer in range(LAYERS):
        scaled.append((target[layer] - passed) * inverse[layer])
        passed = coupling[layer] * scaled[layer]
    nearer = jnp.zeros_like(passed)
    for layer in reversed(range(LAYERS)):
        nearer = scaled[layer] - ratio[layer] * nearer
        store(layer, nearer)


def initial_kernel(grad, pivots, inverse, coupling, ratio, solved):
    for start in range(0, grad.shape[-1], 128):
        lanes = pl.ds(start, 128)

        def store(layer, value):
            solved[layer, :, lanes] = value.astype(solved.dtype)

        sweep([grad[layer, :, lanes].astype(F32) for layer in range(LAYERS)], inverse, coupling, ratio, store)


def change_kernel(grad, initial, off, pivots, inverse, coupling, ratio, solved):
    slim = grad.shape[1]
    for start in range(0, grad.shape[-1], 128):
        lanes = pl.ds(start, 128)
        first = [initial[layer, :, lanes].astype(F32) for layer in range(LAYERS)]
        target = []
        for layer in range(LAYERS):
            applied = pivots[layer] * first[layer] + off[layer, :slim, lanes].astype(F32)
            if layer + 1 < LAYERS:
                applied = applied + coupling[layer] * first[layer + 1]
                applied = applied + off[layer + 1, 2 * slim : 3 * slim, lanes].astype(F32)
            if layer > 0:
                applied = applied + coupling[layer - 1] * first[layer - 1]
                applied = applied + off[layer - 1, slim : 2 * slim, lanes].astype(F32)
            target.append(grad[layer, :, lanes].astype(F32) - applied)

        def store(layer, value):
            solved[layer, :, lanes] = value.astype(solved.dtype)

        sweep(target, inverse, coupling, ratio, store)


def chain_solve(kernel, name, arrays, coefficients):
    return pl.pallas_call(
        kernel,
        out_shape=jax.ShapeDtypeStruct(arrays[0].shape, BF16),
        compiler_params=pltpu.CompilerParams(vmem_limit_bytes=32 * 2**20),
        name=name,
    )(*arrays, *coefficients)


def by_layer(value):
    return lax.all_to_all(value, LAYER, 0, 0)


def block_diagonal(block):
    return jnp.sum(jnp.where(jnp.eye(block.shape[0], dtype=bool), block, 0.0), axis=0)


def body(activations, factor_old, cross_old, gradients, moments, exponents, master):
    acts, factor_old, cross_old, grad = activations[0], factor_old[0], cross_old[0], gradients[0]
    rows, features = factor_old.shape
    outputs = grad.shape[1]
    slim = rows // LAYERS
    place = lax.axis_index(DP)
    start = place * rows
    weight = (1.0 - FACTOR_DECAY) / (rows * GROUP)
    order = piece_order()

    above = along_layers(acts, -1)
    before, beyond = turned(acts, 1), turned(acts, 3)
    grad_rows = by_layer(grad.reshape(LAYERS, slim, outputs))
    cross_blocks = cross_old.astype(BF16).reshape(rows, GROUP, rows).transpose(1, 0, 2)
    wide = acts.astype(F32)
    sums = jnp.stack([jnp.sum(wide * wide, axis=0), jnp.sum(wide * above.astype(F32), axis=0)])
    old_diagonals = jnp.stack(
        [block_diagonal(lax.dynamic_slice_in_dim(old, start, rows, 1)) for old in (factor_old, cross_old)]
    )
    here = (jnp.arange(GROUP) == place)[None, :, None]
    sums = weight * sums.reshape(2, GROUP, rows) + jnp.where(here, FACTOR_DECAY * old_diagonals[:, None, :], 0.0)
    message = sums.reshape(2, GROUP, LAYERS, slim).transpose(2, 1, 0, 3).reshape(LAYERS * GROUP, 2 * slim)
    message = jnp.pad(message, ((0, 0), (0, 128 - 2 * slim)))
    message, grad_rows, cross_blocks, shard, before, beyond = tied(
        message, grad_rows, cross_blocks, acts, before, beyond
    )
    other = across(shard)
    far = turned(before, 1)
    arrived = lax.all_to_all(message, LAYER + DP, 0, 0, tiled=True)
    arrived, other, far = tied(arrived, other, far)
    diagonals = jnp.sum(arrived.reshape(LAYERS, GROUP, 128), axis=1)[:, : 2 * slim].reshape(LAYERS, 2, slim)
    coupling = diagonals[:, 1]
    pivots = DAMPING + diagonals[:, 0]
    inverse = 1.0 / pivots
    coefficients = [
        jnp.broadcast_to(c[:, :, None], (LAYERS, slim, 128))
        for c in (pivots, inverse, coupling, coupling * inverse)
    ]

    initial_rows = chain_solve(initial_kernel, "first_solution", (grad_rows,), coefficients)
    initial_rows, other, far = tied(initial_rows, other, far)
    initial = by_layer(initial_rows).reshape(rows, outputs)

    remote = (far, turned(other, 1), turned(other, 3), across(far))
    initial, cross_slim, cross_blocks, *remote = tied(initial, cross_old.astype(BF16), cross_blocks, *remote)
    pieces = (shard, before, beyond, other, *remote)
    own = own_columns(order, pieces)
    columns = (own, along_layers(own, 1), along_layers(own, -1))
    row_old = along_layers(cross_slim, 1)
    col_old = lax.all_to_all(cross_blocks, DP, 0, 0, tiled=True)
    factor_new, factor_off, row_batch, row_off, col_off = refresh(
        weight, order, pieces, columns, factor_old, row_old
    )
    off = apply_blocks(order, gathered(initial), (factor_off, col_off, row_off), col_old)
    change_rows = chain_solve(change_kernel, "change", (grad_rows, initial_rows, by_layer(off)), coefficients)
    change = by_layer(change_rows).reshape(rows, outputs)
    update = initial.astype(F32) + change.astype(F32)

    dequant = jnp.repeat(jnp.exp2(exponents[0].astype(F32)), SCALE_BLOCK)[:, None]
    requant = jnp.repeat(jnp.exp2(-exponents[0].astype(F32)), SCALE_BLOCK)[:, None]
    moment = MOMENTUM * moments[0].astype(F32) * dequant + (1.0 - MOMENTUM) * update
    moments_new = (moment * requant).astype(BF16)
    master_new = master[0] - STEP_SIZE * moment
    own = master_new.astype(BF16)
    other, before, beyond, far = first_round(own)
    other, row_batch = tied(other, row_batch)
    cross_new = FACTOR_DECAY * cross_old + weight * along_layers(row_batch, -1).astype(F32)
    replicas = place_rows(order[:5], (own, before, beyond, other, far), None)
    replicas, cross_new = tied(replicas, cross_new)
    replicas = place_rows(order[5:], second_round(other, far), replicas)
    return (factor_new[None], cross_new[None], moments_new[None], master_new[None], replicas[None])


def solution(mesh):
    finer = Mesh(mesh.devices.reshape(2, 4, 2, 2, TURN), LAYER + DP)
    sharded = P(LAYER, DP, None)
    in_specs = (sharded,) * 5 + (P(LAYER, DP), sharded)
    out_specs = (sharded,) * 4 + (P(LAYER, None, None),)
    return jax.shard_map(body, mesh=finer, in_specs=in_specs, out_specs=out_specs, check_vma=False)
```

time: 292 us -> 286 us (0.979)
  blocking collectives: 0 us -> 54.2 us
  starting transfers between devices: 111 us -> 72 us
  between operations: 16.6 us -> 0.92 us
  local copies, waits for them, and re-layouts: 28.9 us -> 14.2 us
  Pallas kernels: 22.9 us -> 35.9 us
  waiting for transfers between devices: 94.2 us -> 90.4 us
    all_to_all x0 -> x2, blocking collectives: none -> 54.2 us  [the longest x1 30.1 us: body(): arrived = lax.all_to_all(message, LAYER + DP, 0, 0, tiled=True)]
    ppermute x18 -> x15, waiting for transfers between devices: 27.4 us -> 47.6 us  [turned(): lax.ppermute(value, 'dp_1', [(i, (i + steps) % TURN) for i in range(TURN)])]
    ppermute x10 -> x5, waiting for transfers between devices: 19.8 us -> 0.01 us  [along_layers(): return lax.ppermute(value, LAYER, pairs)]
    ppermute x10 -> x5, starting transfers between devices: 30.2 us -> 17.4 us  [along_layers(): return lax.ppermute(value, LAYER, pairs)]
    pallas_call x0 -> x3, Pallas kernels: none -> 11.6 us  [the longest x2 8.58 us: place_rows(): pl.pallas_call(place_kernel, grid_spec=pltpu.PrefetchScalarGridSpec(num_s...]
    all_to_all x4 -> x3, starting transfers between devices: 23.5 us -> 12.9 us  [by_layer(): return lax.all_to_all(value, LAYER, 0, 0)]
    ppermute x18 -> x15, starting transfers between devices: 30 us -> 21.5 us  [turned(): lax.ppermute(value, 'dp_1', [(i, (i + steps) % TURN) for i in range(TURN)])]
    all_to_all x2 -> x1, starting transfers between devices: 13.8 us -> 7.77 us  [body(): col_old = lax.all_to_all(cross_blocks, DP, 0, 0, tiled=True)]
  transfers between devices with their start and end apart: 40 -> 30, of which waited for: 15 -> 7; matrix products, arithmetic and copies ran while one was open for 13% -> 7% of each run, Pallas kernels for 5% -> 7%
where the time goes in v3:
time: 286 us; the launch traced here: 283 us
  waiting for transfers between devices  90.4 us (32%)
  starting transfers between devices  72 us (25%)
  blocking collectives  54.2 us (19%)
  Pallas kernels  35.9 us (13%)
  other arithmetic  15.4 us (5%)
  local copies, waits for them, and re-layouts  14.2 us (5%)
    ppermute x15, waiting for transfers between devices, turned(): lax.ppermute(value, 'dp_1', [(i, (i + steps) % TURN) for i in range(TURN)])  47.6 us
    all_to_all x1, blocking collectives, body(): arrived = lax.all_to_all(message, LAYER + DP, 0, 0, tiled=True)  30.1 us
    all_to_all x3, waiting for transfers between devices, by_layer(): return lax.all_to_all(value, LAYER, 0, 0)  30.1 us
    all_to_all x1, blocking collectives, by_layer(): return lax.all_to_all(value, LAYER, 0, 0)  24 us
    ppermute x15, starting transfers between devices, turned(): lax.ppermute(value, 'dp_1', [(i, (i + steps) % TURN) for i in range(TURN)])  21.5 us
    ppermute x5, starting transfers between devices, along_layers(): return lax.ppermute(value, LAYER, pairs)  17.4 us
    all_to_all x3, starting transfers between devices, by_layer(): return lax.all_to_all(value, LAYER, 0, 0)  12.9 us
    ppermute x6, waiting for transfers between devices, across(): return lax.ppermute(value, 'dp_0', [(0, 1), (1, 0)])  12.6 us
  transfers between devices with their start and end apart: 30, of which 7 were waited for; matrix products, arithmetic and copies ran while one was open for 7% of the time, Pallas kernels for 7%

profile of v3, /device:TPU:6, one launch (start us, length us, event | category | flops | bytes accessed | tf_op | source)
XLA Modules:
  0.0 283.0 jit_solution(5993726458519462858)
XLA Ops:
  0.6 4.6 %collective-permute-start = (bf16[256,2048]{1,0:T(8,128)(2,1)}, bf16[256,2048]{1,0:T(8,128)(2,1)}, u32[]{:S(2)}, u32[]{:S(2)}) collective-permute-start(bf16[256,2048]{1,0:T(8,128)(2,1)} %bitcast.67), channel_id=1, source_target_pairs={{8,0},{16,8},{24,16},{32,24},{40,32},{48,40},{56,48},{64,56},{72,6... | collective-permute-start | bytes 3145736 | tf_op jit(solution)/shard_map/ppermute | solution.py:27
  5.3 2.0 collective-permute-start.1
  7.3 2.2 collective-permute-start.2
  9.5 3.7 %all-to-all-start = ((bf16[16,16,1024]{2,1,0:T(8,128)(2,1)}), bf16[16,16,1024]{2,1,0:T(8,128)(2,1)S(1)}, u32[]{:S(2)}, u32[]{:S(2)}) async-start(bf16[16,16,1024]{2,1,0:T(8,128)(2,1)} %bitcast.86), calls=%async_computation | async-start | bytes 1048576 | tf_op jit(solution)/shard_map/all_to_all | solution.py:251
  13.2 1.1 fusion.5
  14.4 2.7 convert_element_type.50
  17.2 2.3 copy.22
  19.5 2.3 copy.23
  21.8 1.7 fusion
  24.0 6.7 %collective-permute-done.1.refs_1_.refs_2_ = bf16[256,2048]{1,0:T(8,128)(2,1)S(1)} collective-permute-done((bf16[256,2048]{1,0:T(8,128)(2,1)}, bf16[256,2048]{1,0:T(8,128)(2,1)S(1)}, u32[]{:S(2)}, u32[]{:S(2)}) %collective-permute-start.1) | collective-permute-done | bytes 1048608 | tf_op jit(solution)/shard_map/ppermute | solution.py:31
  30.7 1.4 collective-permute-start.3
  32.1 1.4 collective-permute-start.4
  33.5 30.1 %all_to_all.37 = f32[128,1,128]{2,1,0:T(1,128)S(1)} all-to-all(f32[128,1,128]{2,1,0:T(1,128)S(1)} %bitcast.87), channel_id=1, replica_groups=mesh['layer_0'=2,'layer_1'=4,'layer_2'=2,'dp_0'=2,'dp_1'=4] {'layer_0','..., dimensions={0} | all-to-all | bytes 131072 | tf_op jit(solution)/shard_map/all_to_all | solution.py:286
  64.2 1.1 first_solution.1.initial
  65.8 2.7 collective-permute-start.6
  68.5 1.5 collective-permute-start.7
  70.7 4.3 %all-to-all-start.2 = ((bf16[16,16,1024]{2,1,0:T(8,128)(2,1)}), bf16[16,16,1024]{2,1,0:T(8,128)(2,1)S(1)}, u32[]{:S(2)}, u32[]{:S(2)}) async-start(bf16[16,16,1024]{2,1,0:T(8,128)(2,1)} %first_solution.1.initial), calls=%async_computation.2 | async-start | bytes 1048576 | tf_op jit(solution)/shard_map/all_to_all | solution.py:251
  74.9 2.7 convert_bitcast_fusion
  77.7 20.7 %all-to-all-done.2 = bf16[16,16,1024]{2,1,0:T(8,128)(2,1)S(1)} async-done(((bf16[16,16,1024]{2,1,0:T(8,128)(2,1)}), bf16[16,16,1024]{2,1,0:T(8,128)(2,1)S(1)}, u32[]{:S(2)}, u32[]{:S(2)}) %all-to-all-start.2) | async-done | bytes 524320 | tf_op jit(solution)/shard_map/all_to_all | solution.py:251
  98.3 3.1 %collective-permute-start.11 = (bf16[256,1024]{1,0:T(8,128)(2,1)S(1)}, bf16[256,1024]{1,0:T(8,128)(2,1)S(1)}, u32[]{:S(2)}, u32[]{:S(2)}) collective-permute-start(bf16[256,1024]{1,0:T(8,128)(2,1)S(1)} %bitcast.73), channel_id=1, source_target_pairs={{0,4},{4,0},{1,5},{5,1},{2,6},{6,2},{3,7},{7,3},{8,12},{12,8},{9,1... | collective-permute-start | bytes 1572872 | tf_op jit(solution)/shard_map/ppermute | solution.py:35
  101.5 3.0 %own_columns.1.refs_9_ = bf16[8,256,256]{2,1,0:T(8,128)(2,1)} custom-call(s32[8]{0:T(128)} %fusion.9.order.refs_0_, bf16[256,2048]{1,0:T(8,128)(2,1)} %bitcast.70, bf16[256,2048]{1,0:T(8,128)(2,1)} %copy-done.9, bf16[256,2048]{1,0:T(8,128)(2,1)} %collective-permute-done.2.refs_2_.refs_3_, bf16[256,2048]{1,0:T(8,128)(2,1)} %collective-permute-done.3.refs_3_.refs_4_, ...), custom_call_target="tpu_custom_call" | custom-call | tf_op jit(solution)/shard_map/own_columns/pallas_call | solution.py:73
  104.5 2.0 collective-permute-start.8
  106.5 5.8 %collective-permute-start.9 = (bf16[8,256,256]{2,1,0:T(8,128)(2,1)}, bf16[8,256,256]{2,1,0:T(8,128)(2,1)}, u32[]{:S(2)}, u32[]{:S(2)}) collective-permute-start(bf16[8,256,256]{2,1,0:T(8,128)(2,1)} %own_columns.1.refs_9_), channel_id=1, source_target_pairs={{8,0},{16,8},{24,16},{32,24},{40,32},{48,40},{56,48},{64,56},{72,6... | collective-permute-start | bytes 3145736 | tf_op jit(solution)/shard_map/ppermute | solution.py:27
  112.3 3.3 %collective-permute-start.13 = (bf16[256,1024]{1,0:T(8,128)(2,1)S(1)}, bf16[256,1024]{1,0:T(8,128)(2,1)}, u32[]{:S(2)}, u32[]{:S(2)}) collective-permute-start(bf16[256,1024]{1,0:T(8,128)(2,1)S(1)} %bitcast.75), channel_id=1, source_target_pairs={{0,3},{1,0},{2,1},{3,2},{4,7},{5,4},{6,5},{7,6},{8,11},{9,8},{10,9... | collective-permute-start | bytes 1572872 | tf_op jit(solution)/shard_map/ppermute | solution.py:31
  115.6 1.9 collective-permute-start.10
  117.5 7.8 %all-to-all-start.3 = ((bf16[8,256,256]{2,1,0:T(8,128)(2,1)}), bf16[8,256,256]{2,1,0:T(8,128)(2,1)}, u32[]{:S(2)}, u32[]{:S(2)}) async-start(bf16[8,256,256]{2,1,0:T(8,128)(2,1)} %bitcast.81), calls=%async_computation.3 | async-start | bytes 2097152 | tf_op jit(solution)/shard_map/all_to_all | solution.py:307
  125.3 19.4 %collective-permute-done.13.refs_2_ = bf16[256,1024]{1,0:T(8,128)(2,1)} collective-permute-done((bf16[256,1024]{1,0:T(8,128)(2,1)S(1)}, bf16[256,1024]{1,0:T(8,128)(2,1)}, u32[]{:S(2)}, u32[]{:S(2)}) %collective-permute-start.13) | collective-permute-done | bytes 524320 | tf_op jit(solution)/shard_map/ppermute | solution.py:31
  144.7 1.6 collective-permute-start.15
  146.2 2.2 collective-permute-start.16
  149.1 11.9 %refresh.1 = (f32[256,2048]{1,0:T(8,128)}, bf16[256,2048]{1,0:T(8,128)(2,1)S(1)}, bf16[256,2048]{1,0:T(8,128)(2,1)S(1)}, bf16[256,2048]{1,0:T(8,128)(2,1)S(1)}, bf16[256,2048]{1,0:T(8,128)(2,1)S(1)}) custom-call(s32[8]{0:T(128)S(1)} %copy-done.6, bf16[256,2048]{1,0:T(8,128)(2,1)S(1)} %bitcast.72, bf16[256,2048]{1,0:T(8,128)(2,1)} %copy-done.9, ...), custom_call_target="tpu_custom_call" | custom-call | tf_op jit(solution)/shard_map/refresh/pallas_call | solution.py:112
  163.0 1.0 copy-done.5
  165.0 1.2 copy-done.3
  166.2 8.6 %apply_blocks.1 = bf16[16,48,1024]{2,1,0:T(8,128)(2,1)} custom-call(s32[8]{0:T(128)S(1)} %copy-done.6, bf16[256,1024]{1,0:T(8,128)(2,1)S(1)} %bitcast.77, bf16[256,1024]{1,0:T(8,128)(2,1)} %collective-permute-done.12.refs_1_, bf16[256,1024]{1,0:T(8,128)(2,1)} %collective-permute-done.13.refs_2_, bf16[256,1024]{1,0:T(8,128)(2,1)S(1)} %collective-permute-done.11.refs_3_, ...), custom_call_target="tpu_custom_call" | custom-call | tf_op jit(solution)/shard_map/apply_blocks/pallas_call | solution.py:180
  174.8 24.0 %all_to_all.38.off = bf16[16,48,1024]{2,1,0:T(8,128)(2,1)S(1)} all-to-all(bf16[16,48,1024]{2,1,0:T(8,128)(2,1)} %apply_blocks.1), channel_id=1, replica_groups=mesh['layer_0'=2,'layer_1'=4,'layer_2'=2,'dp_0'=2,'dp_1'=4] {'layer_0','..., dimensions={0} | all-to-all | bytes 3145728 | tf_op jit(solution)/shard_map/all_to_all | solution.py:251
  198.9 2.7 change.1
  201.6 4.9 %all-to-all-start.5 = ((bf16[16,16,1024]{2,1,0:T(8,128)(2,1)}), bf16[16,16,1024]{2,1,0:T(8,128)(2,1)S(1)}, u32[]{:S(2)}, u32[]{:S(2)}) async-start(bf16[16,16,1024]{2,1,0:T(8,128)(2,1)} %change.1), calls=%async_computation.5 | async-start | bytes 1048576 | tf_op jit(solution)/shard_map/all_to_all | solution.py:251
  206.5 9.4 %all-to-all-done.5 = bf16[16,16,1024]{2,1,0:T(8,128)(2,1)S(1)} async-done(((bf16[16,16,1024]{2,1,0:T(8,128)(2,1)}), bf16[16,16,1024]{2,1,0:T(8,128)(2,1)S(1)}, u32[]{:S(2)}, u32[]{:S(2)}) %all-to-all-start.5) | async-done | bytes 524320 | tf_op jit(solution)/shard_map/all_to_all | solution.py:251
  216.0 2.9 %fusion.12 = (bf16[256,1024]{1,0:T(8,128)(2,1)S(1)}, f32[256,1024]{1,0:T(8,128)}, bf16[1,256,1024]{2,1,0:T(8,128)(2,1)}) fusion(bf16[16,16,1024]{2,1,0:T(8,128)(2,1)S(1)} %all-to-all-done.5, bf16[256,1024]{1,0:T(8,128)(2,1)S(1)} %bitcast.78, f32[256]{0:T(256)S(1)} %get-tuple-element.83, bf16[1,256,1024]{2,1,0:T(8,128)(2,1)S(1)} %copy-done.11, ...), kind=kLoop, calls=%fused_computation.35 | loop fusion | flops 3145728 | bytes 4720640 | tf_op jit(solution)/shard_map/convert_element_type | solution.py:321
  218.9 2.9 %collective-permute-start.20 = (bf16[256,1024]{1,0:T(8,128)(2,1)S(1)}, bf16[256,1024]{1,0:T(8,128)(2,1)}, u32[]{:S(2)}, u32[]{:S(2)}) collective-permute-start(bf16[256,1024]{1,0:T(8,128)(2,1)S(1)} %get-tuple-element.71.refs_0_), channel_id=1, source_target_pairs={{0,4},{4,0},{1,5},{5,1},{2,6},{6,2},{3,7},{7,3},{8,12},{12,8},{9,1... | collective-permute-start | bytes 1572872 | tf_op jit(solution)/shard_map/ppermute | solution.py:35
  221.8 12.6 %collective-permute-done.20.refs_3_ = bf16[256,1024]{1,0:T(8,128)(2,1)} collective-permute-done((bf16[256,1024]{1,0:T(8,128)(2,1)S(1)}, bf16[256,1024]{1,0:T(8,128)(2,1)}, u32[]{:S(2)}, u32[]{:S(2)}) %collective-permute-start.20) | collective-permute-done | bytes 524320 | tf_op jit(solution)/shard_map/ppermute | solution.py:35
  234.4 3.1 %collective-permute-start.22 = (bf16[256,2048]{1,0:T(8,128)(2,1)S(1)}, bf16[256,2048]{1,0:T(8,128)(2,1)}, u32[]{:S(2)}, u32[]{:S(2)}) collective-permute-start(bf16[256,2048]{1,0:T(8,128)(2,1)S(1)} %copy-done.8), channel_id=1, source_target_pairs={{8,0},{16,8},{24,16},{32,24},{40,32},{48,40},{56,48},{64,56},{72,6... | collective-permute-start | bytes 3145736 | tf_op jit(solution)/shard_map/ppermute | solution.py:27
  237.6 3.5 %collective-permute-start.21 = (bf16[256,1024]{1,0:T(8,128)(2,1)S(1)}, bf16[256,1024]{1,0:T(8,128)(2,1)}, u32[]{:S(2)}, u32[]{:S(2)}) collective-permute-start(bf16[256,1024]{1,0:T(8,128)(2,1)S(1)} %get-tuple-element.71.refs_0_), channel_id=1, source_target_pairs={{0,2},{1,3},{2,0},{3,1},{4,6},{5,7},{6,4},{7,5},{8,10},{9,11},{10,... | collective-permute-start | bytes 1572872 | tf_op jit(solution)/shard_map/ppermute | solution.py:31
  242.3 1.4 collective-permute-start.23
  243.7 21.0 %collective-permute-done.18.refs_1_ = bf16[256,1024]{1,0:T(8,128)(2,1)} collective-permute-done((bf16[256,1024]{1,0:T(8,128)(2,1)S(1)}, bf16[256,1024]{1,0:T(8,128)(2,1)}, u32[]{:S(2)}, u32[]{:S(2)}) %collective-permute-start.18) | collective-permute-done | bytes 524320 | tf_op jit(solution)/shard_map/ppermute | solution.py:31
  265.3 2.9 %collective-permute-start.25 = (bf16[256,1024]{1,0:T(8,128)(2,1)}, bf16[256,1024]{1,0:T(8,128)(2,1)S(1)}, u32[]{:S(2)}, u32[]{:S(2)}) collective-permute-start(bf16[256,1024]{1,0:T(8,128)(2,1)} %collective-permute-done.21.refs_4_), channel_id=1, source_target_pairs={{0,4},{4,0},{1,5},{5,1},{2,6},{6,2},{3,7},{7,3},{8,12},{12,8},{9,1... | collective-permute-start | bytes 1572872 | tf_op jit(solution)/shard_map/ppermute | solution.py:35
  269.0 4.9 %place_rows.2.refs_3_ = bf16[2048,1024]{1,0:T(8,128)(2,1)} custom-call(s32[5]{0:T(128)} %bitcast.79, bf16[256,1024]{1,0:T(8,128)(2,1)} %copy-done.10, bf16[256,1024]{1,0:T(8,128)(2,1)} %collective-permute-done.18.refs_1_, bf16[256,1024]{1,0:T(8,128)(2,1)} %copy-done.15, bf16[256,1024]{1,0:T(8,128)(2,1)} %collective-permute-done.20.refs_3_, ...), custom_call_target="tpu_custom_call" | custom-call | tf_op jit(solution)/shard_map/place_rows/pallas_call | solution.py:139
  273.8 3.7 %bitcast_add_fusion = f32[256,2048]{1,0:T(8,128)} fusion(bf16[256,2048]{1,0:T(8,128)(2,1)} %collective-permute-done.22, f32[1,256,2048]{2,1,0:T(8,128)} %param.10), kind=kLoop, calls=%fused_computation.4 | loop fusion | flops 2097152 | bytes 5242880 | tf_op jit(solution)/shard_map/add | solution.py:324
  279.3 3.7 %place_rows.3 = bf16[2048,1024]{1,0:T(8,128)(2,1)} custom-call(s32[3]{0:T(128)} %slice.19.order, bf16[256,1024]{1,0:T(8,128)(2,1)} %copy-done.12, bf16[256,1024]{1,0:T(8,128)(2,1)} %copy-done.13, bf16[256,1024]{1,0:T(8,128)(2,1)} %copy-done.14, bf16[2048,1024]{1,0:T(8,128)(2,1)} %place_rows.2.refs_3_), custom_call_target="tpu_custom_call", output_to_operand_aliasing={{}: (4, {})} | custom-call | tf_op jit(solution)/shard_map/place_rows/pallas_call | solution.py:139
  (89 shorter events, 10.5 us)
Async XLA Ops:
  0.6 21.2 %collective-permute-start = (bf16[256,2048]{1,0:T(8,128)(2,1)}, bf16[256,2048]{1,0:T(8,128)(2,1)}, u32[]{:S(2)}, u32[]{:S(2)}) collective-permute-start(bf16[256,2048]{1,0:T(8,128)(2,1)} %bitcast.67), channel_id=1, source_target_pairs={{8,0},{16,8},{24,16},{32,24},{40,32},{48,40},{56,48},{64,56},{72,6... | collective-permute-start | bytes 3145736 | tf_op jit(solution)/shard_map/ppermute | solution.py:27
  5.3 25.4 %collective-permute-start.1 = (bf16[256,2048]{1,0:T(8,128)(2,1)}, bf16[256,2048]{1,0:T(8,128)(2,1)S(1)}, u32[]{:S(2)}, u32[]{:S(2)}) collective-permute-start(bf16[256,2048]{1,0:T(8,128)(2,1)} %bitcast.68), channel_id=1, source_target_pairs={{0,1},{1,2},{2,3},{3,0},{4,5},{5,6},{6,7},{7,4},{8,9},{9,10},{10,1... | collective-permute-start | bytes 3145736 | tf_op jit(solution)/shard_map/ppermute | solution.py:31
  7.3 23.5 %collective-permute-start.2 = (bf16[256,2048]{1,0:T(8,128)(2,1)}, bf16[256,2048]{1,0:T(8,128)(2,1)}, u32[]{:S(2)}, u32[]{:S(2)}) collective-permute-start(bf16[256,2048]{1,0:T(8,128)(2,1)} %bitcast.69), channel_id=1, source_target_pairs={{0,3},{1,0},{2,1},{3,2},{4,7},{5,4},{6,5},{7,6},{8,11},{9,8},{10,9... | collective-permute-start | bytes 3145736 | tf_op jit(solution)/shard_map/ppermute | solution.py:31
  9.5 14.5 %all-to-all-start = ((bf16[16,16,1024]{2,1,0:T(8,128)(2,1)}), bf16[16,16,1024]{2,1,0:T(8,128)(2,1)S(1)}, u32[]{:S(2)}, u32[]{:S(2)}) async-start(bf16[16,16,1024]{2,1,0:T(8,128)(2,1)} %bitcast.86), calls=%async_computation | async-start | bytes 1048576 | tf_op jit(solution)/shard_map/all_to_all | solution.py:251
  17.1 4.6 %copy-start = (bf16[1,256,2048]{2,1,0:T(8,128)(2,1)S(1)}, bf16[1,256,2048]{2,1,0:T(8,128)(2,1)}, u32[]{:S(2)}) copy-start(bf16[1,256,2048]{2,1,0:T(8,128)(2,1)} %param.8) | copy-start | bytes 3145732
  23.5 46.7 %copy-start.16 = (s32[8]{0:T(128)S(1)}, s32[8]{0:T(128)}, u32[]{:S(2)}) copy-start(s32[8]{0:T(128)} %constant.57.clone) | copy-start | bytes 100
  30.7 47.0 %copy-start.9 = (bf16[256,2048]{1,0:T(8,128)(2,1)}, bf16[256,2048]{1,0:T(8,128)(2,1)S(1)}, u32[]{:S(2)}) copy-start(bf16[256,2048]{1,0:T(8,128)(2,1)S(1)} %collective-permute-done.1.refs_1_.refs_2_) | copy-start | bytes 3145732
  30.7 32.9 %collective-permute-start.3 = (bf16[256,2048]{1,0:T(8,128)(2,1)S(1)}, bf16[256,2048]{1,0:T(8,128)(2,1)}, u32[]{:S(2)}, u32[]{:S(2)}) collective-permute-start(bf16[256,2048]{1,0:T(8,128)(2,1)S(1)} %bitcast.71), channel_id=1, source_target_pairs={{0,4},{4,0},{1,5},{5,1},{2,6},{6,2},{3,7},{7,3},{8,12},{12,8},{9,1... | collective-permute-start | bytes 3145736 | tf_op jit(solution)/shard_map/ppermute | solution.py:35
  32.1 31.5 %collective-permute-start.4 = (bf16[256,2048]{1,0:T(8,128)(2,1)S(1)}, bf16[256,2048]{1,0:T(8,128)(2,1)}, u32[]{:S(2)}, u32[]{:S(2)}) collective-permute-start(bf16[256,2048]{1,0:T(8,128)(2,1)S(1)} %collective-permute-done.1.refs_1_.refs_2_), channel_id=1, source_target_pairs={{0,1},{1,2},{2,3},{3,0},{4,5},{5,6},{6,7},{7,4},{8,9},{9,10},{10,1... | collective-permute-start | bytes 3145736 | tf_op jit(solution)/shard_map/ppermute | solution.py:31
  65.3 33.0 %collective-permute-start.5 = (bf16[256,2048]{1,0:T(8,128)(2,1)}, bf16[256,2048]{1,0:T(8,128)(2,1)}, u32[]{:S(2)}, u32[]{:S(2)}) collective-permute-start(bf16[256,2048]{1,0:T(8,128)(2,1)} %collective-permute-done.3.refs_3_.refs_4_), channel_id=1, source_target_pairs={{0,1},{1,2},{2,3},{3,0},{4,5},{5,6},{6,7},{7,4},{8,9},{9,10},{10,1... | collective-permute-start | bytes 3145736 | tf_op jit(solution)/shard_map/ppermute | solution.py:31
  65.8 32.5 %collective-permute-start.6 = (bf16[256,2048]{1,0:T(8,128)(2,1)}, bf16[256,2048]{1,0:T(8,128)(2,1)}, u32[]{:S(2)}, u32[]{:S(2)}) collective-permute-start(bf16[256,2048]{1,0:T(8,128)(2,1)} %collective-permute-done.3.refs_3_.refs_4_), channel_id=1, source_target_pairs={{0,3},{1,0},{2,1},{3,2},{4,7},{5,4},{6,5},{7,6},{8,11},{9,8},{10,9... | collective-permute-start | bytes 3145736 | tf_op jit(solution)/shard_map/ppermute | solution.py:31
  68.5 29.8 %collective-permute-start.7 = (bf16[256,2048]{1,0:T(8,128)(2,1)}, bf16[256,2048]{1,0:T(8,128)(2,1)}, u32[]{:S(2)}, u32[]{:S(2)}) collective-permute-start(bf16[256,2048]{1,0:T(8,128)(2,1)} %collective-permute-done.4.refs_4_.refs_5_), channel_id=1, source_target_pairs={{0,4},{4,0},{1,5},{5,1},{2,6},{6,2},{3,7},{7,3},{8,12},{12,8},{9,1... | collective-permute-start | bytes 3145736 | tf_op jit(solution)/shard_map/ppermute | solution.py:35
  70.7 27.7 %all-to-all-start.2 = ((bf16[16,16,1024]{2,1,0:T(8,128)(2,1)}), bf16[16,16,1024]{2,1,0:T(8,128)(2,1)S(1)}, u32[]{:S(2)}, u32[]{:S(2)}) async-start(bf16[16,16,1024]{2,1,0:T(8,128)(2,1)} %first_solution.1.initial), calls=%async_computation.2 | async-start | bytes 1048576 | tf_op jit(solution)/shard_map/all_to_all | solution.py:251
  98.3 17.3 %collective-permute-start.11 = (bf16[256,1024]{1,0:T(8,128)(2,1)S(1)}, bf16[256,1024]{1,0:T(8,128)(2,1)S(1)}, u32[]{:S(2)}, u32[]{:S(2)}) collective-permute-start(bf16[256,1024]{1,0:T(8,128)(2,1)S(1)} %bitcast.73), channel_id=1, source_target_pairs={{0,4},{4,0},{1,5},{5,1},{2,6},{6,2},{3,7},{7,3},{8,12},{12,8},{9,1... | collective-permute-start | bytes 1572872 | tf_op jit(solution)/shard_map/ppermute | solution.py:35
  101.5 14.1 %collective-permute-start.12 = (bf16[256,1024]{1,0:T(8,128)(2,1)S(1)}, bf16[256,1024]{1,0:T(8,128)(2,1)}, u32[]{:S(2)}, u32[]{:S(2)}) collective-permute-start(bf16[256,1024]{1,0:T(8,128)(2,1)S(1)} %bitcast.74), channel_id=1, source_target_pairs={{0,1},{1,2},{2,3},{3,0},{4,5},{5,6},{6,7},{7,4},{8,9},{9,10},{10,1... | collective-permute-start | bytes 1572872 | tf_op jit(solution)/shard_map/ppermute | solution.py:31
  104.5 44.7 %copy-start.1 = (bf16[1,256,2048]{2,1,0:T(8,128)(2,1)S(1)}, bf16[1,256,2048]{2,1,0:T(8,128)(2,1)}, u32[]{:S(2)}) copy-start(bf16[1,256,2048]{2,1,0:T(8,128)(2,1)} %param.8) | copy-start | bytes 3145732
  104.5 44.7 %copy-start.6 = (s32[8]{0:T(128)S(1)}, s32[8]{0:T(128)}, u32[]{:S(2)}) copy-start(s32[8]{0:T(128)} %fusion.9.order.refs_0_) | copy-start | bytes 100
  104.5 44.0 %collective-permute-start.8 = (bf16[8,256,256]{2,1,0:T(8,128)(2,1)}, bf16[8,256,256]{2,1,0:T(8,128)(2,1)}, u32[]{:S(2)}, u32[]{:S(2)}) collective-permute-start(bf16[8,256,256]{2,1,0:T(8,128)(2,1)} %own_columns.1.refs_9_), channel_id=1, source_target_pairs={{0,8},{8,16},{16,24},{24,32},{32,40},{40,48},{48,56},{56,64},{64,7... | collective-permute-start | bytes 3145736 | tf_op jit(solution)/shard_map/ppermute | solution.py:27
  106.5 42.6 %collective-permute-start.9 = (bf16[8,256,256]{2,1,0:T(8,128)(2,1)}, bf16[8,256,256]{2,1,0:T(8,128)(2,1)}, u32[]{:S(2)}, u32[]{:S(2)}) collective-permute-start(bf16[8,256,256]{2,1,0:T(8,128)(2,1)} %own_columns.1.refs_9_), channel_id=1, source_target_pairs={{8,0},{16,8},{24,16},{32,24},{40,32},{48,40},{56,48},{64,56},{72,6... | collective-permute-start | bytes 3145736 | tf_op jit(solution)/shard_map/ppermute | solution.py:27
  112.3 32.4 %collective-permute-start.13 = (bf16[256,1024]{1,0:T(8,128)(2,1)S(1)}, bf16[256,1024]{1,0:T(8,128)(2,1)}, u32[]{:S(2)}, u32[]{:S(2)}) collective-permute-start(bf16[256,1024]{1,0:T(8,128)(2,1)S(1)} %bitcast.75), channel_id=1, source_target_pairs={{0,3},{1,0},{2,1},{3,2},{4,7},{5,4},{6,5},{7,6},{8,11},{9,8},{10,9... | collective-permute-start | bytes 1572872 | tf_op jit(solution)/shard_map/ppermute | solution.py:31
  115.6 29.1 %collective-permute-start.14 = (bf16[256,1024]{1,0:T(8,128)(2,1)S(1)}, bf16[256,1024]{1,0:T(8,128)(2,1)}, u32[]{:S(2)}, u32[]{:S(2)}) collective-permute-start(bf16[256,1024]{1,0:T(8,128)(2,1)S(1)} %bitcast.76), channel_id=1, source_target_pairs={{0,2},{1,3},{2,0},{3,1},{4,6},{5,7},{6,4},{7,5},{8,10},{9,11},{10,... | collective-permute-start | bytes 1572872 | tf_op jit(solution)/shard_map/ppermute | solution.py:31
  115.6 33.5 %collective-permute-start.10 = (bf16[256,2048]{1,0:T(8,128)(2,1)}, bf16[256,2048]{1,0:T(8,128)(2,1)}, u32[]{:S(2)}, u32[]{:S(2)}) collective-permute-start(bf16[256,2048]{1,0:T(8,128)(2,1)} %convert_bitcast_fusion), channel_id=1, source_target_pairs={{0,8},{8,16},{16,24},{24,32},{32,40},{40,48},{48,56},{56,64},{64,7... | collective-permute-start | bytes 3145736 | tf_op jit(solution)/shard_map/ppermute | solution.py:27
  117.5 47.4 %all-to-all-start.3 = ((bf16[8,256,256]{2,1,0:T(8,128)(2,1)}), bf16[8,256,256]{2,1,0:T(8,128)(2,1)}, u32[]{:S(2)}, u32[]{:S(2)}) async-start(bf16[8,256,256]{2,1,0:T(8,128)(2,1)} %bitcast.81), calls=%async_computation.3 | async-start | bytes 2097152 | tf_op jit(solution)/shard_map/all_to_all | solution.py:307
  144.7 20.3 %collective-permute-start.15 = (bf16[256,1024]{1,0:T(8,128)(2,1)S(1)}, bf16[256,1024]{1,0:T(8,128)(2,1)}, u32[]{:S(2)}, u32[]{:S(2)}) collective-permute-start(bf16[256,1024]{1,0:T(8,128)(2,1)S(1)} %collective-permute-done.11.refs_3_), channel_id=1, source_target_pairs={{0,1},{1,2},{2,3},{3,0},{4,5},{5,6},{6,7},{7,4},{8,9},{9,10},{10,1... | collective-permute-start | bytes 1572872 | tf_op jit(solution)/shard_map/ppermute | solution.py:31
  146.2 18.7 %collective-permute-start.16 = (bf16[256,1024]{1,0:T(8,128)(2,1)S(1)}, bf16[256,1024]{1,0:T(8,128)(2,1)}, u32[]{:S(2)}, u32[]{:S(2)}) collective-permute-start(bf16[256,1024]{1,0:T(8,128)(2,1)S(1)} %collective-permute-done.11.refs_3_), channel_id=1, source_target_pairs={{0,3},{1,0},{2,1},{3,2},{4,7},{5,4},{6,5},{7,6},{8,11},{9,8},{10,9... | collective-permute-start | bytes 1572872 | tf_op jit(solution)/shard_map/ppermute | solution.py:31
  148.5 16.5 %collective-permute-start.17 = (bf16[256,1024]{1,0:T(8,128)(2,1)}, bf16[256,1024]{1,0:T(8,128)(2,1)}, u32[]{:S(2)}, u32[]{:S(2)}) collective-permute-start(bf16[256,1024]{1,0:T(8,128)(2,1)} %collective-permute-done.14.refs_4_), channel_id=1, source_target_pairs={{0,4},{4,0},{1,5},{5,1},{2,6},{6,2},{3,7},{7,3},{8,12},{12,8},{9,1... | collective-permute-start | bytes 1572872 | tf_op jit(solution)/shard_map/ppermute | solution.py:35
  161.0 1.0 copy-start.2
  162.0 1.0 copy-start.4
  163.0 1.0 copy-start.5
  164.0 1.0 copy-start.7
  165.0 1.2 copy-start.3
  198.9 7.6 %copy-start.17 = (s32[1,2]{1,0:T(1,128)S(1)}, s32[1,2]{1,0:T(1,128)}, u32[]{:S(2)}) copy-start(s32[1,2]{1,0:T(1,128)} %param.13) | copy-start | bytes 28
  198.9 17.1 %copy-start.11 = (bf16[1,256,1024]{2,1,0:T(8,128)(2,1)S(1)}, bf16[1,256,1024]{2,1,0:T(8,128)(2,1)}, u32[]{:S(2)}) copy-start(bf16[1,256,1024]{2,1,0:T(8,128)(2,1)} %param.12) | copy-start | bytes 1572868
  201.6 14.4 %all-to-all-start.5 = ((bf16[16,16,1024]{2,1,0:T(8,128)(2,1)}), bf16[16,16,1024]{2,1,0:T(8,128)(2,1)S(1)}, u32[]{:S(2)}, u32[]{:S(2)}) async-start(bf16[16,16,1024]{2,1,0:T(8,128)(2,1)} %change.1), calls=%async_computation.5 | async-start | bytes 1048576 | tf_op jit(solution)/shard_map/all_to_all | solution.py:251
  216.0 18.4 %copy-start.8 = (bf16[256,2048]{1,0:T(8,128)(2,1)S(1)}, bf16[256,2048]{1,0:T(8,128)(2,1)}, u32[]{:S(2)}) copy-start(bf16[256,2048]{1,0:T(8,128)(2,1)} %copy-done.7) | copy-start | bytes 3145732
  218.9 50.1 %copy-start.10 = (bf16[256,1024]{1,0:T(8,128)(2,1)}, bf16[256,1024]{1,0:T(8,128)(2,1)S(1)}, u32[]{:S(2)}) copy-start(bf16[256,1024]{1,0:T(8,128)(2,1)S(1)} %get-tuple-element.71.refs_0_) | copy-start | bytes 1572868
  218.9 15.5 %collective-permute-start.20 = (bf16[256,1024]{1,0:T(8,128)(2,1)S(1)}, bf16[256,1024]{1,0:T(8,128)(2,1)}, u32[]{:S(2)}, u32[]{:S(2)}) collective-permute-start(bf16[256,1024]{1,0:T(8,128)(2,1)S(1)} %get-tuple-element.71.refs_0_), channel_id=1, source_target_pairs={{0,4},{4,0},{1,5},{5,1},{2,6},{6,2},{3,7},{7,3},{8,12},{12,8},{9,1... | collective-permute-start | bytes 1572872 | tf_op jit(solution)/shard_map/ppermute | solution.py:35
  234.4 39.5 %collective-permute-start.22 = (bf16[256,2048]{1,0:T(8,128)(2,1)S(1)}, bf16[256,2048]{1,0:T(8,128)(2,1)}, u32[]{:S(2)}, u32[]{:S(2)}) collective-permute-start(bf16[256,2048]{1,0:T(8,128)(2,1)S(1)} %copy-done.8), channel_id=1, source_target_pairs={{8,0},{16,8},{24,16},{32,24},{40,32},{48,40},{56,48},{64,56},{72,6... | collective-permute-start | bytes 3145736 | tf_op jit(solution)/shard_map/ppermute | solution.py:27
  237.5 27.2 %collective-permute-start.18 = (bf16[256,1024]{1,0:T(8,128)(2,1)S(1)}, bf16[256,1024]{1,0:T(8,128)(2,1)}, u32[]{:S(2)}, u32[]{:S(2)}) collective-permute-start(bf16[256,1024]{1,0:T(8,128)(2,1)S(1)} %get-tuple-element.71.refs_0_), channel_id=1, source_target_pairs={{0,1},{1,2},{2,3},{3,0},{4,5},{5,6},{6,7},{7,4},{8,9},{9,10},{10,1... | collective-permute-start | bytes 1572872 | tf_op jit(solution)/shard_map/ppermute | solution.py:31
  237.6 27.7 %collective-permute-start.21 = (bf16[256,1024]{1,0:T(8,128)(2,1)S(1)}, bf16[256,1024]{1,0:T(8,128)(2,1)}, u32[]{:S(2)}, u32[]{:S(2)}) collective-permute-start(bf16[256,1024]{1,0:T(8,128)(2,1)S(1)} %get-tuple-element.71.refs_0_), channel_id=1, source_target_pairs={{0,2},{1,3},{2,0},{3,1},{4,6},{5,7},{6,4},{7,5},{8,10},{9,11},{10,... | collective-permute-start | bytes 1572872 | tf_op jit(solution)/shard_map/ppermute | solution.py:31
  241.0 27.1 %collective-permute-start.19 = (bf16[256,1024]{1,0:T(8,128)(2,1)S(1)}, bf16[256,1024]{1,0:T(8,128)(2,1)S(1)}, u32[]{:S(2)}, u32[]{:S(2)}) collective-permute-start(bf16[256,1024]{1,0:T(8,128)(2,1)S(1)} %get-tuple-element.71.refs_0_), channel_id=1, source_target_pairs={{0,3},{1,0},{2,1},{3,2},{4,7},{5,4},{6,5},{7,6},{8,11},{9,8},{10,9... | collective-permute-start | bytes 1572872 | tf_op jit(solution)/shard_map/ppermute | solution.py:31
  242.3 35.2 %collective-permute-start.23 = (bf16[256,1024]{1,0:T(8,128)(2,1)}, bf16[256,1024]{1,0:T(8,128)(2,1)S(1)}, u32[]{:S(2)}, u32[]{:S(2)}) collective-permute-start(bf16[256,1024]{1,0:T(8,128)(2,1)} %collective-permute-done.20.refs_3_), channel_id=1, source_target_pairs={{0,1},{1,2},{2,3},{3,0},{4,5},{5,6},{6,7},{7,4},{8,9},{9,10},{10,1... | collective-permute-start | bytes 1572872 | tf_op jit(solution)/shard_map/ppermute | solution.py:31
  264.7 12.9 %collective-permute-start.24 = (bf16[256,1024]{1,0:T(8,128)(2,1)}, bf16[256,1024]{1,0:T(8,128)(2,1)S(1)}, u32[]{:S(2)}, u32[]{:S(2)}) collective-permute-start(bf16[256,1024]{1,0:T(8,128)(2,1)} %collective-permute-done.20.refs_3_), channel_id=1, source_target_pairs={{0,3},{1,0},{2,1},{3,2},{4,7},{5,4},{6,5},{7,6},{8,11},{9,8},{10,9... | collective-permute-start | bytes 1572872 | tf_op jit(solution)/shard_map/ppermute | solution.py:31
  265.3 12.3 %collective-permute-start.25 = (bf16[256,1024]{1,0:T(8,128)(2,1)}, bf16[256,1024]{1,0:T(8,128)(2,1)S(1)}, u32[]{:S(2)}, u32[]{:S(2)}) collective-permute-start(bf16[256,1024]{1,0:T(8,128)(2,1)} %collective-permute-done.21.refs_4_), channel_id=1, source_target_pairs={{0,4},{4,0},{1,5},{5,1},{2,6},{6,2},{3,7},{7,3},{8,12},{12,8},{9,1... | collective-permute-start | bytes 1572872 | tf_op jit(solution)/shard_map/ppermute | solution.py:35
  268.2 0.8 copy-start.15
  277.5 0.8 copy-start.12
  277.5 1.0 copy-start.13
  278.5 0.8 copy-start.14

commit v4 on v3

--- a/solution.py
+++ b/solution.py
@@ -278,13 +278,11 @@
     sums = weight * sums.reshape(2, GROUP, rows) + jnp.where(here, FACTOR_DECAY * old_diagonals[:, None, :], 0.0)
     message = sums.reshape(2, GROUP, LAYERS, slim).transpose(2, 1, 0, 3).reshape(LAYERS * GROUP, 2 * slim)
     message = jnp.pad(message, ((0, 0), (0, 128 - 2 * slim)))
-    message, grad_rows, cross_blocks, shard, before, beyond = tied(
-        message, grad_rows, cross_blocks, acts, before, beyond
-    )
+    message, grad_rows, cross_blocks, shard = tied(message, grad_rows, cross_blocks, acts)
     other = across(shard)
     far = turned(before, 1)
     arrived = lax.all_to_all(message, LAYER + DP, 0, 0, tiled=True)
-    arrived, other, far = tied(arrived, other, far)
+    arrived, other, far, before, beyond = tied(arrived, other, far, before, beyond)
     diagonals = jnp.sum(arrived.reshape(LAYERS, GROUP, 128), axis=1)[:, : 2 * slim].reshape(LAYERS, 2, slim)
     coupling = diagonals[:, 1]
     pivots = DAMPING + diagonals[:, 0]
@@ -310,6 +308,7 @@
     )
     off = apply_blocks(order, gathered(initial), (factor_off, col_off, row_off), col_old)
     change_rows = chain_solve(change_kernel, "change", (grad_rows, initial_rows, by_layer(off)), coefficients)
+    change_rows, row_batch = tied(change_rows, row_batch)
     change = by_layer(change_rows).reshape(rows, outputs)
     update = initial.astype(F32) + change.astype(F32)
 
@@ -319,8 +318,7 @@
     moments_new = (moment * requant).astype(BF16)
     master_new = master[0] - STEP_SIZE * moment
     own = master_new.astype(BF16)
-    other, before, beyond, far = first_round(own)
-    other, row_batch = tied(other, row_batch)
+    other, before, beyond, far = tied(*first_round(own))
     cross_new = FACTOR_DECAY * cross_old + weight * along_layers(row_batch, -1).astype(F32)
     replicas = place_rows(order[:5], (own, before, beyond, other, far), None)
     replicas, cross_new = tied(replicas, cross_new)

time: 286 us -> 268 us (0.937)
  blocking collectives: 54.2 us -> 24 us
  starting transfers between devices: 72 us -> 84 us
  waiting for transfers between devices: 90.4 us -> 93.7 us
    all_to_all x1 -> x0, blocking collectives: 30.1 us -> none  [body(): arrived = lax.all_to_all(message, LAYER + DP, 0, 0, tiled=True)]
    all_to_all x0 -> x1, waiting for transfers between devices: none -> 16.1 us  [body(): arrived = lax.all_to_all(message, LAYER + DP, 0, 0, tiled=True)]
    ppermute x15, waiting for transfers between devices: 47.6 us -> 35 us  [turned(): lax.ppermute(value, 'dp_1', [(i, (i + steps) % TURN) for i in range(TURN)])]
    all_to_all x0 -> x1, starting transfers between devices: none -> 9.67 us  [body(): arrived = lax.all_to_all(message, LAYER + DP, 0, 0, tiled=True)]
    all_to_all x3, waiting for transfers between devices: 30.1 us -> 26.1 us  [by_layer(): return lax.all_to_all(value, LAYER, 0, 0)]
    ppermute x6, waiting for transfers between devices: 12.6 us -> 16.4 us  [across(): return lax.ppermute(value, 'dp_0', [(0, 1), (1, 0)])]
  transfers between devices with their start and end apart: 30 -> 31, of which waited for: 7 -> 10; matrix products, arithmetic and copies ran while one was open for 7% -> 8% of each run, Pallas kernels for 7% -> 7%
where the time goes in v4:
time: 268 us; the launch traced here: 267 us
  waiting for transfers between devices  93.7 us (35%)
  starting transfers between devices  84 us (31%)
  Pallas kernels  36 us (13%)
  blocking collectives  24 us (9%)
  other arithmetic  15.5 us (6%)
  local copies, waits for them, and re-layouts  13 us (5%)
    ppermute x15, waiting for transfers between devices, turned(): lax.ppermute(value, 'dp_1', [(i, (i + steps) % TURN) for i in range(TURN)])  35 us
    all_to_all x3, waiting for transfers between devices, by_layer(): return lax.all_to_all(value, LAYER, 0, 0)  26.1 us
    all_to_all x1, blocking collectives, by_layer(): return lax.all_to_all(value, LAYER, 0, 0)  24 us
    ppermute x15, starting transfers between devices, turned(): lax.ppermute(value, 'dp_1', [(i, (i + steps) % TURN) for i in range(TURN)])  21.4 us
    ppermute x5, starting transfers between devices, along_layers(): return lax.ppermute(value, LAYER, pairs)  18.7 us
    ppermute x6, waiting for transfers between devices, across(): return lax.ppermute(value, 'dp_0', [(0, 1), (1, 0)])  16.4 us
    all_to_all x1, waiting for transfers between devices, body(): arrived = lax.all_to_all(message, LAYER + DP, 0, 0, tiled=True)  16.1 us
    all_to_all x3, starting transfers between devices, by_layer(): return lax.all_to_all(value, LAYER, 0, 0)  14.6 us
  transfers between devices with their start and end apart: 31, of which 10 were waited for; matrix products, arithmetic and copies ran while one was open for 8% of the time, Pallas kernels for 7%

profile of v4, /device:TPU:6, one launch (start us, length us, event | category | flops | bytes accessed | tf_op | source)
XLA Modules:
  0.0 267.1 jit_solution(14660048471560495818)
XLA Ops:
  0.6 4.6 %collective-permute-start = (bf16[256,2048]{1,0:T(8,128)(2,1)}, bf16[256,2048]{1,0:T(8,128)(2,1)}, u32[]{:S(2)}, u32[]{:S(2)}) collective-permute-start(bf16[256,2048]{1,0:T(8,128)(2,1)} %bitcast.67), channel_id=1, source_target_pairs={{8,0},{16,8},{24,16},{32,24},{40,32},{48,40},{56,48},{64,56},{72,6... | collective-permute-start | bytes 3145736 | tf_op jit(solution)/shard_map/ppermute | solution.py:27
  5.3 2.0 collective-permute-start.2
  7.3 2.2 collective-permute-start.4
  9.5 3.7 %all-to-all-start = ((bf16[16,16,1024]{2,1,0:T(8,128)(2,1)}), bf16[16,16,1024]{2,1,0:T(8,128)(2,1)S(1)}, u32[]{:S(2)}, u32[]{:S(2)}) async-start(bf16[16,16,1024]{2,1,0:T(8,128)(2,1)} %bitcast.86), calls=%async_computation | async-start | bytes 1048576 | tf_op jit(solution)/shard_map/all_to_all | solution.py:251
  14.4 2.7 %convert_element_type.50 = bf16[1,256,2048]{2,1,0:T(8,128)(2,1)} convert(f32[1,256,2048]{2,1,0:T(8,128)} %param.10) | non-fusion elementwise | flops 524288 | bytes 3145728 | tf_op jit(solution)/shard_map/convert_element_type | solution.py:271
  17.1 2.3 copy.22
  19.5 2.3 copy.23
  21.8 1.7 fusion
  24.6 1.4 collective-permute-start.1
  26.0 4.7 %collective-permute-done.2.refs_1_.refs_2_ = bf16[256,2048]{1,0:T(8,128)(2,1)S(1)} collective-permute-done((bf16[256,2048]{1,0:T(8,128)(2,1)}, bf16[256,2048]{1,0:T(8,128)(2,1)S(1)}, u32[]{:S(2)}, u32[]{:S(2)}) %collective-permute-start.2) | collective-permute-done | bytes 1048608 | tf_op jit(solution)/shard_map/ppermute | solution.py:31
  30.7 9.7 %all-to-all-start.1 = ((f32[128,1,128]{2,1,0:T(1,128)}), f32[128,1,128]{2,1,0:T(1,128)S(1)}, u32[]{:S(2)}, u32[]{:S(2)}) async-start(f32[128,1,128]{2,1,0:T(1,128)} %bitcast.10), calls=%async_computation.1 | async-start | bytes 131072 | tf_op jit(solution)/shard_map/all_to_all | solution.py:284
  40.4 16.1 %all-to-all-done.1 = f32[128,1,128]{2,1,0:T(1,128)S(1)} async-done(((f32[128,1,128]{2,1,0:T(1,128)}), f32[128,1,128]{2,1,0:T(1,128)S(1)}, u32[]{:S(2)}, u32[]{:S(2)}) %all-to-all-start.1) | async-done | bytes 65568 | tf_op jit(solution)/shard_map/all_to_all | solution.py:284
  57.0 1.1 first_solution.1.initial
  59.0 2.3 collective-permute-start.6
  61.4 3.2 %collective-permute-start.7 = (bf16[256,2048]{1,0:T(8,128)(2,1)}, bf16[256,2048]{1,0:T(8,128)(2,1)}, u32[]{:S(2)}, u32[]{:S(2)}) collective-permute-start(bf16[256,2048]{1,0:T(8,128)(2,1)} %collective-permute-done.3.refs_4_.refs_5_), channel_id=1, source_target_pairs={{0,4},{4,0},{1,5},{5,1},{2,6},{6,2},{3,7},{7,3},{8,12},{12,8},{9,1... | collective-permute-start | bytes 3145736 | tf_op jit(solution)/shard_map/ppermute | solution.py:35
  65.2 6.0 %all-to-all-start.2 = ((bf16[16,16,1024]{2,1,0:T(8,128)(2,1)}), bf16[16,16,1024]{2,1,0:T(8,128)(2,1)S(1)}, u32[]{:S(2)}, u32[]{:S(2)}) async-start(bf16[16,16,1024]{2,1,0:T(8,128)(2,1)} %first_solution.1.initial), calls=%async_computation.2 | async-start | bytes 1048576 | tf_op jit(solution)/shard_map/all_to_all | solution.py:251
  71.2 2.7 %convert_bitcast_fusion = bf16[256,2048]{1,0:T(8,128)(2,1)} fusion(f32[1,256,2048]{2,1,0:T(8,128)} %param.10), kind=kLoop, calls=%fused_computation.37 | loop fusion | flops 524288 | bytes 3145728 | tf_op jit(solution)/shard_map/convert_element_type | solution.py:271
  73.9 21.0 %all-to-all-done.2 = bf16[16,16,1024]{2,1,0:T(8,128)(2,1)S(1)} async-done(((bf16[16,16,1024]{2,1,0:T(8,128)(2,1)}), bf16[16,16,1024]{2,1,0:T(8,128)(2,1)S(1)}, u32[]{:S(2)}, u32[]{:S(2)}) %all-to-all-start.2) | async-done | bytes 524320 | tf_op jit(solution)/shard_map/all_to_all | solution.py:251
  94.9 3.5 %collective-permute-start.11 = (bf16[256,1024]{1,0:T(8,128)(2,1)S(1)}, bf16[256,1024]{1,0:T(8,128)(2,1)S(1)}, u32[]{:S(2)}, u32[]{:S(2)}) collective-permute-start(bf16[256,1024]{1,0:T(8,128)(2,1)S(1)} %bitcast.73), channel_id=1, source_target_pairs={{0,4},{4,0},{1,5},{5,1},{2,6},{6,2},{3,7},{7,3},{8,12},{12,8},{9,1... | collective-permute-start | bytes 1572872 | tf_op jit(solution)/shard_map/ppermute | solution.py:35
  98.4 3.0 %own_columns.1.refs_9_ = bf16[8,256,256]{2,1,0:T(8,128)(2,1)} custom-call(s32[8]{0:T(128)} %fusion.9.order.refs_0_, bf16[256,2048]{1,0:T(8,128)(2,1)} %bitcast.70, bf16[256,2048]{1,0:T(8,128)(2,1)} %copy-done.9, bf16[256,2048]{1,0:T(8,128)(2,1)} %collective-permute-done.4.refs_2_.refs_3_, bf16[256,2048]{1,0:T(8,128)(2,1)} %collective-permute-done.1.refs_3_.refs_4_, ...), custom_call_target="tpu_custom_call" | custom-call | tf_op jit(solution)/shard_map/own_columns/pallas_call | solution.py:73
  101.4 2.0 collective-permute-start.8
  103.5 5.8 %collective-permute-start.9 = (bf16[8,256,256]{2,1,0:T(8,128)(2,1)}, bf16[8,256,256]{2,1,0:T(8,128)(2,1)}, u32[]{:S(2)}, u32[]{:S(2)}) collective-permute-start(bf16[8,256,256]{2,1,0:T(8,128)(2,1)} %own_columns.1.refs_9_), channel_id=1, source_target_pairs={{8,0},{16,8},{24,16},{32,24},{40,32},{48,40},{56,48},{64,56},{72,6... | collective-permute-start | bytes 3145736 | tf_op jit(solution)/shard_map/ppermute | solution.py:27
  109.2 3.3 %collective-permute-start.13 = (bf16[256,1024]{1,0:T(8,128)(2,1)S(1)}, bf16[256,1024]{1,0:T(8,128)(2,1)}, u32[]{:S(2)}, u32[]{:S(2)}) collective-permute-start(bf16[256,1024]{1,0:T(8,128)(2,1)S(1)} %bitcast.75), channel_id=1, source_target_pairs={{0,3},{1,0},{2,1},{3,2},{4,7},{5,4},{6,5},{7,6},{8,11},{9,8},{10,9... | collective-permute-start | bytes 1572872 | tf_op jit(solution)/shard_map/ppermute | solution.py:31
  112.6 1.9 collective-permute-start.10
  114.5 7.8 %all-to-all-start.3 = ((bf16[8,256,256]{2,1,0:T(8,128)(2,1)}), bf16[8,256,256]{2,1,0:T(8,128)(2,1)}, u32[]{:S(2)}, u32[]{:S(2)}) async-start(bf16[8,256,256]{2,1,0:T(8,128)(2,1)} %bitcast.81), calls=%async_computation.3 | async-start | bytes 2097152 | tf_op jit(solution)/shard_map/all_to_all | solution.py:305
  122.3 19.6 %collective-permute-done.13.refs_2_ = bf16[256,1024]{1,0:T(8,128)(2,1)} collective-permute-done((bf16[256,1024]{1,0:T(8,128)(2,1)S(1)}, bf16[256,1024]{1,0:T(8,128)(2,1)}, u32[]{:S(2)}, u32[]{:S(2)}) %collective-permute-start.13) | collective-permute-done | bytes 524320 | tf_op jit(solution)/shard_map/ppermute | solution.py:31
  141.8 1.4 collective-permute-start.15
  143.2 2.4 collective-permute-start.16
  145.8 11.9 %refresh.1 = (f32[256,2048]{1,0:T(8,128)}, bf16[256,2048]{1,0:T(8,128)(2,1)S(1)}, bf16[256,2048]{1,0:T(8,128)(2,1)S(1)}, bf16[256,2048]{1,0:T(8,128)(2,1)S(1)}, bf16[256,2048]{1,0:T(8,128)(2,1)S(1)}) custom-call(s32[8]{0:T(128)S(1)} %copy-done.6, bf16[256,2048]{1,0:T(8,128)(2,1)S(1)} %bitcast.72, bf16[256,2048]{1,0:T(8,128)(2,1)} %copy-done.9, ...), custom_call_target="tpu_custom_call" | custom-call | tf_op jit(solution)/shard_map/refresh/pallas_call | solution.py:112
  161.7 1.2 copy-done.3
  162.9 8.6 %apply_blocks.1 = bf16[16,48,1024]{2,1,0:T(8,128)(2,1)} custom-call(s32[8]{0:T(128)S(1)} %copy-done.6, bf16[256,1024]{1,0:T(8,128)(2,1)S(1)} %bitcast.77, bf16[256,1024]{1,0:T(8,128)(2,1)} %collective-permute-done.12.refs_1_, bf16[256,1024]{1,0:T(8,128)(2,1)} %collective-permute-done.13.refs_2_, bf16[256,1024]{1,0:T(8,128)(2,1)S(1)} %collective-permute-done.11.refs_3_, ...), custom_call_target="tpu_custom_call" | custom-call | tf_op jit(solution)/shard_map/apply_blocks/pallas_call | solution.py:180
  171.5 24.0 %all_to_all.37.off = bf16[16,48,1024]{2,1,0:T(8,128)(2,1)S(1)} all-to-all(bf16[16,48,1024]{2,1,0:T(8,128)(2,1)} %apply_blocks.1), channel_id=1, replica_groups=mesh['layer_0'=2,'layer_1'=4,'layer_2'=2,'dp_0'=2,'dp_1'=4] {'layer_0','..., dimensions={0} | all-to-all | bytes 3145728 | tf_op jit(solution)/shard_map/all_to_all | solution.py:251
  195.6 2.7 %change.1 = bf16[16,16,1024]{2,1,0:T(8,128)(2,1)} custom-call(bf16[16,16,1024]{2,1,0:T(8,128)(2,1)S(1)} %all-to-all-done.grad, bf16[16,16,1024]{2,1,0:T(8,128)(2,1)} %first_solution.1.initial, bf16[16,48,1024]{2,1,0:T(8,128)(2,1)S(1)} %all_to_all.37.off, f32[16,16,128]{2,1,0:T(8,128)S(1)} %broadcast_in_dim.77.pivots, ...), custom_call_target="tpu_custom_call" | custom-call | tf_op jit(solution)/shard_map/change/pallas_call | solution.py:242
  198.3 4.9 %all-to-all-start.5 = ((bf16[16,16,1024]{2,1,0:T(8,128)(2,1)}), bf16[16,16,1024]{2,1,0:T(8,128)(2,1)S(1)}, u32[]{:S(2)}, u32[]{:S(2)}) async-start(bf16[16,16,1024]{2,1,0:T(8,128)(2,1)} %change.1), calls=%async_computation.5 | async-start | bytes 1048576 | tf_op jit(solution)/shard_map/all_to_all | solution.py:251
  203.2 4.3 %collective-permute-start.22 = (bf16[256,2048]{1,0:T(8,128)(2,1)S(1)}, bf16[256,2048]{1,0:T(8,128)(2,1)}, u32[]{:S(2)}, u32[]{:S(2)}) collective-permute-start(bf16[256,2048]{1,0:T(8,128)(2,1)S(1)} %copy-done.8), channel_id=1, source_target_pairs={{8,0},{16,8},{24,16},{32,24},{40,32},{48,40},{56,48},{64,56},{72,6... | collective-permute-start | bytes 3145736 | tf_op jit(solution)/shard_map/ppermute | solution.py:27
  207.6 5.1 %all-to-all-done.5 = bf16[16,16,1024]{2,1,0:T(8,128)(2,1)S(1)} async-done(((bf16[16,16,1024]{2,1,0:T(8,128)(2,1)}), bf16[16,16,1024]{2,1,0:T(8,128)(2,1)S(1)}, u32[]{:S(2)}, u32[]{:S(2)}) %all-to-all-start.5) | async-done | bytes 524320 | tf_op jit(solution)/shard_map/all_to_all | solution.py:251
  212.7 3.0 %fusion.12 = (bf16[256,1024]{1,0:T(8,128)(2,1)S(1)}, f32[256,1024]{1,0:T(8,128)}, bf16[1,256,1024]{2,1,0:T(8,128)(2,1)}) fusion(bf16[16,16,1024]{2,1,0:T(8,128)(2,1)S(1)} %all-to-all-done.5, bf16[256,1024]{1,0:T(8,128)(2,1)S(1)} %bitcast.78, f32[256]{0:T(256)S(1)} %get-tuple-element.91, bf16[1,256,1024]{2,1,0:T(8,128)(2,1)} %param.12, ...), kind=kLoop, calls=%fused_computation.35 | loop fusion | flops 3145728 | bytes 4720640 | tf_op jit(solution)/shard_map/convert_element_type | solution.py:320
  215.7 3.3 %collective-permute-start.18 = (bf16[256,1024]{1,0:T(8,128)(2,1)S(1)}, bf16[256,1024]{1,0:T(8,128)(2,1)}, u32[]{:S(2)}, u32[]{:S(2)}) collective-permute-start(bf16[256,1024]{1,0:T(8,128)(2,1)S(1)} %get-tuple-element.79.refs_0_), channel_id=1, source_target_pairs={{0,4},{4,0},{1,5},{5,1},{2,6},{6,2},{3,7},{7,3},{8,12},{12,8},{9,1... | collective-permute-start | bytes 1572872 | tf_op jit(solution)/shard_map/ppermute | solution.py:35
  219.0 3.2 %collective-permute-start.20 = (bf16[256,1024]{1,0:T(8,128)(2,1)S(1)}, bf16[256,1024]{1,0:T(8,128)(2,1)S(1)}, u32[]{:S(2)}, u32[]{:S(2)}) collective-permute-start(bf16[256,1024]{1,0:T(8,128)(2,1)S(1)} %get-tuple-element.79.refs_0_), channel_id=1, source_target_pairs={{0,3},{1,0},{2,1},{3,2},{4,7},{5,4},{6,5},{7,6},{8,11},{9,8},{10,9... | collective-permute-start | bytes 1572872 | tf_op jit(solution)/shard_map/ppermute | solution.py:31
  223.1 13.5 %collective-permute-done.18.refs_3_ = bf16[256,1024]{1,0:T(8,128)(2,1)} collective-permute-done((bf16[256,1024]{1,0:T(8,128)(2,1)S(1)}, bf16[256,1024]{1,0:T(8,128)(2,1)}, u32[]{:S(2)}, u32[]{:S(2)}) %collective-permute-start.18) | collective-permute-done | bytes 524320 | tf_op jit(solution)/shard_map/ppermute | solution.py:35
  236.6 7.8 %collective-permute-done.20.refs_2_ = bf16[256,1024]{1,0:T(8,128)(2,1)S(1)} collective-permute-done((bf16[256,1024]{1,0:T(8,128)(2,1)S(1)}, bf16[256,1024]{1,0:T(8,128)(2,1)S(1)}, u32[]{:S(2)}, u32[]{:S(2)}) %collective-permute-start.20) | collective-permute-done | bytes 524320 | tf_op jit(solution)/shard_map/ppermute | solution.py:31
  245.4 1.1 collective-permute-start.23
  246.6 2.3 collective-permute-start.24
  249.1 4.9 %place_rows.2.refs_3_ = bf16[2048,1024]{1,0:T(8,128)(2,1)} custom-call(s32[5]{0:T(128)} %bitcast.79, bf16[256,1024]{1,0:T(8,128)(2,1)} %copy-done.10, bf16[256,1024]{1,0:T(8,128)(2,1)} %copy-done.14, bf16[256,1024]{1,0:T(8,128)(2,1)} %copy-done.15, bf16[256,1024]{1,0:T(8,128)(2,1)} %collective-permute-done.18.refs_3_, ...), custom_call_target="tpu_custom_call" | custom-call | tf_op jit(solution)/shard_map/place_rows/pallas_call | solution.py:139
  254.0 3.7 %bitcast_add_fusion = f32[256,2048]{1,0:T(8,128)} fusion(bf16[256,2048]{1,0:T(8,128)(2,1)} %collective-permute-done.22, f32[1,256,2048]{2,1,0:T(8,128)} %param.10), kind=kLoop, calls=%fused_computation.4 | loop fusion | flops 2097152 | bytes 5242880 | tf_op jit(solution)/shard_map/add | solution.py:322
  257.7 1.9 collective-permute-done.23.refs_0_
  259.6 3.0 %collective-permute-done.25.refs_2_ = bf16[256,1024]{1,0:T(8,128)(2,1)S(1)} collective-permute-done((bf16[256,1024]{1,0:T(8,128)(2,1)}, bf16[256,1024]{1,0:T(8,128)(2,1)S(1)}, u32[]{:S(2)}, u32[]{:S(2)}) %collective-permute-start.25) | collective-permute-done | bytes 524320 | tf_op jit(solution)/shard_map/ppermute | solution.py:35
  263.4 3.7 %place_rows.3 = bf16[2048,1024]{1,0:T(8,128)(2,1)} custom-call(s32[3]{0:T(128)} %slice.19.order, bf16[256,1024]{1,0:T(8,128)(2,1)} %copy-done.11, bf16[256,1024]{1,0:T(8,128)(2,1)} %copy-done.12, bf16[256,1024]{1,0:T(8,128)(2,1)} %copy-done.13, bf16[2048,1024]{1,0:T(8,128)(2,1)} %place_rows.2.refs_3_), custom_call_target="tpu_custom_call", output_to_operand_aliasing={{}: (4, {})} | custom-call | tf_op jit(solution)/shard_map/place_rows/pallas_call | solution.py:139
  (90 shorter events, 11.7 us)
Async XLA Ops:
  0.6 21.1 %collective-permute-start = (bf16[256,2048]{1,0:T(8,128)(2,1)}, bf16[256,2048]{1,0:T(8,128)(2,1)}, u32[]{:S(2)}, u32[]{:S(2)}) collective-permute-start(bf16[256,2048]{1,0:T(8,128)(2,1)} %bitcast.67), channel_id=1, source_target_pairs={{8,0},{16,8},{24,16},{32,24},{40,32},{48,40},{56,48},{64,56},{72,6... | collective-permute-start | bytes 3145736 | tf_op jit(solution)/shard_map/ppermute | solution.py:27
  5.3 25.4 %collective-permute-start.2 = (bf16[256,2048]{1,0:T(8,128)(2,1)}, bf16[256,2048]{1,0:T(8,128)(2,1)S(1)}, u32[]{:S(2)}, u32[]{:S(2)}) collective-permute-start(bf16[256,2048]{1,0:T(8,128)(2,1)} %bitcast.68), channel_id=1, source_target_pairs={{0,1},{1,2},{2,3},{3,0},{4,5},{5,6},{6,7},{7,4},{8,9},{9,10},{10,1... | collective-permute-start | bytes 3145736 | tf_op jit(solution)/shard_map/ppermute | solution.py:31
  7.3 33.1 %collective-permute-start.4 = (bf16[256,2048]{1,0:T(8,128)(2,1)}, bf16[256,2048]{1,0:T(8,128)(2,1)}, u32[]{:S(2)}, u32[]{:S(2)}) collective-permute-start(bf16[256,2048]{1,0:T(8,128)(2,1)} %bitcast.69), channel_id=1, source_target_pairs={{0,3},{1,0},{2,1},{3,2},{4,7},{5,4},{6,5},{7,6},{8,11},{9,8},{10,9... | collective-permute-start | bytes 3145736 | tf_op jit(solution)/shard_map/ppermute | solution.py:31
  9.5 15.2 %all-to-all-start = ((bf16[16,16,1024]{2,1,0:T(8,128)(2,1)}), bf16[16,16,1024]{2,1,0:T(8,128)(2,1)S(1)}, u32[]{:S(2)}, u32[]{:S(2)}) async-start(bf16[16,16,1024]{2,1,0:T(8,128)(2,1)} %bitcast.86), calls=%async_computation | async-start | bytes 1048576 | tf_op jit(solution)/shard_map/all_to_all | solution.py:251
  17.1 4.6 %copy-start = (bf16[1,256,2048]{2,1,0:T(8,128)(2,1)S(1)}, bf16[1,256,2048]{2,1,0:T(8,128)(2,1)}, u32[]{:S(2)}) copy-start(bf16[1,256,2048]{2,1,0:T(8,128)(2,1)} %param.8) | copy-start | bytes 3145732
  23.5 41.2 %copy-start.16 = (s32[8]{0:T(128)S(1)}, s32[8]{0:T(128)}, u32[]{:S(2)}) copy-start(s32[8]{0:T(128)} %constant.57.clone) | copy-start | bytes 100
  24.6 31.9 %collective-permute-start.1 = (bf16[256,2048]{1,0:T(8,128)(2,1)S(1)}, bf16[256,2048]{1,0:T(8,128)(2,1)}, u32[]{:S(2)}, u32[]{:S(2)}) collective-permute-start(bf16[256,2048]{1,0:T(8,128)(2,1)S(1)} %bitcast.71), channel_id=1, source_target_pairs={{0,4},{4,0},{1,5},{5,1},{2,6},{6,2},{3,7},{7,3},{8,12},{12,8},{9,1... | collective-permute-start | bytes 3145736 | tf_op jit(solution)/shard_map/ppermute | solution.py:35
  30.7 43.2 %copy-start.9 = (bf16[256,2048]{1,0:T(8,128)(2,1)}, bf16[256,2048]{1,0:T(8,128)(2,1)S(1)}, u32[]{:S(2)}) copy-start(bf16[256,2048]{1,0:T(8,128)(2,1)S(1)} %collective-permute-done.2.refs_1_.refs_2_) | copy-start | bytes 3145732
  30.7 25.8 %collective-permute-start.3 = (bf16[256,2048]{1,0:T(8,128)(2,1)S(1)}, bf16[256,2048]{1,0:T(8,128)(2,1)}, u32[]{:S(2)}, u32[]{:S(2)}) collective-permute-start(bf16[256,2048]{1,0:T(8,128)(2,1)S(1)} %collective-permute-done.2.refs_1_.refs_2_), channel_id=1, source_target_pairs={{0,1},{1,2},{2,3},{3,0},{4,5},{5,6},{6,7},{7,4},{8,9},{9,10},{10,1... | collective-permute-start | bytes 3145736 | tf_op jit(solution)/shard_map/ppermute | solution.py:31
  30.7 25.8 %all-to-all-start.1 = ((f32[128,1,128]{2,1,0:T(1,128)}), f32[128,1,128]{2,1,0:T(1,128)S(1)}, u32[]{:S(2)}, u32[]{:S(2)}) async-start(f32[128,1,128]{2,1,0:T(1,128)} %bitcast.10), calls=%async_computation.1 | async-start | bytes 131072 | tf_op jit(solution)/shard_map/all_to_all | solution.py:284
  58.1 36.7 %collective-permute-start.5 = (bf16[256,2048]{1,0:T(8,128)(2,1)}, bf16[256,2048]{1,0:T(8,128)(2,1)}, u32[]{:S(2)}, u32[]{:S(2)}) collective-permute-start(bf16[256,2048]{1,0:T(8,128)(2,1)} %collective-permute-done.1.refs_3_.refs_4_), channel_id=1, source_target_pairs={{0,1},{1,2},{2,3},{3,0},{4,5},{5,6},{6,7},{7,4},{8,9},{9,10},{10,1... | collective-permute-start | bytes 3145736 | tf_op jit(solution)/shard_map/ppermute | solution.py:31
  59.0 35.9 %collective-permute-start.6 = (bf16[256,2048]{1,0:T(8,128)(2,1)}, bf16[256,2048]{1,0:T(8,128)(2,1)}, u32[]{:S(2)}, u32[]{:S(2)}) collective-permute-start(bf16[256,2048]{1,0:T(8,128)(2,1)} %collective-permute-done.1.refs_3_.refs_4_), channel_id=1, source_target_pairs={{0,3},{1,0},{2,1},{3,2},{4,7},{5,4},{6,5},{7,6},{8,11},{9,8},{10,9... | collective-permute-start | bytes 3145736 | tf_op jit(solution)/shard_map/ppermute | solution.py:31
  61.4 33.5 %collective-permute-start.7 = (bf16[256,2048]{1,0:T(8,128)(2,1)}, bf16[256,2048]{1,0:T(8,128)(2,1)}, u32[]{:S(2)}, u32[]{:S(2)}) collective-permute-start(bf16[256,2048]{1,0:T(8,128)(2,1)} %collective-permute-done.3.refs_4_.refs_5_), channel_id=1, source_target_pairs={{0,4},{4,0},{1,5},{5,1},{2,6},{6,2},{3,7},{7,3},{8,12},{12,8},{9,1... | collective-permute-start | bytes 3145736 | tf_op jit(solution)/shard_map/ppermute | solution.py:35
  65.2 29.7 %all-to-all-start.2 = ((bf16[16,16,1024]{2,1,0:T(8,128)(2,1)}), bf16[16,16,1024]{2,1,0:T(8,128)(2,1)S(1)}, u32[]{:S(2)}, u32[]{:S(2)}) async-start(bf16[16,16,1024]{2,1,0:T(8,128)(2,1)} %first_solution.1.initial), calls=%async_computation.2 | async-start | bytes 1048576 | tf_op jit(solution)/shard_map/all_to_all | solution.py:251
  94.9 17.7 %collective-permute-start.11 = (bf16[256,1024]{1,0:T(8,128)(2,1)S(1)}, bf16[256,1024]{1,0:T(8,128)(2,1)S(1)}, u32[]{:S(2)}, u32[]{:S(2)}) collective-permute-start(bf16[256,1024]{1,0:T(8,128)(2,1)S(1)} %bitcast.73), channel_id=1, source_target_pairs={{0,4},{4,0},{1,5},{5,1},{2,6},{6,2},{3,7},{7,3},{8,12},{12,8},{9,1... | collective-permute-start | bytes 1572872 | tf_op jit(solution)/shard_map/ppermute | solution.py:35
  98.4 14.1 %collective-permute-start.12 = (bf16[256,1024]{1,0:T(8,128)(2,1)S(1)}, bf16[256,1024]{1,0:T(8,128)(2,1)}, u32[]{:S(2)}, u32[]{:S(2)}) collective-permute-start(bf16[256,1024]{1,0:T(8,128)(2,1)S(1)} %bitcast.74), channel_id=1, source_target_pairs={{0,1},{1,2},{2,3},{3,0},{4,5},{5,6},{6,7},{7,4},{8,9},{9,10},{10,1... | collective-permute-start | bytes 1572872 | tf_op jit(solution)/shard_map/ppermute | solution.py:31
  101.4 44.4 %copy-start.1 = (bf16[1,256,2048]{2,1,0:T(8,128)(2,1)S(1)}, bf16[1,256,2048]{2,1,0:T(8,128)(2,1)}, u32[]{:S(2)}) copy-start(bf16[1,256,2048]{2,1,0:T(8,128)(2,1)} %param.8) | copy-start | bytes 3145732
  101.4 44.4 %copy-start.6 = (s32[8]{0:T(128)S(1)}, s32[8]{0:T(128)}, u32[]{:S(2)}) copy-start(s32[8]{0:T(128)} %fusion.9.order.refs_0_) | copy-start | bytes 100
  101.4 44.2 %collective-permute-start.8 = (bf16[8,256,256]{2,1,0:T(8,128)(2,1)}, bf16[8,256,256]{2,1,0:T(8,128)(2,1)}, u32[]{:S(2)}, u32[]{:S(2)}) collective-permute-start(bf16[8,256,256]{2,1,0:T(8,128)(2,1)} %own_columns.1.refs_9_), channel_id=1, source_target_pairs={{0,8},{8,16},{16,24},{24,32},{32,40},{40,48},{48,56},{56,64},{64,7... | collective-permute-start | bytes 3145736 | tf_op jit(solution)/shard_map/ppermute | solution.py:27
  103.5 42.3 %collective-permute-start.9 = (bf16[8,256,256]{2,1,0:T(8,128)(2,1)}, bf16[8,256,256]{2,1,0:T(8,128)(2,1)}, u32[]{:S(2)}, u32[]{:S(2)}) collective-permute-start(bf16[8,256,256]{2,1,0:T(8,128)(2,1)} %own_columns.1.refs_9_), channel_id=1, source_target_pairs={{8,0},{16,8},{24,16},{32,24},{40,32},{48,40},{56,48},{64,56},{72,6... | collective-permute-start | bytes 3145736 | tf_op jit(solution)/shard_map/ppermute | solution.py:27
  109.2 32.6 %collective-permute-start.13 = (bf16[256,1024]{1,0:T(8,128)(2,1)S(1)}, bf16[256,1024]{1,0:T(8,128)(2,1)}, u32[]{:S(2)}, u32[]{:S(2)}) collective-permute-start(bf16[256,1024]{1,0:T(8,128)(2,1)S(1)} %bitcast.75), channel_id=1, source_target_pairs={{0,3},{1,0},{2,1},{3,2},{4,7},{5,4},{6,5},{7,6},{8,11},{9,8},{10,9... | collective-permute-start | bytes 1572872 | tf_op jit(solution)/shard_map/ppermute | solution.py:31
  112.5 29.3 %collective-permute-start.14 = (bf16[256,1024]{1,0:T(8,128)(2,1)S(1)}, bf16[256,1024]{1,0:T(8,128)(2,1)}, u32[]{:S(2)}, u32[]{:S(2)}) collective-permute-start(bf16[256,1024]{1,0:T(8,128)(2,1)S(1)} %bitcast.76), channel_id=1, source_target_pairs={{0,2},{1,3},{2,0},{3,1},{4,6},{5,7},{6,4},{7,5},{8,10},{9,11},{10,... | collective-permute-start | bytes 1572872 | tf_op jit(solution)/shard_map/ppermute | solution.py:31
  112.6 33.3 %collective-permute-start.10 = (bf16[256,2048]{1,0:T(8,128)(2,1)}, bf16[256,2048]{1,0:T(8,128)(2,1)}, u32[]{:S(2)}, u32[]{:S(2)}) collective-permute-start(bf16[256,2048]{1,0:T(8,128)(2,1)} %convert_bitcast_fusion), channel_id=1, source_target_pairs={{0,8},{8,16},{16,24},{24,32},{32,40},{40,48},{48,56},{56,64},{64,7... | collective-permute-start | bytes 3145736 | tf_op jit(solution)/shard_map/ppermute | solution.py:27
  114.5 47.1 %all-to-all-start.3 = ((bf16[8,256,256]{2,1,0:T(8,128)(2,1)}), bf16[8,256,256]{2,1,0:T(8,128)(2,1)}, u32[]{:S(2)}, u32[]{:S(2)}) async-start(bf16[8,256,256]{2,1,0:T(8,128)(2,1)} %bitcast.81), calls=%async_computation.3 | async-start | bytes 2097152 | tf_op jit(solution)/shard_map/all_to_all | solution.py:305
  141.8 19.8 %collective-permute-start.15 = (bf16[256,1024]{1,0:T(8,128)(2,1)S(1)}, bf16[256,1024]{1,0:T(8,128)(2,1)}, u32[]{:S(2)}, u32[]{:S(2)}) collective-permute-start(bf16[256,1024]{1,0:T(8,128)(2,1)S(1)} %collective-permute-done.11.refs_3_), channel_id=1, source_target_pairs={{0,1},{1,2},{2,3},{3,0},{4,5},{5,6},{6,7},{7,4},{8,9},{9,10},{10,1... | collective-permute-start | bytes 1572872 | tf_op jit(solution)/shard_map/ppermute | solution.py:31
  143.2 18.4 %collective-permute-start.16 = (bf16[256,1024]{1,0:T(8,128)(2,1)S(1)}, bf16[256,1024]{1,0:T(8,128)(2,1)}, u32[]{:S(2)}, u32[]{:S(2)}) collective-permute-start(bf16[256,1024]{1,0:T(8,128)(2,1)S(1)} %collective-permute-done.11.refs_3_), channel_id=1, source_target_pairs={{0,3},{1,0},{2,1},{3,2},{4,7},{5,4},{6,5},{7,6},{8,11},{9,8},{10,9... | collective-permute-start | bytes 1572872 | tf_op jit(solution)/shard_map/ppermute | solution.py:31
  145.6 16.0 %collective-permute-start.17 = (bf16[256,1024]{1,0:T(8,128)(2,1)}, bf16[256,1024]{1,0:T(8,128)(2,1)}, u32[]{:S(2)}, u32[]{:S(2)}) collective-permute-start(bf16[256,1024]{1,0:T(8,128)(2,1)} %collective-permute-done.14.refs_4_), channel_id=1, source_target_pairs={{0,4},{4,0},{1,5},{5,1},{2,6},{6,2},{3,7},{7,3},{8,12},{12,8},{9,1... | collective-permute-start | bytes 1572872 | tf_op jit(solution)/shard_map/ppermute | solution.py:35
  157.7 1.0 copy-start.2
  158.7 1.0 copy-start.4
  159.7 1.0 copy-start.5
  160.7 1.0 copy-start.7
  161.7 1.2 copy-start.3
  195.6 7.6 %copy-start.17 = (s32[1,2]{1,0:T(1,128)S(1)}, s32[1,2]{1,0:T(1,128)}, u32[]{:S(2)}) copy-start(s32[1,2]{1,0:T(1,128)} %param.13) | copy-start | bytes 28
  195.6 7.6 %copy-start.8 = (bf16[256,2048]{1,0:T(8,128)(2,1)S(1)}, bf16[256,2048]{1,0:T(8,128)(2,1)}, u32[]{:S(2)}) copy-start(bf16[256,2048]{1,0:T(8,128)(2,1)} %copy-done.7) | copy-start | bytes 3145732
  198.3 14.4 %all-to-all-start.5 = ((bf16[16,16,1024]{2,1,0:T(8,128)(2,1)}), bf16[16,16,1024]{2,1,0:T(8,128)(2,1)S(1)}, u32[]{:S(2)}, u32[]{:S(2)}) async-start(bf16[16,16,1024]{2,1,0:T(8,128)(2,1)} %change.1), calls=%async_computation.5 | async-start | bytes 1048576 | tf_op jit(solution)/shard_map/all_to_all | solution.py:251
  203.2 50.8 %collective-permute-start.22 = (bf16[256,2048]{1,0:T(8,128)(2,1)S(1)}, bf16[256,2048]{1,0:T(8,128)(2,1)}, u32[]{:S(2)}, u32[]{:S(2)}) collective-permute-start(bf16[256,2048]{1,0:T(8,128)(2,1)S(1)} %copy-done.8), channel_id=1, source_target_pairs={{8,0},{16,8},{24,16},{32,24},{40,32},{48,40},{56,48},{64,56},{72,6... | collective-permute-start | bytes 3145736 | tf_op jit(solution)/shard_map/ppermute | solution.py:27
  215.7 33.5 %copy-start.10 = (bf16[256,1024]{1,0:T(8,128)(2,1)}, bf16[256,1024]{1,0:T(8,128)(2,1)S(1)}, u32[]{:S(2)}) copy-start(bf16[256,1024]{1,0:T(8,128)(2,1)S(1)} %get-tuple-element.79.refs_0_) | copy-start | bytes 1572868
  215.7 20.9 %collective-permute-start.18 = (bf16[256,1024]{1,0:T(8,128)(2,1)S(1)}, bf16[256,1024]{1,0:T(8,128)(2,1)}, u32[]{:S(2)}, u32[]{:S(2)}) collective-permute-start(bf16[256,1024]{1,0:T(8,128)(2,1)S(1)} %get-tuple-element.79.refs_0_), channel_id=1, source_target_pairs={{0,4},{4,0},{1,5},{5,1},{2,6},{6,2},{3,7},{7,3},{8,12},{12,8},{9,1... | collective-permute-start | bytes 1572872 | tf_op jit(solution)/shard_map/ppermute | solution.py:35
  219.0 17.6 %collective-permute-start.19 = (bf16[256,1024]{1,0:T(8,128)(2,1)S(1)}, bf16[256,1024]{1,0:T(8,128)(2,1)S(1)}, u32[]{:S(2)}, u32[]{:S(2)}) collective-permute-start(bf16[256,1024]{1,0:T(8,128)(2,1)S(1)} %get-tuple-element.79.refs_0_), channel_id=1, source_target_pairs={{0,1},{1,2},{2,3},{3,0},{4,5},{5,6},{6,7},{7,4},{8,9},{9,10},{10,1... | collective-permute-start | bytes 1572872 | tf_op jit(solution)/shard_map/ppermute | solution.py:31
  219.0 25.3 %collective-permute-start.20 = (bf16[256,1024]{1,0:T(8,128)(2,1)S(1)}, bf16[256,1024]{1,0:T(8,128)(2,1)S(1)}, u32[]{:S(2)}, u32[]{:S(2)}) collective-permute-start(bf16[256,1024]{1,0:T(8,128)(2,1)S(1)} %get-tuple-element.79.refs_0_), channel_id=1, source_target_pairs={{0,3},{1,0},{2,1},{3,2},{4,7},{5,4},{6,5},{7,6},{8,11},{9,8},{10,9... | collective-permute-start | bytes 1572872 | tf_op jit(solution)/shard_map/ppermute | solution.py:31
  222.2 23.2 %collective-permute-start.21 = (bf16[256,1024]{1,0:T(8,128)(2,1)S(1)}, bf16[256,1024]{1,0:T(8,128)(2,1)}, u32[]{:S(2)}, u32[]{:S(2)}) collective-permute-start(bf16[256,1024]{1,0:T(8,128)(2,1)S(1)} %get-tuple-element.79.refs_0_), channel_id=1, source_target_pairs={{0,2},{1,3},{2,0},{3,1},{4,6},{5,7},{6,4},{7,5},{8,10},{9,11},{10,... | collective-permute-start | bytes 1572872 | tf_op jit(solution)/shard_map/ppermute | solution.py:31
  236.6 7.8 %copy-start.14 = (bf16[256,1024]{1,0:T(8,128)(2,1)}, bf16[256,1024]{1,0:T(8,128)(2,1)S(1)}, u32[]{:S(2)}) copy-start(bf16[256,1024]{1,0:T(8,128)(2,1)S(1)} %collective-permute-done.19.refs_1_) | copy-start | bytes 1572868
  244.3 2.2 copy-start.15
  245.4 14.2 %collective-permute-start.23 = (bf16[256,1024]{1,0:T(8,128)(2,1)}, bf16[256,1024]{1,0:T(8,128)(2,1)S(1)}, u32[]{:S(2)}, u32[]{:S(2)}) collective-permute-start(bf16[256,1024]{1,0:T(8,128)(2,1)} %collective-permute-done.18.refs_3_), channel_id=1, source_target_pairs={{0,1},{1,2},{2,3},{3,0},{4,5},{5,6},{6,7},{7,4},{8,9},{9,10},{10,1... | collective-permute-start | bytes 1572872 | tf_op jit(solution)/shard_map/ppermute | solution.py:31
  246.6 13.0 %collective-permute-start.24 = (bf16[256,1024]{1,0:T(8,128)(2,1)}, bf16[256,1024]{1,0:T(8,128)(2,1)S(1)}, u32[]{:S(2)}, u32[]{:S(2)}) collective-permute-start(bf16[256,1024]{1,0:T(8,128)(2,1)} %collective-permute-done.18.refs_3_), channel_id=1, source_target_pairs={{0,3},{1,0},{2,1},{3,2},{4,7},{5,4},{6,5},{7,6},{8,11},{9,8},{10,9... | collective-permute-start | bytes 1572872 | tf_op jit(solution)/shard_map/ppermute | solution.py:31
  248.8 13.7 %collective-permute-start.25 = (bf16[256,1024]{1,0:T(8,128)(2,1)}, bf16[256,1024]{1,0:T(8,128)(2,1)S(1)}, u32[]{:S(2)}, u32[]{:S(2)}) collective-permute-start(bf16[256,1024]{1,0:T(8,128)(2,1)} %collective-permute-done.21.refs_4_), channel_id=1, source_target_pairs={{0,4},{4,0},{1,5},{5,1},{2,6},{6,2},{3,7},{7,3},{8,12},{12,8},{9,1... | collective-permute-start | bytes 1572872 | tf_op jit(solution)/shard_map/ppermute | solution.py:35
  259.6 3.0 %copy-start.11 = (bf16[256,1024]{1,0:T(8,128)(2,1)}, bf16[256,1024]{1,0:T(8,128)(2,1)S(1)}, u32[]{:S(2)}) copy-start(bf16[256,1024]{1,0:T(8,128)(2,1)S(1)} %collective-permute-done.23.refs_0_) | copy-start | bytes 1572868
  259.6 3.0 %copy-start.12 = (bf16[256,1024]{1,0:T(8,128)(2,1)}, bf16[256,1024]{1,0:T(8,128)(2,1)S(1)}, u32[]{:S(2)}) copy-start(bf16[256,1024]{1,0:T(8,128)(2,1)S(1)} %collective-permute-done.24.refs_1_) | copy-start | bytes 1572868
  (1 other events, 0.8 us)

commit v5 on v4

--- a/solution.py
+++ b/solution.py
@@ -120,7 +120,7 @@
             out_specs=[column] * len(kinds),
         ),
         out_shape=[jax.ShapeDtypeStruct((rows, features), kind) for kind in kinds],
-        compiler_params=pltpu.CompilerParams(vmem_limit_bytes=48 * 2**20),
+        compiler_params=pltpu.CompilerParams(vmem_limit_bytes=60 * 2**20),
         name="refresh",
     )(order, *pieces, *columns, factor_old, row_old)
 
@@ -189,7 +189,7 @@
             scratch_shapes=[pltpu.VMEM((features, tile), BF16)],
         ),
         out_shape=jax.ShapeDtypeStruct((LAYERS, 3 * slim, outputs), BF16),
-        compiler_params=pltpu.CompilerParams(vmem_limit_bytes=48 * 2**20),
+        compiler_params=pltpu.CompilerParams(vmem_limit_bytes=60 * 2**20),
         name="apply_blocks",
     )(order, *pieces, *matrices, col_old)
 

time: 268 us -> 265 us (0.989)
  local copies, waits for them, and re-layouts: 13 us -> 5.99 us
  waiting for transfers between devices: 93.7 us -> 99.3 us
  other arithmetic: 15.5 us -> 12.3 us
    unnamed x36 -> x18, local copies, waits for them, and re-layouts: 5.97 us -> 0.04 us
  transfers between devices with their start and end apart: 31 -> 31, of which waited for: 10 -> 12; matrix products, arithmetic and copies ran while one was open for 8% -> 7% of each run, Pallas kernels for 7% -> 8%
where the time goes in v5:
time: 265 us; the launch traced here: 263 us
  waiting for transfers between devices  99.3 us (37%)
  starting transfers between devices  83.3 us (31%)
  Pallas kernels  37.5 us (14%)
  blocking collectives  24 us (9%)
  other arithmetic  12.3 us (5%)
  local copies, waits for them, and re-layouts  5.99 us (2%)
    ppermute x15, waiting for transfers between devices, turned(): lax.ppermute(value, 'dp_1', [(i, (i + steps) % TURN) for i in range(TURN)])  37.4 us
    all_to_all x3, waiting for transfers between devices, by_layer(): return lax.all_to_all(value, LAYER, 0, 0)  27.8 us
    all_to_all x1, blocking collectives, by_layer(): return lax.all_to_all(value, LAYER, 0, 0)  24 us
    ppermute x15, starting transfers between devices, turned(): lax.ppermute(value, 'dp_1', [(i, (i + steps) % TURN) for i in range(TURN)])  21.3 us
    ppermute x5, starting transfers between devices, along_layers(): return lax.ppermute(value, LAYER, pairs)  18.5 us
    ppermute x6, waiting for transfers between devices, across(): return lax.ppermute(value, 'dp_0', [(0, 1), (1, 0)])  16.4 us
    all_to_all x1, waiting for transfers between devices, body(): arrived = lax.all_to_all(message, LAYER + DP, 0, 0, tiled=True)  16.2 us
    all_to_all x3, starting transfers between devices, by_layer(): return lax.all_to_all(value, LAYER, 0, 0)  14.6 us
  transfers between devices with their start and end apart: 31, of which 12 were waited for; matrix products, arithmetic and copies ran while one was open for 7% of the time, Pallas kernels for 8%

profile of v5, /device:TPU:6, one launch (start us, length us, event | category | flops | bytes accessed | tf_op | source)
XLA Modules:
  0.0 263.5 jit_solution(13648817297668021378)
XLA Ops:
  0.6 4.6 %collective-permute-start = (bf16[256,2048]{1,0:T(8,128)(2,1)}, bf16[256,2048]{1,0:T(8,128)(2,1)}, u32[]{:S(2)}, u32[]{:S(2)}) collective-permute-start(bf16[256,2048]{1,0:T(8,128)(2,1)} %bitcast.68), channel_id=1, source_target_pairs={{8,0},{16,8},{24,16},{32,24},{40,32},{48,40},{56,48},{64,56},{72,6... | collective-permute-start | bytes 3145736 | tf_op jit(solution)/shard_map/ppermute | solution.py:27
  5.3 2.0 collective-permute-start.2
  7.3 2.2 collective-permute-start.4
  9.5 3.7 %all-to-all-start = ((bf16[16,16,1024]{2,1,0:T(8,128)(2,1)}), bf16[16,16,1024]{2,1,0:T(8,128)(2,1)S(1)}, u32[]{:S(2)}, u32[]{:S(2)}) async-start(bf16[16,16,1024]{2,1,0:T(8,128)(2,1)} %bitcast.79), calls=%async_computation | async-start | bytes 1048576 | tf_op jit(solution)/shard_map/all_to_all | solution.py:251
  14.4 1.7 convert_element_type.50
  16.2 1.3 copy.22
  17.5 2.3 copy.23
  19.7 1.4 collective-permute-done
  21.2 1.7 fusion
  25.0 5.8 %collective-permute-done.2.refs_1_.refs_2_ = bf16[256,2048]{1,0:T(8,128)(2,1)} collective-permute-done((bf16[256,2048]{1,0:T(8,128)(2,1)}, bf16[256,2048]{1,0:T(8,128)(2,1)}, u32[]{:S(2)}, u32[]{:S(2)}) %collective-permute-start.2) | collective-permute-done | bytes 1048608 | tf_op jit(solution)/shard_map/ppermute | solution.py:31
  30.8 9.7 %all-to-all-start.1 = ((f32[128,1,128]{2,1,0:T(1,128)}), f32[128,1,128]{2,1,0:T(1,128)S(1)}, u32[]{:S(2)}, u32[]{:S(2)}) async-start(f32[128,1,128]{2,1,0:T(1,128)} %bitcast.10), calls=%async_computation.1 | async-start | bytes 131072 | tf_op jit(solution)/shard_map/all_to_all | solution.py:284
  40.5 16.2 %all-to-all-done.1 = f32[128,1,128]{2,1,0:T(1,128)S(1)} async-done(((f32[128,1,128]{2,1,0:T(1,128)}), f32[128,1,128]{2,1,0:T(1,128)S(1)}, u32[]{:S(2)}, u32[]{:S(2)}) %all-to-all-start.1) | async-done | bytes 65568 | tf_op jit(solution)/shard_map/all_to_all | solution.py:284
  57.2 1.1 first_solution.1.initial
  59.2 2.3 collective-permute-start.6
  61.6 3.2 %collective-permute-start.7 = (bf16[256,2048]{1,0:T(8,128)(2,1)}, bf16[256,2048]{1,0:T(8,128)(2,1)}, u32[]{:S(2)}, u32[]{:S(2)}) collective-permute-start(bf16[256,2048]{1,0:T(8,128)(2,1)} %collective-permute-done.3.refs_4_.refs_5_), channel_id=1, source_target_pairs={{0,4},{4,0},{1,5},{5,1},{2,6},{6,2},{3,7},{7,3},{8,12},{12,8},{9,1... | collective-permute-start | bytes 3145736 | tf_op jit(solution)/shard_map/ppermute | solution.py:35
  65.4 6.0 %all-to-all-start.2 = ((bf16[16,16,1024]{2,1,0:T(8,128)(2,1)}), bf16[16,16,1024]{2,1,0:T(8,128)(2,1)}, u32[]{:S(2)}, u32[]{:S(2)}) async-start(bf16[16,16,1024]{2,1,0:T(8,128)(2,1)} %first_solution.1.initial), calls=%async_computation.2 | async-start | bytes 1048576 | tf_op jit(solution)/shard_map/all_to_all | solution.py:251
  71.4 1.1 convert_bitcast_fusion
  72.5 22.7 %all-to-all-done.2 = bf16[16,16,1024]{2,1,0:T(8,128)(2,1)} async-done(((bf16[16,16,1024]{2,1,0:T(8,128)(2,1)}), bf16[16,16,1024]{2,1,0:T(8,128)(2,1)}, u32[]{:S(2)}, u32[]{:S(2)}) %all-to-all-start.2) | async-done | bytes 524320 | tf_op jit(solution)/shard_map/all_to_all | solution.py:251
  95.2 3.6 %collective-permute-start.11 = (bf16[256,1024]{1,0:T(8,128)(2,1)}, bf16[256,1024]{1,0:T(8,128)(2,1)}, u32[]{:S(2)}, u32[]{:S(2)}) collective-permute-start(bf16[256,1024]{1,0:T(8,128)(2,1)} %bitcast.15.refs_0_), channel_id=1, source_target_pairs={{0,4},{4,0},{1,5},{5,1},{2,6},{6,2},{3,7},{7,3},{8,12},{12,8},{9,1... | collective-permute-start | bytes 1572872 | tf_op jit(solution)/shard_map/ppermute | solution.py:35
  98.8 3.0 %own_columns.1.refs_9_ = bf16[8,256,256]{2,1,0:T(8,128)(2,1)} custom-call(s32[8]{0:T(128)} %fusion.9.order.refs_0_, bf16[256,2048]{1,0:T(8,128)(2,1)} %bitcast.72, bf16[256,2048]{1,0:T(8,128)(2,1)} %collective-permute-done.2.refs_1_.refs_2_, bf16[256,2048]{1,0:T(8,128)(2,1)} %collective-permute-done.4.refs_2_.refs_3_, ...), custom_call_target="tpu_custom_call" | custom-call | tf_op jit(solution)/shard_map/own_columns/pallas_call | solution.py:73
  101.8 1.9 collective-permute-start.8
  103.8 5.8 %collective-permute-start.9 = (bf16[8,256,256]{2,1,0:T(8,128)(2,1)}, bf16[8,256,256]{2,1,0:T(8,128)(2,1)}, u32[]{:S(2)}, u32[]{:S(2)}) collective-permute-start(bf16[8,256,256]{2,1,0:T(8,128)(2,1)} %own_columns.1.refs_9_), channel_id=1, source_target_pairs={{8,0},{16,8},{24,16},{32,24},{40,32},{48,40},{56,48},{64,56},{72,6... | collective-permute-start | bytes 3145736 | tf_op jit(solution)/shard_map/ppermute | solution.py:27
  109.5 3.3 %collective-permute-start.13 = (bf16[256,1024]{1,0:T(8,128)(2,1)}, bf16[256,1024]{1,0:T(8,128)(2,1)}, u32[]{:S(2)}, u32[]{:S(2)}) collective-permute-start(bf16[256,1024]{1,0:T(8,128)(2,1)} %bitcast.15.refs_0_), channel_id=1, source_target_pairs={{0,3},{1,0},{2,1},{3,2},{4,7},{5,4},{6,5},{7,6},{8,11},{9,8},{10,9... | collective-permute-start | bytes 1572872 | tf_op jit(solution)/shard_map/ppermute | solution.py:31
  112.9 1.9 collective-permute-start.10
  114.9 7.7 %all-to-all-start.3 = ((bf16[8,256,256]{2,1,0:T(8,128)(2,1)}), bf16[8,256,256]{2,1,0:T(8,128)(2,1)}, u32[]{:S(2)}, u32[]{:S(2)}) async-start(bf16[8,256,256]{2,1,0:T(8,128)(2,1)} %bitcast.74), calls=%async_computation.3 | async-start | bytes 2097152 | tf_op jit(solution)/shard_map/all_to_all | solution.py:305
  122.5 19.9 %collective-permute-done.13.refs_2_ = bf16[256,1024]{1,0:T(8,128)(2,1)} collective-permute-done((bf16[256,1024]{1,0:T(8,128)(2,1)}, bf16[256,1024]{1,0:T(8,128)(2,1)}, u32[]{:S(2)}, u32[]{:S(2)}) %collective-permute-start.13) | collective-permute-done | bytes 524320 | tf_op jit(solution)/shard_map/ppermute | solution.py:31
  142.4 1.3 collective-permute-start.15
  143.7 2.4 collective-permute-start.16
  146.1 12.7 %refresh.1 = (f32[256,2048]{1,0:T(8,128)}, bf16[256,2048]{1,0:T(8,128)(2,1)}, bf16[256,2048]{1,0:T(8,128)(2,1)}, bf16[256,2048]{1,0:T(8,128)(2,1)}, bf16[256,2048]{1,0:T(8,128)(2,1)}) custom-call(s32[8]{0:T(128)} %fusion.9.order.refs_0_, bf16[256,2048]{1,0:T(8,128)(2,1)} %bitcast.73, bf16[256,2048]{1,0:T(8,128)(2,1)} %collective-permute-done.2.refs_1_.refs_2_, ...), custom_call_target="tpu_custom_call" | custom-call | tf_op jit(solution)/shard_map/refresh/pallas_call | solution.py:112
  158.9 9.5 %apply_blocks.1 = bf16[16,48,1024]{2,1,0:T(8,128)(2,1)} custom-call(s32[8]{0:T(128)} %fusion.9.order.refs_0_, bf16[256,1024]{1,0:T(8,128)(2,1)} %bitcast.15.refs_0_, bf16[256,1024]{1,0:T(8,128)(2,1)} %collective-permute-done.12.refs_1_, bf16[256,1024]{1,0:T(8,128)(2,1)} %collective-permute-done.13.refs_2_, ...), custom_call_target="tpu_custom_call" | custom-call | tf_op jit(solution)/shard_map/apply_blocks/pallas_call | solution.py:180
  168.4 24.0 %all_to_all.37.off = bf16[16,48,1024]{2,1,0:T(8,128)(2,1)S(1)} all-to-all(bf16[16,48,1024]{2,1,0:T(8,128)(2,1)} %apply_blocks.1), channel_id=1, replica_groups=mesh['layer_0'=2,'layer_1'=4,'layer_2'=2,'dp_0'=2,'dp_1'=4] {'layer_0','..., dimensions={0} | all-to-all | bytes 3145728 | tf_op jit(solution)/shard_map/all_to_all | solution.py:251
  192.4 2.7 %change.1 = bf16[16,16,1024]{2,1,0:T(8,128)(2,1)} custom-call(bf16[16,16,1024]{2,1,0:T(8,128)(2,1)S(1)} %all-to-all-done.grad, bf16[16,16,1024]{2,1,0:T(8,128)(2,1)} %first_solution.1.initial, bf16[16,48,1024]{2,1,0:T(8,128)(2,1)S(1)} %all_to_all.37.off, f32[16,16,128]{2,1,0:T(8,128)S(1)} %broadcast_in_dim.77.pivots, ...), custom_call_target="tpu_custom_call" | custom-call | tf_op jit(solution)/shard_map/change/pallas_call | solution.py:242
  195.1 4.9 %all-to-all-start.5 = ((bf16[16,16,1024]{2,1,0:T(8,128)(2,1)}), bf16[16,16,1024]{2,1,0:T(8,128)(2,1)S(1)}, u32[]{:S(2)}, u32[]{:S(2)}) async-start(bf16[16,16,1024]{2,1,0:T(8,128)(2,1)} %change.1), calls=%async_computation.5 | async-start | bytes 1048576 | tf_op jit(solution)/shard_map/all_to_all | solution.py:251
  200.0 4.3 %collective-permute-start.22 = (bf16[256,2048]{1,0:T(8,128)(2,1)}, bf16[256,2048]{1,0:T(8,128)(2,1)}, u32[]{:S(2)}, u32[]{:S(2)}) collective-permute-start(bf16[256,2048]{1,0:T(8,128)(2,1)} %get-tuple-element.74), channel_id=1, source_target_pairs={{8,0},{16,8},{24,16},{32,24},{40,32},{48,40},{56,48},{64,56},{72,6... | collective-permute-start | bytes 3145736 | tf_op jit(solution)/shard_map/ppermute | solution.py:27
  204.4 5.1 %all-to-all-done.5 = bf16[16,16,1024]{2,1,0:T(8,128)(2,1)S(1)} async-done(((bf16[16,16,1024]{2,1,0:T(8,128)(2,1)}), bf16[16,16,1024]{2,1,0:T(8,128)(2,1)S(1)}, u32[]{:S(2)}, u32[]{:S(2)}) %all-to-all-start.5) | async-done | bytes 524320 | tf_op jit(solution)/shard_map/all_to_all | solution.py:251
  209.5 3.1 %fusion.12 = (bf16[256,1024]{1,0:T(8,128)(2,1)S(1)}, f32[256,1024]{1,0:T(8,128)}, bf16[1,256,1024]{2,1,0:T(8,128)(2,1)}) fusion(bf16[16,16,1024]{2,1,0:T(8,128)(2,1)S(1)} %all-to-all-done.5, bf16[256,1024]{1,0:T(8,128)(2,1)} %bitcast.15.refs_0_, f32[256]{0:T(256)S(1)} %get-tuple-element.91, bf16[1,256,1024]{2,1,0:T(8,128)(2,1)} %param.12, ...), kind=kLoop, calls=%fused_computation.35 | loop fusion | flops 3145728 | bytes 4720640 | tf_op jit(solution)/shard_map/convert_element_type | solution.py:320
  212.6 3.5 %collective-permute-start.18 = (bf16[256,1024]{1,0:T(8,128)(2,1)S(1)}, bf16[256,1024]{1,0:T(8,128)(2,1)}, u32[]{:S(2)}, u32[]{:S(2)}) collective-permute-start(bf16[256,1024]{1,0:T(8,128)(2,1)S(1)} %get-tuple-element.79.refs_0_), channel_id=1, source_target_pairs={{0,4},{4,0},{1,5},{5,1},{2,6},{6,2},{3,7},{7,3},{8,12},{12,8},{9,1... | collective-permute-start | bytes 1572872 | tf_op jit(solution)/shard_map/ppermute | solution.py:35
  216.1 3.2 %collective-permute-start.20 = (bf16[256,1024]{1,0:T(8,128)(2,1)S(1)}, bf16[256,1024]{1,0:T(8,128)(2,1)S(1)}, u32[]{:S(2)}, u32[]{:S(2)}) collective-permute-start(bf16[256,1024]{1,0:T(8,128)(2,1)S(1)} %get-tuple-element.79.refs_0_), channel_id=1, source_target_pairs={{0,3},{1,0},{2,1},{3,2},{4,7},{5,4},{6,5},{7,6},{8,11},{9,8},{10,9... | collective-permute-start | bytes 1572872 | tf_op jit(solution)/shard_map/ppermute | solution.py:31
  220.1 13.4 %collective-permute-done.18.refs_3_ = bf16[256,1024]{1,0:T(8,128)(2,1)} collective-permute-done((bf16[256,1024]{1,0:T(8,128)(2,1)S(1)}, bf16[256,1024]{1,0:T(8,128)(2,1)}, u32[]{:S(2)}, u32[]{:S(2)}) %collective-permute-start.18) | collective-permute-done | bytes 524320 | tf_op jit(solution)/shard_map/ppermute | solution.py:35
  233.5 7.9 %collective-permute-done.20.refs_2_ = bf16[256,1024]{1,0:T(8,128)(2,1)S(1)} collective-permute-done((bf16[256,1024]{1,0:T(8,128)(2,1)S(1)}, bf16[256,1024]{1,0:T(8,128)(2,1)S(1)}, u32[]{:S(2)}, u32[]{:S(2)}) %collective-permute-start.20) | collective-permute-done | bytes 524320 | tf_op jit(solution)/shard_map/ppermute | solution.py:31
  241.4 1.1 collective-permute-done.21.refs_4_
  242.5 1.1 collective-permute-start.23
  243.6 2.3 collective-permute-start.24
  246.2 4.9 %place_rows.2.refs_3_ = bf16[2048,1024]{1,0:T(8,128)(2,1)} custom-call(s32[5]{0:T(128)} %bitcast.86, bf16[256,1024]{1,0:T(8,128)(2,1)} %copy-done.2, bf16[256,1024]{1,0:T(8,128)(2,1)} %copy-done.4, bf16[256,1024]{1,0:T(8,128)(2,1)} %copy-done.5, bf16[256,1024]{1,0:T(8,128)(2,1)} %collective-permute-done.18.refs_3_, ...), custom_call_target="tpu_custom_call" | custom-call | tf_op jit(solution)/shard_map/place_rows/pallas_call | solution.py:139
  251.1 3.0 %bitcast_add_fusion = f32[256,2048]{1,0:T(8,128)} fusion(bf16[256,2048]{1,0:T(8,128)(2,1)} %collective-permute-done.22, f32[1,256,2048]{2,1,0:T(8,128)S(1)} %copy-done), kind=kLoop, calls=%fused_computation.4 | loop fusion | flops 2097152 | bytes 5242880 | tf_op jit(solution)/shard_map/add | solution.py:322
  254.0 2.6 collective-permute-done.23.refs_0_
  256.7 3.1 %collective-permute-done.25.refs_2_ = bf16[256,1024]{1,0:T(8,128)(2,1)} collective-permute-done((bf16[256,1024]{1,0:T(8,128)(2,1)}, bf16[256,1024]{1,0:T(8,128)(2,1)}, u32[]{:S(2)}, u32[]{:S(2)}) %collective-permute-start.25) | collective-permute-done | bytes 524320 | tf_op jit(solution)/shard_map/ppermute | solution.py:35
  259.7 3.7 %place_rows.3 = bf16[2048,1024]{1,0:T(8,128)(2,1)} custom-call(s32[3]{0:T(128)} %slice.19.order, bf16[256,1024]{1,0:T(8,128)(2,1)} %copy-done.3, bf16[256,1024]{1,0:T(8,128)(2,1)} %collective-permute-done.24.refs_1_, bf16[256,1024]{1,0:T(8,128)(2,1)} %collective-permute-done.25.refs_2_, ...), custom_call_target="tpu_custom_call", output_to_operand_aliasing={{}: (4, {})} | custom-call | tf_op jit(solution)/shard_map/place_rows/pallas_call | solution.py:139
  (72 shorter events, 6.7 us)
Async XLA Ops:
  0.6 20.6 %collective-permute-start = (bf16[256,2048]{1,0:T(8,128)(2,1)}, bf16[256,2048]{1,0:T(8,128)(2,1)}, u32[]{:S(2)}, u32[]{:S(2)}) collective-permute-start(bf16[256,2048]{1,0:T(8,128)(2,1)} %bitcast.68), channel_id=1, source_target_pairs={{8,0},{16,8},{24,16},{32,24},{40,32},{48,40},{56,48},{64,56},{72,6... | collective-permute-start | bytes 3145736 | tf_op jit(solution)/shard_map/ppermute | solution.py:27
  5.3 25.5 %collective-permute-start.2 = (bf16[256,2048]{1,0:T(8,128)(2,1)}, bf16[256,2048]{1,0:T(8,128)(2,1)}, u32[]{:S(2)}, u32[]{:S(2)}) collective-permute-start(bf16[256,2048]{1,0:T(8,128)(2,1)} %bitcast.69), channel_id=1, source_target_pairs={{0,1},{1,2},{2,3},{3,0},{4,5},{5,6},{6,7},{7,4},{8,9},{9,10},{10,1... | collective-permute-start | bytes 3145736 | tf_op jit(solution)/shard_map/ppermute | solution.py:31
  7.3 33.2 %collective-permute-start.4 = (bf16[256,2048]{1,0:T(8,128)(2,1)}, bf16[256,2048]{1,0:T(8,128)(2,1)}, u32[]{:S(2)}, u32[]{:S(2)}) collective-permute-start(bf16[256,2048]{1,0:T(8,128)(2,1)} %bitcast.70), channel_id=1, source_target_pairs={{0,3},{1,0},{2,1},{3,2},{4,7},{5,4},{6,5},{7,6},{8,11},{9,8},{10,9... | collective-permute-start | bytes 3145736 | tf_op jit(solution)/shard_map/ppermute | solution.py:31
  9.5 14.6 %all-to-all-start = ((bf16[16,16,1024]{2,1,0:T(8,128)(2,1)}), bf16[16,16,1024]{2,1,0:T(8,128)(2,1)S(1)}, u32[]{:S(2)}, u32[]{:S(2)}) async-start(bf16[16,16,1024]{2,1,0:T(8,128)(2,1)} %bitcast.79), calls=%async_computation | async-start | bytes 1048576 | tf_op jit(solution)/shard_map/all_to_all | solution.py:251
  16.2 5.0 %copy-start.1 = (bf16[1,256,2048]{2,1,0:T(8,128)(2,1)S(1)}, bf16[1,256,2048]{2,1,0:T(8,128)(2,1)}, u32[]{:S(2)}) copy-start(bf16[1,256,2048]{2,1,0:T(8,128)(2,1)} %param.8) | copy-start | bytes 3145732
  22.9 42.0 %copy-start.7 = (s32[8]{0:T(128)S(1)}, s32[8]{0:T(128)}, u32[]{:S(2)}) copy-start(s32[8]{0:T(128)} %constant.57.clone) | copy-start | bytes 100
  23.1 48.2 %copy-start = (f32[1,256,2048]{2,1,0:T(8,128)S(1)}, f32[1,256,2048]{2,1,0:T(8,128)}, u32[]{:S(2)}) copy-start(f32[1,256,2048]{2,1,0:T(8,128)} %param.10) | copy-start | bytes 6291460
  24.0 32.7 %collective-permute-start.1 = (bf16[256,2048]{1,0:T(8,128)(2,1)}, bf16[256,2048]{1,0:T(8,128)(2,1)}, u32[]{:S(2)}, u32[]{:S(2)}) collective-permute-start(bf16[256,2048]{1,0:T(8,128)(2,1)} %bitcast.71), channel_id=1, source_target_pairs={{0,4},{4,0},{1,5},{5,1},{2,6},{6,2},{3,7},{7,3},{8,12},{12,8},{9,1... | collective-permute-start | bytes 3145736 | tf_op jit(solution)/shard_map/ppermute | solution.py:35
  30.8 25.9 %collective-permute-start.3 = (bf16[256,2048]{1,0:T(8,128)(2,1)}, bf16[256,2048]{1,0:T(8,128)(2,1)}, u32[]{:S(2)}, u32[]{:S(2)}) collective-permute-start(bf16[256,2048]{1,0:T(8,128)(2,1)} %collective-permute-done.2.refs_1_.refs_2_), channel_id=1, source_target_pairs={{0,1},{1,2},{2,3},{3,0},{4,5},{5,6},{6,7},{7,4},{8,9},{9,10},{10,1... | collective-permute-start | bytes 3145736 | tf_op jit(solution)/shard_map/ppermute | solution.py:31
  30.8 25.9 %all-to-all-start.1 = ((f32[128,1,128]{2,1,0:T(1,128)}), f32[128,1,128]{2,1,0:T(1,128)S(1)}, u32[]{:S(2)}, u32[]{:S(2)}) async-start(f32[128,1,128]{2,1,0:T(1,128)} %bitcast.10), calls=%async_computation.1 | async-start | bytes 131072 | tf_op jit(solution)/shard_map/all_to_all | solution.py:284
  58.4 36.8 %collective-permute-start.5 = (bf16[256,2048]{1,0:T(8,128)(2,1)}, bf16[256,2048]{1,0:T(8,128)(2,1)}, u32[]{:S(2)}, u32[]{:S(2)}) collective-permute-start(bf16[256,2048]{1,0:T(8,128)(2,1)} %collective-permute-done.1.refs_3_.refs_4_), channel_id=1, source_target_pairs={{0,1},{1,2},{2,3},{3,0},{4,5},{5,6},{6,7},{7,4},{8,9},{9,10},{10,1... | collective-permute-start | bytes 3145736 | tf_op jit(solution)/shard_map/ppermute | solution.py:31
  59.2 36.0 %collective-permute-start.6 = (bf16[256,2048]{1,0:T(8,128)(2,1)}, bf16[256,2048]{1,0:T(8,128)(2,1)}, u32[]{:S(2)}, u32[]{:S(2)}) collective-permute-start(bf16[256,2048]{1,0:T(8,128)(2,1)} %collective-permute-done.1.refs_3_.refs_4_), channel_id=1, source_target_pairs={{0,3},{1,0},{2,1},{3,2},{4,7},{5,4},{6,5},{7,6},{8,11},{9,8},{10,9... | collective-permute-start | bytes 3145736 | tf_op jit(solution)/shard_map/ppermute | solution.py:31
  61.6 33.6 %collective-permute-start.7 = (bf16[256,2048]{1,0:T(8,128)(2,1)}, bf16[256,2048]{1,0:T(8,128)(2,1)}, u32[]{:S(2)}, u32[]{:S(2)}) collective-permute-start(bf16[256,2048]{1,0:T(8,128)(2,1)} %collective-permute-done.3.refs_4_.refs_5_), channel_id=1, source_target_pairs={{0,4},{4,0},{1,5},{5,1},{2,6},{6,2},{3,7},{7,3},{8,12},{12,8},{9,1... | collective-permute-start | bytes 3145736 | tf_op jit(solution)/shard_map/ppermute | solution.py:35
  65.4 29.8 %all-to-all-start.2 = ((bf16[16,16,1024]{2,1,0:T(8,128)(2,1)}), bf16[16,16,1024]{2,1,0:T(8,128)(2,1)}, u32[]{:S(2)}, u32[]{:S(2)}) async-start(bf16[16,16,1024]{2,1,0:T(8,128)(2,1)} %first_solution.1.initial), calls=%async_computation.2 | async-start | bytes 1048576 | tf_op jit(solution)/shard_map/all_to_all | solution.py:251
  95.2 17.6 %collective-permute-start.11 = (bf16[256,1024]{1,0:T(8,128)(2,1)}, bf16[256,1024]{1,0:T(8,128)(2,1)}, u32[]{:S(2)}, u32[]{:S(2)}) collective-permute-start(bf16[256,1024]{1,0:T(8,128)(2,1)} %bitcast.15.refs_0_), channel_id=1, source_target_pairs={{0,4},{4,0},{1,5},{5,1},{2,6},{6,2},{3,7},{7,3},{8,12},{12,8},{9,1... | collective-permute-start | bytes 1572872 | tf_op jit(solution)/shard_map/ppermute | solution.py:35
  98.8 14.1 %collective-permute-start.12 = (bf16[256,1024]{1,0:T(8,128)(2,1)}, bf16[256,1024]{1,0:T(8,128)(2,1)}, u32[]{:S(2)}, u32[]{:S(2)}) collective-permute-start(bf16[256,1024]{1,0:T(8,128)(2,1)} %bitcast.15.refs_0_), channel_id=1, source_target_pairs={{0,1},{1,2},{2,3},{3,0},{4,5},{5,6},{6,7},{7,4},{8,9},{9,10},{10,1... | collective-permute-start | bytes 1572872 | tf_op jit(solution)/shard_map/ppermute | solution.py:31
  101.8 44.3 %collective-permute-start.8 = (bf16[8,256,256]{2,1,0:T(8,128)(2,1)}, bf16[8,256,256]{2,1,0:T(8,128)(2,1)}, u32[]{:S(2)}, u32[]{:S(2)}) collective-permute-start(bf16[8,256,256]{2,1,0:T(8,128)(2,1)} %own_columns.1.refs_9_), channel_id=1, source_target_pairs={{0,8},{8,16},{16,24},{24,32},{32,40},{40,48},{48,56},{56,64},{64,7... | collective-permute-start | bytes 3145736 | tf_op jit(solution)/shard_map/ppermute | solution.py:27
  103.8 42.4 %collective-permute-start.9 = (bf16[8,256,256]{2,1,0:T(8,128)(2,1)}, bf16[8,256,256]{2,1,0:T(8,128)(2,1)}, u32[]{:S(2)}, u32[]{:S(2)}) collective-permute-start(bf16[8,256,256]{2,1,0:T(8,128)(2,1)} %own_columns.1.refs_9_), channel_id=1, source_target_pairs={{8,0},{16,8},{24,16},{32,24},{40,32},{48,40},{56,48},{64,56},{72,6... | collective-permute-start | bytes 3145736 | tf_op jit(solution)/shard_map/ppermute | solution.py:27
  109.5 32.9 %collective-permute-start.13 = (bf16[256,1024]{1,0:T(8,128)(2,1)}, bf16[256,1024]{1,0:T(8,128)(2,1)}, u32[]{:S(2)}, u32[]{:S(2)}) collective-permute-start(bf16[256,1024]{1,0:T(8,128)(2,1)} %bitcast.15.refs_0_), channel_id=1, source_target_pairs={{0,3},{1,0},{2,1},{3,2},{4,7},{5,4},{6,5},{7,6},{8,11},{9,8},{10,9... | collective-permute-start | bytes 1572872 | tf_op jit(solution)/shard_map/ppermute | solution.py:31
  112.8 29.6 %collective-permute-start.14 = (bf16[256,1024]{1,0:T(8,128)(2,1)}, bf16[256,1024]{1,0:T(8,128)(2,1)}, u32[]{:S(2)}, u32[]{:S(2)}) collective-permute-start(bf16[256,1024]{1,0:T(8,128)(2,1)} %bitcast.15.refs_0_), channel_id=1, source_target_pairs={{0,2},{1,3},{2,0},{3,1},{4,6},{5,7},{6,4},{7,5},{8,10},{9,11},{10,... | collective-permute-start | bytes 1572872 | tf_op jit(solution)/shard_map/ppermute | solution.py:31
  112.9 33.2 %collective-permute-start.10 = (bf16[256,2048]{1,0:T(8,128)(2,1)}, bf16[256,2048]{1,0:T(8,128)(2,1)}, u32[]{:S(2)}, u32[]{:S(2)}) collective-permute-start(bf16[256,2048]{1,0:T(8,128)(2,1)} %convert_bitcast_fusion), channel_id=1, source_target_pairs={{0,8},{8,16},{16,24},{24,32},{32,40},{40,48},{48,56},{56,64},{64,7... | collective-permute-start | bytes 3145736 | tf_op jit(solution)/shard_map/ppermute | solution.py:27
  114.9 44.0 %all-to-all-start.3 = ((bf16[8,256,256]{2,1,0:T(8,128)(2,1)}), bf16[8,256,256]{2,1,0:T(8,128)(2,1)}, u32[]{:S(2)}, u32[]{:S(2)}) async-start(bf16[8,256,256]{2,1,0:T(8,128)(2,1)} %bitcast.74), calls=%async_computation.3 | async-start | bytes 2097152 | tf_op jit(solution)/shard_map/all_to_all | solution.py:305
  142.4 16.5 %collective-permute-start.15 = (bf16[256,1024]{1,0:T(8,128)(2,1)}, bf16[256,1024]{1,0:T(8,128)(2,1)}, u32[]{:S(2)}, u32[]{:S(2)}) collective-permute-start(bf16[256,1024]{1,0:T(8,128)(2,1)} %collective-permute-done.11.refs_3_), channel_id=1, source_target_pairs={{0,1},{1,2},{2,3},{3,0},{4,5},{5,6},{6,7},{7,4},{8,9},{9,10},{10,1... | collective-permute-start | bytes 1572872 | tf_op jit(solution)/shard_map/ppermute | solution.py:31
  143.7 15.2 %collective-permute-start.16 = (bf16[256,1024]{1,0:T(8,128)(2,1)}, bf16[256,1024]{1,0:T(8,128)(2,1)}, u32[]{:S(2)}, u32[]{:S(2)}) collective-permute-start(bf16[256,1024]{1,0:T(8,128)(2,1)} %collective-permute-done.11.refs_3_), channel_id=1, source_target_pairs={{0,3},{1,0},{2,1},{3,2},{4,7},{5,4},{6,5},{7,6},{8,11},{9,8},{10,9... | collective-permute-start | bytes 1572872 | tf_op jit(solution)/shard_map/ppermute | solution.py:31
  146.1 12.8 %collective-permute-start.17 = (bf16[256,1024]{1,0:T(8,128)(2,1)}, bf16[256,1024]{1,0:T(8,128)(2,1)}, u32[]{:S(2)}, u32[]{:S(2)}) collective-permute-start(bf16[256,1024]{1,0:T(8,128)(2,1)} %collective-permute-done.14.refs_4_), channel_id=1, source_target_pairs={{0,4},{4,0},{1,5},{5,1},{2,6},{6,2},{3,7},{7,3},{8,12},{12,8},{9,1... | collective-permute-start | bytes 1572872 | tf_op jit(solution)/shard_map/ppermute | solution.py:35
  192.4 7.5 %copy-start.8 = (s32[1,2]{1,0:T(1,128)S(1)}, s32[1,2]{1,0:T(1,128)}, u32[]{:S(2)}) copy-start(s32[1,2]{1,0:T(1,128)} %param.13) | copy-start | bytes 28
  195.1 14.4 %all-to-all-start.5 = ((bf16[16,16,1024]{2,1,0:T(8,128)(2,1)}), bf16[16,16,1024]{2,1,0:T(8,128)(2,1)S(1)}, u32[]{:S(2)}, u32[]{:S(2)}) async-start(bf16[16,16,1024]{2,1,0:T(8,128)(2,1)} %change.1), calls=%async_computation.5 | async-start | bytes 1048576 | tf_op jit(solution)/shard_map/all_to_all | solution.py:251
  200.0 51.1 %collective-permute-start.22 = (bf16[256,2048]{1,0:T(8,128)(2,1)}, bf16[256,2048]{1,0:T(8,128)(2,1)}, u32[]{:S(2)}, u32[]{:S(2)}) collective-permute-start(bf16[256,2048]{1,0:T(8,128)(2,1)} %get-tuple-element.74), channel_id=1, source_target_pairs={{8,0},{16,8},{24,16},{32,24},{40,32},{48,40},{56,48},{64,56},{72,6... | collective-permute-start | bytes 3145736 | tf_op jit(solution)/shard_map/ppermute | solution.py:27
  209.5 10.1 %copy-start.6 = (s32[8]{0:T(128)S(1)}, s32[8]{0:T(128)}, u32[]{:S(2)}) copy-start(s32[8]{0:T(128)} %fusion.9.order.refs_0_) | copy-start | bytes 100
  212.6 33.6 %copy-start.2 = (bf16[256,1024]{1,0:T(8,128)(2,1)}, bf16[256,1024]{1,0:T(8,128)(2,1)S(1)}, u32[]{:S(2)}) copy-start(bf16[256,1024]{1,0:T(8,128)(2,1)S(1)} %get-tuple-element.79.refs_0_) | copy-start | bytes 1572868
  212.6 20.9 %collective-permute-start.18 = (bf16[256,1024]{1,0:T(8,128)(2,1)S(1)}, bf16[256,1024]{1,0:T(8,128)(2,1)}, u32[]{:S(2)}, u32[]{:S(2)}) collective-permute-start(bf16[256,1024]{1,0:T(8,128)(2,1)S(1)} %get-tuple-element.79.refs_0_), channel_id=1, source_target_pairs={{0,4},{4,0},{1,5},{5,1},{2,6},{6,2},{3,7},{7,3},{8,12},{12,8},{9,1... | collective-permute-start | bytes 1572872 | tf_op jit(solution)/shard_map/ppermute | solution.py:35
  216.1 17.4 %collective-permute-start.19 = (bf16[256,1024]{1,0:T(8,128)(2,1)S(1)}, bf16[256,1024]{1,0:T(8,128)(2,1)S(1)}, u32[]{:S(2)}, u32[]{:S(2)}) collective-permute-start(bf16[256,1024]{1,0:T(8,128)(2,1)S(1)} %get-tuple-element.79.refs_0_), channel_id=1, source_target_pairs={{0,1},{1,2},{2,3},{3,0},{4,5},{5,6},{6,7},{7,4},{8,9},{9,10},{10,1... | collective-permute-start | bytes 1572872 | tf_op jit(solution)/shard_map/ppermute | solution.py:31
  216.1 25.3 %collective-permute-start.20 = (bf16[256,1024]{1,0:T(8,128)(2,1)S(1)}, bf16[256,1024]{1,0:T(8,128)(2,1)S(1)}, u32[]{:S(2)}, u32[]{:S(2)}) collective-permute-start(bf16[256,1024]{1,0:T(8,128)(2,1)S(1)} %get-tuple-element.79.refs_0_), channel_id=1, source_target_pairs={{0,3},{1,0},{2,1},{3,2},{4,7},{5,4},{6,5},{7,6},{8,11},{9,8},{10,9... | collective-permute-start | bytes 1572872 | tf_op jit(solution)/shard_map/ppermute | solution.py:31
  219.3 23.2 %collective-permute-start.21 = (bf16[256,1024]{1,0:T(8,128)(2,1)S(1)}, bf16[256,1024]{1,0:T(8,128)(2,1)}, u32[]{:S(2)}, u32[]{:S(2)}) collective-permute-start(bf16[256,1024]{1,0:T(8,128)(2,1)S(1)} %get-tuple-element.79.refs_0_), channel_id=1, source_target_pairs={{0,2},{1,3},{2,0},{3,1},{4,6},{5,7},{6,4},{7,5},{8,10},{9,11},{10,... | collective-permute-start | bytes 1572872 | tf_op jit(solution)/shard_map/ppermute | solution.py:31
  233.5 7.9 %copy-start.4 = (bf16[256,1024]{1,0:T(8,128)(2,1)}, bf16[256,1024]{1,0:T(8,128)(2,1)S(1)}, u32[]{:S(2)}) copy-start(bf16[256,1024]{1,0:T(8,128)(2,1)S(1)} %collective-permute-done.19.refs_1_) | copy-start | bytes 1572868
  241.4 1.1 copy-start.5
  242.5 14.2 %collective-permute-start.23 = (bf16[256,1024]{1,0:T(8,128)(2,1)}, bf16[256,1024]{1,0:T(8,128)(2,1)S(1)}, u32[]{:S(2)}, u32[]{:S(2)}) collective-permute-start(bf16[256,1024]{1,0:T(8,128)(2,1)} %collective-permute-done.18.refs_3_), channel_id=1, source_target_pairs={{0,1},{1,2},{2,3},{3,0},{4,5},{5,6},{6,7},{7,4},{8,9},{9,10},{10,1... | collective-permute-start | bytes 1572872 | tf_op jit(solution)/shard_map/ppermute | solution.py:31
  243.6 13.0 %collective-permute-start.24 = (bf16[256,1024]{1,0:T(8,128)(2,1)}, bf16[256,1024]{1,0:T(8,128)(2,1)}, u32[]{:S(2)}, u32[]{:S(2)}) collective-permute-start(bf16[256,1024]{1,0:T(8,128)(2,1)} %collective-permute-done.18.refs_3_), channel_id=1, source_target_pairs={{0,3},{1,0},{2,1},{3,2},{4,7},{5,4},{6,5},{7,6},{8,11},{9,8},{10,9... | collective-permute-start | bytes 1572872 | tf_op jit(solution)/shard_map/ppermute | solution.py:31
  245.9 13.8 %collective-permute-start.25 = (bf16[256,1024]{1,0:T(8,128)(2,1)}, bf16[256,1024]{1,0:T(8,128)(2,1)}, u32[]{:S(2)}, u32[]{:S(2)}) collective-permute-start(bf16[256,1024]{1,0:T(8,128)(2,1)} %collective-permute-done.21.refs_4_), channel_id=1, source_target_pairs={{0,4},{4,0},{1,5},{5,1},{2,6},{6,2},{3,7},{7,3},{8,12},{12,8},{9,1... | collective-permute-start | bytes 1572872 | tf_op jit(solution)/shard_map/ppermute | solution.py:35
  256.7 3.1 %copy-start.3 = (bf16[256,1024]{1,0:T(8,128)(2,1)}, bf16[256,1024]{1,0:T(8,128)(2,1)S(1)}, u32[]{:S(2)}) copy-start(bf16[256,1024]{1,0:T(8,128)(2,1)S(1)} %collective-permute-done.23.refs_0_) | copy-start | bytes 1572868

commit v6 on v5

--- a/solution.py
+++ b/solution.py
@@ -242,7 +242,7 @@
     return pl.pallas_call(
         kernel,
         out_shape=jax.ShapeDtypeStruct(arrays[0].shape, BF16),
-        compiler_params=pltpu.CompilerParams(vmem_limit_bytes=32 * 2**20),
+        compiler_params=pltpu.CompilerParams(vmem_limit_bytes=60 * 2**20),
         name=name,
     )(*arrays, *coefficients)
 

time: 265 us -> 270 us (1.019)
  transfers between devices with their start and end apart: 31 -> 31, of which waited for: 12 -> 11; matrix products, arithmetic and copies ran while one was open for 7% -> 6% of each run, Pallas kernels for 8% -> 8%
where the time goes in v6:
time: 270 us; the launch traced here: 269 us
  waiting for transfers between devices  99.6 us (37%)
  starting transfers between devices  84.2 us (31%)
  Pallas kernels  39.6 us (15%)
  blocking collectives  24.1 us (9%)
  other arithmetic  12.3 us (5%)
  local copies, waits for them, and re-layouts  7.75 us (3%)
    ppermute x15, waiting for transfers between devices, turned(): lax.ppermute(value, 'dp_1', [(i, (i + steps) % TURN) for i in range(TURN)])  36.8 us
    all_to_all x3, waiting for transfers between devices, by_layer(): return lax.all_to_all(value, LAYER, 0, 0)  27.6 us
    all_to_all x1, blocking collectives, by_layer(): return lax.all_to_all(value, LAYER, 0, 0)  24.1 us
    ppermute x15, starting transfers between devices, turned(): lax.ppermute(value, 'dp_1', [(i, (i + steps) % TURN) for i in range(TURN)])  21.5 us
    ppermute x5, starting transfers between devices, along_layers(): return lax.ppermute(value, LAYER, pairs)  18.5 us
    ppermute x6, waiting for transfers between devices, across(): return lax.ppermute(value, 'dp_0', [(0, 1), (1, 0)])  16.5 us
    all_to_all x1, waiting for transfers between devices, body(): arrived = lax.all_to_all(message, LAYER + DP, 0, 0, tiled=True)  16 us
    all_to_all x3, starting transfers between devices, by_layer(): return lax.all_to_all(value, LAYER, 0, 0)  15.1 us
  transfers between devices with their start and end apart: 31, of which 11 were waited for; matrix products, arithmetic and copies ran while one was open for 6% of the time, Pallas kernels for 8%

profile of v6, /device:TPU:6, one launch (start us, length us, event | category | flops | bytes accessed | tf_op | source)
XLA Modules:
  0.0 268.6 jit_solution(15644145685390807293)
XLA Ops:
  0.6 4.6 %collective-permute-start = (bf16[256,2048]{1,0:T(8,128)(2,1)}, bf16[256,2048]{1,0:T(8,128)(2,1)}, u32[]{:S(2)}, u32[]{:S(2)}) collective-permute-start(bf16[256,2048]{1,0:T(8,128)(2,1)} %bitcast.68), channel_id=1, source_target_pairs={{8,0},{16,8},{24,16},{32,24},{40,32},{48,40},{56,48},{64,56},{72,6... | collective-permute-start | bytes 3145736 | tf_op jit(solution)/shard_map/ppermute | solution.py:27
  5.3 2.0 collective-permute-start.2
  7.3 2.2 collective-permute-start.4
  9.5 4.1 %all-to-all-start = ((bf16[16,16,1024]{2,1,0:T(8,128)(2,1)}), bf16[16,16,1024]{2,1,0:T(8,128)(2,1)}, u32[]{:S(2)}, u32[]{:S(2)}) async-start(bf16[16,16,1024]{2,1,0:T(8,128)(2,1)} %bitcast.85), calls=%async_computation | async-start | bytes 1048576 | tf_op jit(solution)/shard_map/all_to_all | solution.py:251
  13.6 1.1 fusion.5
  14.9 1.7 convert_element_type.50
  17.2 1.3 copy.23
  18.5 2.7 %collective-permute-done = bf16[256,2048]{1,0:T(8,128)(2,1)} collective-permute-done((bf16[256,2048]{1,0:T(8,128)(2,1)}, bf16[256,2048]{1,0:T(8,128)(2,1)}, u32[]{:S(2)}, u32[]{:S(2)}) %collective-permute-start) | collective-permute-done | bytes 1048608 | tf_op jit(solution)/shard_map/ppermute | solution.py:27
  21.2 1.7 fusion
  25.0 5.8 %collective-permute-done.2.refs_1_.refs_2_ = bf16[256,2048]{1,0:T(8,128)(2,1)} collective-permute-done((bf16[256,2048]{1,0:T(8,128)(2,1)}, bf16[256,2048]{1,0:T(8,128)(2,1)}, u32[]{:S(2)}, u32[]{:S(2)}) %collective-permute-start.2) | collective-permute-done | bytes 1048608 | tf_op jit(solution)/shard_map/ppermute | solution.py:31
  30.8 9.7 %all-to-all-start.1 = ((f32[128,1,128]{2,1,0:T(1,128)}), f32[128,1,128]{2,1,0:T(1,128)S(1)}, u32[]{:S(2)}, u32[]{:S(2)}) async-start(f32[128,1,128]{2,1,0:T(1,128)} %bitcast.10), calls=%async_computation.1 | async-start | bytes 131072 | tf_op jit(solution)/shard_map/all_to_all | solution.py:284
  40.5 16.0 %all-to-all-done.1 = f32[128,1,128]{2,1,0:T(1,128)S(1)} async-done(((f32[128,1,128]{2,1,0:T(1,128)}), f32[128,1,128]{2,1,0:T(1,128)S(1)}, u32[]{:S(2)}, u32[]{:S(2)}) %all-to-all-start.1) | async-done | bytes 65568 | tf_op jit(solution)/shard_map/all_to_all | solution.py:284
  59.6 2.3 first_solution.1.initial
  62.9 2.3 collective-permute-start.6
  65.2 3.3 %collective-permute-start.7 = (bf16[256,2048]{1,0:T(8,128)(2,1)}, bf16[256,2048]{1,0:T(8,128)(2,1)}, u32[]{:S(2)}, u32[]{:S(2)}) collective-permute-start(bf16[256,2048]{1,0:T(8,128)(2,1)} %collective-permute-done.3.refs_4_.refs_5_), channel_id=1, source_target_pairs={{0,4},{4,0},{1,5},{5,1},{2,6},{6,2},{3,7},{7,3},{8,12},{12,8},{9,1... | collective-permute-start | bytes 3145736 | tf_op jit(solution)/shard_map/ppermute | solution.py:35
  69.2 6.1 %all-to-all-start.2 = ((bf16[16,16,1024]{2,1,0:T(8,128)(2,1)}), bf16[16,16,1024]{2,1,0:T(8,128)(2,1)S(1)}, u32[]{:S(2)}, u32[]{:S(2)}) async-start(bf16[16,16,1024]{2,1,0:T(8,128)(2,1)} %first_solution.1.initial), calls=%async_computation.2 | async-start | bytes 1048576 | tf_op jit(solution)/shard_map/all_to_all | solution.py:251
  75.3 1.1 convert_bitcast_fusion
  76.4 22.5 %all-to-all-done.2 = bf16[16,16,1024]{2,1,0:T(8,128)(2,1)S(1)} async-done(((bf16[16,16,1024]{2,1,0:T(8,128)(2,1)}), bf16[16,16,1024]{2,1,0:T(8,128)(2,1)S(1)}, u32[]{:S(2)}, u32[]{:S(2)}) %all-to-all-start.2) | async-done | bytes 524320 | tf_op jit(solution)/shard_map/all_to_all | solution.py:251
  98.9 3.6 %collective-permute-start.11 = (bf16[256,1024]{1,0:T(8,128)(2,1)S(1)}, bf16[256,1024]{1,0:T(8,128)(2,1)S(1)}, u32[]{:S(2)}, u32[]{:S(2)}) collective-permute-start(bf16[256,1024]{1,0:T(8,128)(2,1)S(1)} %bitcast.74), channel_id=1, source_target_pairs={{0,4},{4,0},{1,5},{5,1},{2,6},{6,2},{3,7},{7,3},{8,12},{12,8},{9,1... | collective-permute-start | bytes 1572872 | tf_op jit(solution)/shard_map/ppermute | solution.py:35
  102.6 3.0 %own_columns.1.refs_9_ = bf16[8,256,256]{2,1,0:T(8,128)(2,1)} custom-call(s32[8]{0:T(128)} %fusion.9.order.refs_0_, bf16[256,2048]{1,0:T(8,128)(2,1)} %bitcast.71, bf16[256,2048]{1,0:T(8,128)(2,1)} %collective-permute-done.2.refs_1_.refs_2_, bf16[256,2048]{1,0:T(8,128)(2,1)} %collective-permute-done.4.refs_2_.refs_3_, ...), custom_call_target="tpu_custom_call" | custom-call | tf_op jit(solution)/shard_map/own_columns/pallas_call | solution.py:73
  105.6 1.9 collective-permute-start.8
  107.5 5.8 %collective-permute-start.9 = (bf16[8,256,256]{2,1,0:T(8,128)(2,1)}, bf16[8,256,256]{2,1,0:T(8,128)(2,1)}, u32[]{:S(2)}, u32[]{:S(2)}) collective-permute-start(bf16[8,256,256]{2,1,0:T(8,128)(2,1)} %own_columns.1.refs_9_), channel_id=1, source_target_pairs={{8,0},{16,8},{24,16},{32,24},{40,32},{48,40},{56,48},{64,56},{72,6... | collective-permute-start | bytes 3145736 | tf_op jit(solution)/shard_map/ppermute | solution.py:27
  113.2 3.3 %collective-permute-start.13 = (bf16[256,1024]{1,0:T(8,128)(2,1)S(1)}, bf16[256,1024]{1,0:T(8,128)(2,1)}, u32[]{:S(2)}, u32[]{:S(2)}) collective-permute-start(bf16[256,1024]{1,0:T(8,128)(2,1)S(1)} %bitcast.76), channel_id=1, source_target_pairs={{0,3},{1,0},{2,1},{3,2},{4,7},{5,4},{6,5},{7,6},{8,11},{9,8},{10,9... | collective-permute-start | bytes 1572872 | tf_op jit(solution)/shard_map/ppermute | solution.py:31
  116.7 1.9 collective-permute-start.10
  118.6 7.7 %all-to-all-start.3 = ((bf16[8,256,256]{2,1,0:T(8,128)(2,1)}), bf16[8,256,256]{2,1,0:T(8,128)(2,1)}, u32[]{:S(2)}, u32[]{:S(2)}) async-start(bf16[8,256,256]{2,1,0:T(8,128)(2,1)} %bitcast.80), calls=%async_computation.3 | async-start | bytes 2097152 | tf_op jit(solution)/shard_map/all_to_all | solution.py:305
  126.3 19.5 %collective-permute-done.13.refs_2_ = bf16[256,1024]{1,0:T(8,128)(2,1)} collective-permute-done((bf16[256,1024]{1,0:T(8,128)(2,1)S(1)}, bf16[256,1024]{1,0:T(8,128)(2,1)}, u32[]{:S(2)}, u32[]{:S(2)}) %collective-permute-start.13) | collective-permute-done | bytes 524320 | tf_op jit(solution)/shard_map/ppermute | solution.py:31
  145.8 1.4 collective-permute-start.15
  147.2 2.4 collective-permute-start.16
  149.9 12.7 %refresh.1 = (f32[256,2048]{1,0:T(8,128)}, bf16[256,2048]{1,0:T(8,128)(2,1)}, bf16[256,2048]{1,0:T(8,128)(2,1)}, bf16[256,2048]{1,0:T(8,128)(2,1)}, bf16[256,2048]{1,0:T(8,128)(2,1)}) custom-call(s32[8]{0:T(128)} %fusion.9.order.refs_0_, bf16[256,2048]{1,0:T(8,128)(2,1)} %bitcast.72, bf16[256,2048]{1,0:T(8,128)(2,1)} %collective-permute-done.2.refs_1_.refs_2_, ...), custom_call_target="tpu_custom_call" | custom-call | tf_op jit(solution)/shard_map/refresh/pallas_call | solution.py:112
  163.4 9.5 %apply_blocks.1 = bf16[16,48,1024]{2,1,0:T(8,128)(2,1)} custom-call(s32[8]{0:T(128)} %fusion.9.order.refs_0_, bf16[256,1024]{1,0:T(8,128)(2,1)} %bitcast.78, bf16[256,1024]{1,0:T(8,128)(2,1)} %collective-permute-done.12.refs_1_, bf16[256,1024]{1,0:T(8,128)(2,1)} %collective-permute-done.13.refs_2_, bf16[256,1024]{1,0:T(8,128)(2,1)} %copy-done.5, ...), custom_call_target="tpu_custom_call" | custom-call | tf_op jit(solution)/shard_map/apply_blocks/pallas_call | solution.py:180
  172.9 24.1 %all_to_all.37.off = bf16[16,48,1024]{2,1,0:T(8,128)(2,1)} all-to-all(bf16[16,48,1024]{2,1,0:T(8,128)(2,1)} %apply_blocks.1), channel_id=1, replica_groups=mesh['layer_0'=2,'layer_1'=4,'layer_2'=2,'dp_0'=2,'dp_1'=4] {'layer_0','..., dimensions={0} | all-to-all | bytes 3145728 | tf_op jit(solution)/shard_map/all_to_all | solution.py:251
  197.1 3.5 %change.1 = bf16[16,16,1024]{2,1,0:T(8,128)(2,1)} custom-call(bf16[16,16,1024]{2,1,0:T(8,128)(2,1)} %all-to-all-done.grad, bf16[16,16,1024]{2,1,0:T(8,128)(2,1)} %first_solution.1.initial, bf16[16,48,1024]{2,1,0:T(8,128)(2,1)} %all_to_all.37.off, f32[16,16,128]{2,1,0:T(8,128)} %broadcast_in_dim.77.pivots, f32[16,16,128]{2,1,0:T(8,128)} %broadcast_in_dim.78.inverse, ...), custom_call_target="tpu_custom_call" | custom-call | tf_op jit(solution)/shard_map/change/pallas_call | solution.py:242
  200.5 4.9 %all-to-all-start.5 = ((bf16[16,16,1024]{2,1,0:T(8,128)(2,1)}), bf16[16,16,1024]{2,1,0:T(8,128)(2,1)S(1)}, u32[]{:S(2)}, u32[]{:S(2)}) async-start(bf16[16,16,1024]{2,1,0:T(8,128)(2,1)} %change.1), calls=%async_computation.5 | async-start | bytes 1048576 | tf_op jit(solution)/shard_map/all_to_all | solution.py:251
  205.4 4.3 %collective-permute-start.22 = (bf16[256,2048]{1,0:T(8,128)(2,1)}, bf16[256,2048]{1,0:T(8,128)(2,1)}, u32[]{:S(2)}, u32[]{:S(2)}) collective-permute-start(bf16[256,2048]{1,0:T(8,128)(2,1)} %get-tuple-element.74), channel_id=1, source_target_pairs={{8,0},{16,8},{24,16},{32,24},{40,32},{48,40},{56,48},{64,56},{72,6... | collective-permute-start | bytes 3145736 | tf_op jit(solution)/shard_map/ppermute | solution.py:27
  209.8 5.1 %all-to-all-done.5 = bf16[16,16,1024]{2,1,0:T(8,128)(2,1)S(1)} async-done(((bf16[16,16,1024]{2,1,0:T(8,128)(2,1)}), bf16[16,16,1024]{2,1,0:T(8,128)(2,1)S(1)}, u32[]{:S(2)}, u32[]{:S(2)}) %all-to-all-start.5) | async-done | bytes 524320 | tf_op jit(solution)/shard_map/all_to_all | solution.py:251
  214.9 3.0 %fusion.12 = (bf16[256,1024]{1,0:T(8,128)(2,1)S(1)}, f32[256,1024]{1,0:T(8,128)}, bf16[1,256,1024]{2,1,0:T(8,128)(2,1)}) fusion(bf16[16,16,1024]{2,1,0:T(8,128)(2,1)S(1)} %all-to-all-done.5, bf16[256,1024]{1,0:T(8,128)(2,1)S(1)} %bitcast.79, f32[256]{0:T(256)S(1)} %get-tuple-element.91, bf16[1,256,1024]{2,1,0:T(8,128)(2,1)} %param.12, ...), kind=kLoop, calls=%fused_computation.35 | loop fusion | flops 3145728 | bytes 4720640 | tf_op jit(solution)/shard_map/convert_element_type | solution.py:320
  217.9 3.3 %collective-permute-start.18 = (bf16[256,1024]{1,0:T(8,128)(2,1)S(1)}, bf16[256,1024]{1,0:T(8,128)(2,1)}, u32[]{:S(2)}, u32[]{:S(2)}) collective-permute-start(bf16[256,1024]{1,0:T(8,128)(2,1)S(1)} %get-tuple-element.79.refs_0_), channel_id=1, source_target_pairs={{0,4},{4,0},{1,5},{5,1},{2,6},{6,2},{3,7},{7,3},{8,12},{12,8},{9,1... | collective-permute-start | bytes 1572872 | tf_op jit(solution)/shard_map/ppermute | solution.py:35
  221.2 3.2 %collective-permute-start.20 = (bf16[256,1024]{1,0:T(8,128)(2,1)S(1)}, bf16[256,1024]{1,0:T(8,128)(2,1)S(1)}, u32[]{:S(2)}, u32[]{:S(2)}) collective-permute-start(bf16[256,1024]{1,0:T(8,128)(2,1)S(1)} %get-tuple-element.79.refs_0_), channel_id=1, source_target_pairs={{0,3},{1,0},{2,1},{3,2},{4,7},{5,4},{6,5},{7,6},{8,11},{9,8},{10,9... | collective-permute-start | bytes 1572872 | tf_op jit(solution)/shard_map/ppermute | solution.py:31
  225.3 13.4 %collective-permute-done.18.refs_3_ = bf16[256,1024]{1,0:T(8,128)(2,1)} collective-permute-done((bf16[256,1024]{1,0:T(8,128)(2,1)S(1)}, bf16[256,1024]{1,0:T(8,128)(2,1)}, u32[]{:S(2)}, u32[]{:S(2)}) %collective-permute-start.18) | collective-permute-done | bytes 524320 | tf_op jit(solution)/shard_map/ppermute | solution.py:35
  238.7 7.8 %collective-permute-done.20.refs_2_ = bf16[256,1024]{1,0:T(8,128)(2,1)S(1)} collective-permute-done((bf16[256,1024]{1,0:T(8,128)(2,1)S(1)}, bf16[256,1024]{1,0:T(8,128)(2,1)S(1)}, u32[]{:S(2)}, u32[]{:S(2)}) %collective-permute-start.20) | collective-permute-done | bytes 524320 | tf_op jit(solution)/shard_map/ppermute | solution.py:31
  246.5 1.1 collective-permute-done.21.refs_4_
  247.6 1.1 collective-permute-start.23
  248.7 2.3 collective-permute-start.24
  251.3 4.9 %place_rows.2.refs_3_ = bf16[2048,1024]{1,0:T(8,128)(2,1)} custom-call(s32[5]{0:T(128)} %bitcast.92, bf16[256,1024]{1,0:T(8,128)(2,1)} %copy-done.4, bf16[256,1024]{1,0:T(8,128)(2,1)} %copy-done.9, bf16[256,1024]{1,0:T(8,128)(2,1)} %copy-done.10, bf16[256,1024]{1,0:T(8,128)(2,1)} %collective-permute-done.18.refs_3_, ...), custom_call_target="tpu_custom_call" | custom-call | tf_op jit(solution)/shard_map/place_rows/pallas_call | solution.py:139
  256.1 3.0 %bitcast_add_fusion = f32[256,2048]{1,0:T(8,128)} fusion(bf16[256,2048]{1,0:T(8,128)(2,1)} %collective-permute-done.22, f32[1,256,2048]{2,1,0:T(8,128)S(1)} %copy-done), kind=kLoop, calls=%fused_computation.4 | loop fusion | flops 2097152 | bytes 5242880 | tf_op jit(solution)/shard_map/add | solution.py:322
  259.1 2.6 collective-permute-done.23.refs_0_
  261.8 3.1 %collective-permute-done.25.refs_2_ = bf16[256,1024]{1,0:T(8,128)(2,1)} collective-permute-done((bf16[256,1024]{1,0:T(8,128)(2,1)}, bf16[256,1024]{1,0:T(8,128)(2,1)}, u32[]{:S(2)}, u32[]{:S(2)}) %collective-permute-start.25) | collective-permute-done | bytes 524320 | tf_op jit(solution)/shard_map/ppermute | solution.py:35
  264.8 3.7 %place_rows.3 = bf16[2048,1024]{1,0:T(8,128)(2,1)} custom-call(s32[3]{0:T(128)} %slice.19.order, bf16[256,1024]{1,0:T(8,128)(2,1)} %copy-done.7, bf16[256,1024]{1,0:T(8,128)(2,1)} %copy-done.8, bf16[256,1024]{1,0:T(8,128)(2,1)} %collective-permute-done.25.refs_2_, bf16[2048,1024]{1,0:T(8,128)(2,1)} %place_rows.2.refs_3_), custom_call_target="tpu_custom_call", output_to_operand_aliasing={{}: (4, {})} | custom-call | tf_op jit(solution)/shard_map/place_rows/pallas_call | solution.py:139
  (82 shorter events, 9.9 us)
Async XLA Ops:
  0.6 20.6 %collective-permute-start = (bf16[256,2048]{1,0:T(8,128)(2,1)}, bf16[256,2048]{1,0:T(8,128)(2,1)}, u32[]{:S(2)}, u32[]{:S(2)}) collective-permute-start(bf16[256,2048]{1,0:T(8,128)(2,1)} %bitcast.68), channel_id=1, source_target_pairs={{8,0},{16,8},{24,16},{32,24},{40,32},{48,40},{56,48},{64,56},{72,6... | collective-permute-start | bytes 3145736 | tf_op jit(solution)/shard_map/ppermute | solution.py:27
  5.3 25.5 %collective-permute-start.2 = (bf16[256,2048]{1,0:T(8,128)(2,1)}, bf16[256,2048]{1,0:T(8,128)(2,1)}, u32[]{:S(2)}, u32[]{:S(2)}) collective-permute-start(bf16[256,2048]{1,0:T(8,128)(2,1)} %bitcast.69), channel_id=1, source_target_pairs={{0,1},{1,2},{2,3},{3,0},{4,5},{5,6},{6,7},{7,4},{8,9},{9,10},{10,1... | collective-permute-start | bytes 3145736 | tf_op jit(solution)/shard_map/ppermute | solution.py:31
  7.3 33.2 %collective-permute-start.4 = (bf16[256,2048]{1,0:T(8,128)(2,1)}, bf16[256,2048]{1,0:T(8,128)(2,1)}, u32[]{:S(2)}, u32[]{:S(2)}) collective-permute-start(bf16[256,2048]{1,0:T(8,128)(2,1)} %bitcast.70), channel_id=1, source_target_pairs={{0,3},{1,0},{2,1},{3,2},{4,7},{5,4},{6,5},{7,6},{8,11},{9,8},{10,9... | collective-permute-start | bytes 3145736 | tf_op jit(solution)/shard_map/ppermute | solution.py:31
  9.5 14.6 %all-to-all-start = ((bf16[16,16,1024]{2,1,0:T(8,128)(2,1)}), bf16[16,16,1024]{2,1,0:T(8,128)(2,1)}, u32[]{:S(2)}, u32[]{:S(2)}) async-start(bf16[16,16,1024]{2,1,0:T(8,128)(2,1)} %bitcast.85), calls=%async_computation | async-start | bytes 1048576 | tf_op jit(solution)/shard_map/all_to_all | solution.py:251
  16.6 4.6 %copy-start.1 = (bf16[1,256,2048]{2,1,0:T(8,128)(2,1)S(1)}, bf16[1,256,2048]{2,1,0:T(8,128)(2,1)}, u32[]{:S(2)}) copy-start(bf16[1,256,2048]{2,1,0:T(8,128)(2,1)} %param.8) | copy-start | bytes 3145732
  22.9 45.7 %copy-start.12 = (s32[8]{0:T(128)S(1)}, s32[8]{0:T(128)}, u32[]{:S(2)}) copy-start(s32[8]{0:T(128)} %constant.57.clone) | copy-start | bytes 100
  23.1 52.1 %copy-start = (f32[1,256,2048]{2,1,0:T(8,128)S(1)}, f32[1,256,2048]{2,1,0:T(8,128)}, u32[]{:S(2)}) copy-start(f32[1,256,2048]{2,1,0:T(8,128)} %param.10) | copy-start | bytes 6291460
  24.0 32.4 %collective-permute-start.1 = (bf16[256,2048]{1,0:T(8,128)(2,1)S(1)}, bf16[256,2048]{1,0:T(8,128)(2,1)}, u32[]{:S(2)}, u32[]{:S(2)}) collective-permute-start(bf16[256,2048]{1,0:T(8,128)(2,1)S(1)} %bitcast.73), channel_id=1, source_target_pairs={{0,4},{4,0},{1,5},{5,1},{2,6},{6,2},{3,7},{7,3},{8,12},{12,8},{9,1... | collective-permute-start | bytes 3145736 | tf_op jit(solution)/shard_map/ppermute | solution.py:35
  30.8 25.7 %collective-permute-start.3 = (bf16[256,2048]{1,0:T(8,128)(2,1)}, bf16[256,2048]{1,0:T(8,128)(2,1)}, u32[]{:S(2)}, u32[]{:S(2)}) collective-permute-start(bf16[256,2048]{1,0:T(8,128)(2,1)} %collective-permute-done.2.refs_1_.refs_2_), channel_id=1, source_target_pairs={{0,1},{1,2},{2,3},{3,0},{4,5},{5,6},{6,7},{7,4},{8,9},{9,10},{10,1... | collective-permute-start | bytes 3145736 | tf_op jit(solution)/shard_map/ppermute | solution.py:31
  30.8 25.7 %all-to-all-start.1 = ((f32[128,1,128]{2,1,0:T(1,128)}), f32[128,1,128]{2,1,0:T(1,128)S(1)}, u32[]{:S(2)}, u32[]{:S(2)}) async-start(f32[128,1,128]{2,1,0:T(1,128)} %bitcast.10), calls=%async_computation.1 | async-start | bytes 131072 | tf_op jit(solution)/shard_map/all_to_all | solution.py:284
  62.0 37.0 %collective-permute-start.5 = (bf16[256,2048]{1,0:T(8,128)(2,1)}, bf16[256,2048]{1,0:T(8,128)(2,1)}, u32[]{:S(2)}, u32[]{:S(2)}) collective-permute-start(bf16[256,2048]{1,0:T(8,128)(2,1)} %collective-permute-done.1.refs_3_.refs_4_), channel_id=1, source_target_pairs={{0,1},{1,2},{2,3},{3,0},{4,5},{5,6},{6,7},{7,4},{8,9},{9,10},{10,1... | collective-permute-start | bytes 3145736 | tf_op jit(solution)/shard_map/ppermute | solution.py:31
  62.9 36.1 %collective-permute-start.6 = (bf16[256,2048]{1,0:T(8,128)(2,1)}, bf16[256,2048]{1,0:T(8,128)(2,1)}, u32[]{:S(2)}, u32[]{:S(2)}) collective-permute-start(bf16[256,2048]{1,0:T(8,128)(2,1)} %collective-permute-done.1.refs_3_.refs_4_), channel_id=1, source_target_pairs={{0,3},{1,0},{2,1},{3,2},{4,7},{5,4},{6,5},{7,6},{8,11},{9,8},{10,9... | collective-permute-start | bytes 3145736 | tf_op jit(solution)/shard_map/ppermute | solution.py:31
  65.2 33.7 %collective-permute-start.7 = (bf16[256,2048]{1,0:T(8,128)(2,1)}, bf16[256,2048]{1,0:T(8,128)(2,1)}, u32[]{:S(2)}, u32[]{:S(2)}) collective-permute-start(bf16[256,2048]{1,0:T(8,128)(2,1)} %collective-permute-done.3.refs_4_.refs_5_), channel_id=1, source_target_pairs={{0,4},{4,0},{1,5},{5,1},{2,6},{6,2},{3,7},{7,3},{8,12},{12,8},{9,1... | collective-permute-start | bytes 3145736 | tf_op jit(solution)/shard_map/ppermute | solution.py:35
  69.2 29.7 %all-to-all-start.2 = ((bf16[16,16,1024]{2,1,0:T(8,128)(2,1)}), bf16[16,16,1024]{2,1,0:T(8,128)(2,1)S(1)}, u32[]{:S(2)}, u32[]{:S(2)}) async-start(bf16[16,16,1024]{2,1,0:T(8,128)(2,1)} %first_solution.1.initial), calls=%async_computation.2 | async-start | bytes 1048576 | tf_op jit(solution)/shard_map/all_to_all | solution.py:251
  98.9 17.6 %copy-start.2 = (bf16[16,16,1024]{2,1,0:T(8,128)(2,1)}, bf16[16,16,1024]{2,1,0:T(8,128)(2,1)S(1)}, u32[]{:S(2)}) copy-start(bf16[16,16,1024]{2,1,0:T(8,128)(2,1)S(1)} %all-to-all-done.2) | copy-start | bytes 1572868
  98.9 17.6 %collective-permute-start.11 = (bf16[256,1024]{1,0:T(8,128)(2,1)S(1)}, bf16[256,1024]{1,0:T(8,128)(2,1)S(1)}, u32[]{:S(2)}, u32[]{:S(2)}) collective-permute-start(bf16[256,1024]{1,0:T(8,128)(2,1)S(1)} %bitcast.74), channel_id=1, source_target_pairs={{0,4},{4,0},{1,5},{5,1},{2,6},{6,2},{3,7},{7,3},{8,12},{12,8},{9,1... | collective-permute-start | bytes 1572872 | tf_op jit(solution)/shard_map/ppermute | solution.py:35
  102.6 14.1 %collective-permute-start.12 = (bf16[256,1024]{1,0:T(8,128)(2,1)S(1)}, bf16[256,1024]{1,0:T(8,128)(2,1)}, u32[]{:S(2)}, u32[]{:S(2)}) collective-permute-start(bf16[256,1024]{1,0:T(8,128)(2,1)S(1)} %bitcast.75), channel_id=1, source_target_pairs={{0,1},{1,2},{2,3},{3,0},{4,5},{5,6},{6,7},{7,4},{8,9},{9,10},{10,1... | collective-permute-start | bytes 1572872 | tf_op jit(solution)/shard_map/ppermute | solution.py:31
  105.6 44.1 %collective-permute-start.8 = (bf16[8,256,256]{2,1,0:T(8,128)(2,1)}, bf16[8,256,256]{2,1,0:T(8,128)(2,1)}, u32[]{:S(2)}, u32[]{:S(2)}) collective-permute-start(bf16[8,256,256]{2,1,0:T(8,128)(2,1)} %own_columns.1.refs_9_), channel_id=1, source_target_pairs={{0,8},{8,16},{16,24},{24,32},{32,40},{40,48},{48,56},{56,64},{64,7... | collective-permute-start | bytes 3145736 | tf_op jit(solution)/shard_map/ppermute | solution.py:27
  107.5 42.4 %collective-permute-start.9 = (bf16[8,256,256]{2,1,0:T(8,128)(2,1)}, bf16[8,256,256]{2,1,0:T(8,128)(2,1)}, u32[]{:S(2)}, u32[]{:S(2)}) collective-permute-start(bf16[8,256,256]{2,1,0:T(8,128)(2,1)} %own_columns.1.refs_9_), channel_id=1, source_target_pairs={{8,0},{16,8},{24,16},{32,24},{40,32},{48,40},{56,48},{64,56},{72,6... | collective-permute-start | bytes 3145736 | tf_op jit(solution)/shard_map/ppermute | solution.py:27
  113.2 32.6 %collective-permute-start.13 = (bf16[256,1024]{1,0:T(8,128)(2,1)S(1)}, bf16[256,1024]{1,0:T(8,128)(2,1)}, u32[]{:S(2)}, u32[]{:S(2)}) collective-permute-start(bf16[256,1024]{1,0:T(8,128)(2,1)S(1)} %bitcast.76), channel_id=1, source_target_pairs={{0,3},{1,0},{2,1},{3,2},{4,7},{5,4},{6,5},{7,6},{8,11},{9,8},{10,9... | collective-permute-start | bytes 1572872 | tf_op jit(solution)/shard_map/ppermute | solution.py:31
  116.6 46.1 %copy-start.5 = (bf16[256,1024]{1,0:T(8,128)(2,1)}, bf16[256,1024]{1,0:T(8,128)(2,1)S(1)}, u32[]{:S(2)}) copy-start(bf16[256,1024]{1,0:T(8,128)(2,1)S(1)} %collective-permute-done.11.refs_3_) | copy-start | bytes 1572868
  116.6 29.3 %collective-permute-start.14 = (bf16[256,1024]{1,0:T(8,128)(2,1)S(1)}, bf16[256,1024]{1,0:T(8,128)(2,1)}, u32[]{:S(2)}, u32[]{:S(2)}) collective-permute-start(bf16[256,1024]{1,0:T(8,128)(2,1)S(1)} %bitcast.77), channel_id=1, source_target_pairs={{0,2},{1,3},{2,0},{3,1},{4,6},{5,7},{6,4},{7,5},{8,10},{9,11},{10,... | collective-permute-start | bytes 1572872 | tf_op jit(solution)/shard_map/ppermute | solution.py:31
  116.7 33.2 %collective-permute-start.10 = (bf16[256,2048]{1,0:T(8,128)(2,1)}, bf16[256,2048]{1,0:T(8,128)(2,1)}, u32[]{:S(2)}, u32[]{:S(2)}) collective-permute-start(bf16[256,2048]{1,0:T(8,128)(2,1)} %convert_bitcast_fusion), channel_id=1, source_target_pairs={{0,8},{8,16},{16,24},{24,32},{32,40},{40,48},{48,56},{56,64},{64,7... | collective-permute-start | bytes 3145736 | tf_op jit(solution)/shard_map/ppermute | solution.py:27
  118.6 44.0 %all-to-all-start.3 = ((bf16[8,256,256]{2,1,0:T(8,128)(2,1)}), bf16[8,256,256]{2,1,0:T(8,128)(2,1)}, u32[]{:S(2)}, u32[]{:S(2)}) async-start(bf16[8,256,256]{2,1,0:T(8,128)(2,1)} %bitcast.80), calls=%async_computation.3 | async-start | bytes 2097152 | tf_op jit(solution)/shard_map/all_to_all | solution.py:305
  145.8 16.8 %collective-permute-start.15 = (bf16[256,1024]{1,0:T(8,128)(2,1)S(1)}, bf16[256,1024]{1,0:T(8,128)(2,1)S(1)}, u32[]{:S(2)}, u32[]{:S(2)}) collective-permute-start(bf16[256,1024]{1,0:T(8,128)(2,1)S(1)} %collective-permute-done.11.refs_3_), channel_id=1, source_target_pairs={{0,1},{1,2},{2,3},{3,0},{4,5},{5,6},{6,7},{7,4},{8,9},{9,10},{10,1... | collective-permute-start | bytes 1572872 | tf_op jit(solution)/shard_map/ppermute | solution.py:31
  147.2 15.5 %collective-permute-start.16 = (bf16[256,1024]{1,0:T(8,128)(2,1)S(1)}, bf16[256,1024]{1,0:T(8,128)(2,1)}, u32[]{:S(2)}, u32[]{:S(2)}) collective-permute-start(bf16[256,1024]{1,0:T(8,128)(2,1)S(1)} %collective-permute-done.11.refs_3_), channel_id=1, source_target_pairs={{0,3},{1,0},{2,1},{3,2},{4,7},{5,4},{6,5},{7,6},{8,11},{9,8},{10,9... | collective-permute-start | bytes 1572872 | tf_op jit(solution)/shard_map/ppermute | solution.py:31
  149.6 13.1 %collective-permute-start.17 = (bf16[256,1024]{1,0:T(8,128)(2,1)}, bf16[256,1024]{1,0:T(8,128)(2,1)}, u32[]{:S(2)}, u32[]{:S(2)}) collective-permute-start(bf16[256,1024]{1,0:T(8,128)(2,1)} %collective-permute-done.14.refs_4_), channel_id=1, source_target_pairs={{0,4},{4,0},{1,5},{5,1},{2,6},{6,2},{3,7},{7,3},{8,12},{12,8},{9,1... | collective-permute-start | bytes 1572872 | tf_op jit(solution)/shard_map/ppermute | solution.py:35
  162.7 0.8 copy-start.6
  197.1 8.4 %copy-start.13 = (s32[1,2]{1,0:T(1,128)S(1)}, s32[1,2]{1,0:T(1,128)}, u32[]{:S(2)}) copy-start(s32[1,2]{1,0:T(1,128)} %param.13) | copy-start | bytes 28
  197.1 17.9 %copy-start.3 = (bf16[16,16,1024]{2,1,0:T(8,128)(2,1)S(1)}, bf16[16,16,1024]{2,1,0:T(8,128)(2,1)}, u32[]{:S(2)}) copy-start(bf16[16,16,1024]{2,1,0:T(8,128)(2,1)} %copy-done.2) | copy-start | bytes 1572868
  200.5 14.4 %all-to-all-start.5 = ((bf16[16,16,1024]{2,1,0:T(8,128)(2,1)}), bf16[16,16,1024]{2,1,0:T(8,128)(2,1)S(1)}, u32[]{:S(2)}, u32[]{:S(2)}) async-start(bf16[16,16,1024]{2,1,0:T(8,128)(2,1)} %change.1), calls=%async_computation.5 | async-start | bytes 1048576 | tf_op jit(solution)/shard_map/all_to_all | solution.py:251
  205.4 50.7 %collective-permute-start.22 = (bf16[256,2048]{1,0:T(8,128)(2,1)}, bf16[256,2048]{1,0:T(8,128)(2,1)}, u32[]{:S(2)}, u32[]{:S(2)}) collective-permute-start(bf16[256,2048]{1,0:T(8,128)(2,1)} %get-tuple-element.74), channel_id=1, source_target_pairs={{8,0},{16,8},{24,16},{32,24},{40,32},{48,40},{56,48},{64,56},{72,6... | collective-permute-start | bytes 3145736 | tf_op jit(solution)/shard_map/ppermute | solution.py:27
  214.9 9.7 %copy-start.11 = (s32[8]{0:T(128)S(1)}, s32[8]{0:T(128)}, u32[]{:S(2)}) copy-start(s32[8]{0:T(128)} %fusion.9.order.refs_0_) | copy-start | bytes 100
  217.9 6.5 %copy-start.4 = (bf16[256,1024]{1,0:T(8,128)(2,1)}, bf16[256,1024]{1,0:T(8,128)(2,1)S(1)}, u32[]{:S(2)}) copy-start(bf16[256,1024]{1,0:T(8,128)(2,1)S(1)} %get-tuple-element.79.refs_0_) | copy-start | bytes 1572868
  217.9 20.8 %collective-permute-start.18 = (bf16[256,1024]{1,0:T(8,128)(2,1)S(1)}, bf16[256,1024]{1,0:T(8,128)(2,1)}, u32[]{:S(2)}, u32[]{:S(2)}) collective-permute-start(bf16[256,1024]{1,0:T(8,128)(2,1)S(1)} %get-tuple-element.79.refs_0_), channel_id=1, source_target_pairs={{0,4},{4,0},{1,5},{5,1},{2,6},{6,2},{3,7},{7,3},{8,12},{12,8},{9,1... | collective-permute-start | bytes 1572872 | tf_op jit(solution)/shard_map/ppermute | solution.py:35
  221.2 17.6 %collective-permute-start.19 = (bf16[256,1024]{1,0:T(8,128)(2,1)S(1)}, bf16[256,1024]{1,0:T(8,128)(2,1)S(1)}, u32[]{:S(2)}, u32[]{:S(2)}) collective-permute-start(bf16[256,1024]{1,0:T(8,128)(2,1)S(1)} %get-tuple-element.79.refs_0_), channel_id=1, source_target_pairs={{0,1},{1,2},{2,3},{3,0},{4,5},{5,6},{6,7},{7,4},{8,9},{9,10},{10,1... | collective-permute-start | bytes 1572872 | tf_op jit(solution)/shard_map/ppermute | solution.py:31
  221.2 25.3 %collective-permute-start.20 = (bf16[256,1024]{1,0:T(8,128)(2,1)S(1)}, bf16[256,1024]{1,0:T(8,128)(2,1)S(1)}, u32[]{:S(2)}, u32[]{:S(2)}) collective-permute-start(bf16[256,1024]{1,0:T(8,128)(2,1)S(1)} %get-tuple-element.79.refs_0_), channel_id=1, source_target_pairs={{0,3},{1,0},{2,1},{3,2},{4,7},{5,4},{6,5},{7,6},{8,11},{9,8},{10,9... | collective-permute-start | bytes 1572872 | tf_op jit(solution)/shard_map/ppermute | solution.py:31
  224.4 23.2 %collective-permute-start.21 = (bf16[256,1024]{1,0:T(8,128)(2,1)S(1)}, bf16[256,1024]{1,0:T(8,128)(2,1)}, u32[]{:S(2)}, u32[]{:S(2)}) collective-permute-start(bf16[256,1024]{1,0:T(8,128)(2,1)S(1)} %get-tuple-element.79.refs_0_), channel_id=1, source_target_pairs={{0,2},{1,3},{2,0},{3,1},{4,6},{5,7},{6,4},{7,5},{8,10},{9,11},{10,... | collective-permute-start | bytes 1572872 | tf_op jit(solution)/shard_map/ppermute | solution.py:31
  238.7 8.9 %copy-start.9 = (bf16[256,1024]{1,0:T(8,128)(2,1)}, bf16[256,1024]{1,0:T(8,128)(2,1)S(1)}, u32[]{:S(2)}) copy-start(bf16[256,1024]{1,0:T(8,128)(2,1)S(1)} %collective-permute-done.19.refs_1_) | copy-start | bytes 1572868
  246.5 2.2 copy-start.10
  247.6 14.2 %collective-permute-start.23 = (bf16[256,1024]{1,0:T(8,128)(2,1)}, bf16[256,1024]{1,0:T(8,128)(2,1)S(1)}, u32[]{:S(2)}, u32[]{:S(2)}) collective-permute-start(bf16[256,1024]{1,0:T(8,128)(2,1)} %collective-permute-done.18.refs_3_), channel_id=1, source_target_pairs={{0,1},{1,2},{2,3},{3,0},{4,5},{5,6},{6,7},{7,4},{8,9},{9,10},{10,1... | collective-permute-start | bytes 1572872 | tf_op jit(solution)/shard_map/ppermute | solution.py:31
  248.7 13.0 %collective-permute-start.24 = (bf16[256,1024]{1,0:T(8,128)(2,1)}, bf16[256,1024]{1,0:T(8,128)(2,1)S(1)}, u32[]{:S(2)}, u32[]{:S(2)}) collective-permute-start(bf16[256,1024]{1,0:T(8,128)(2,1)} %collective-permute-done.18.refs_3_), channel_id=1, source_target_pairs={{0,3},{1,0},{2,1},{3,2},{4,7},{5,4},{6,5},{7,6},{8,11},{9,8},{10,9... | collective-permute-start | bytes 1572872 | tf_op jit(solution)/shard_map/ppermute | solution.py:31
  251.0 13.8 %collective-permute-start.25 = (bf16[256,1024]{1,0:T(8,128)(2,1)}, bf16[256,1024]{1,0:T(8,128)(2,1)}, u32[]{:S(2)}, u32[]{:S(2)}) collective-permute-start(bf16[256,1024]{1,0:T(8,128)(2,1)} %collective-permute-done.21.refs_4_), channel_id=1, source_target_pairs={{0,4},{4,0},{1,5},{5,1},{2,6},{6,2},{3,7},{7,3},{8,12},{12,8},{9,1... | collective-permute-start | bytes 1572872 | tf_op jit(solution)/shard_map/ppermute | solution.py:35
  261.8 3.1 %copy-start.7 = (bf16[256,1024]{1,0:T(8,128)(2,1)}, bf16[256,1024]{1,0:T(8,128)(2,1)S(1)}, u32[]{:S(2)}) copy-start(bf16[256,1024]{1,0:T(8,128)(2,1)S(1)} %collective-permute-done.23.refs_0_) | copy-start | bytes 1572868
  261.8 3.1 %copy-start.8 = (bf16[256,1024]{1,0:T(8,128)(2,1)}, bf16[256,1024]{1,0:T(8,128)(2,1)S(1)}, u32[]{:S(2)}) copy-start(bf16[256,1024]{1,0:T(8,128)(2,1)S(1)} %collective-permute-done.24.refs_1_) | copy-start | bytes 1572868
